TPU v7x, 128 devices: a whole 4x4x4 slice. The times are simulated.
128 devices in a mesh: sub: 32 (over z, x, y_hi), node: 4 (over y_lo, core).
Axes of the slice: x: 4, y: 4 (y_hi: 2, y_lo: 2; y = y_hi * 2 + y_lo), z: 4, core: 2. Of those that a mesh axis runs over, the one named last changes fastest.
Arguments:
- search_vectors: float32 [32768, 256], P('sub'), may hold values from -60 to 60
- ritz_values: float32 [256], replicated, may hold values from -0.9 to 0.9
- matrix_blocks: float32 [256, 4, 128, 128], P('sub'), may hold values from -0.25 to 0.25
- block_lists: int32 [256, 4], P('sub'), may hold values from 0 to 255, as said below
- inverses: float32 [8, 2, 256, 128, 128], P('node', None, 'sub'), may hold values from -0.5 to 0.5
- panels: float32 [32, 512, 1024], P('sub'), may hold values from -0.1875 to 0.1875
- separator_map: int32 [32, 4], P('sub'), may hold values from 0 to 7, as said below
- separator_shift: float32 [1024], replicated, may hold values from -0.9 to 0.9
Outputs:
- normalized_vectors: float32 [32768, 256], P('sub', 'node')
Inputs may be any that keep to these rules, and one draw needn't show every extreme that they name: `block_lists`: entry 0 of row g is g; the other entries of row g are distinct blocks from g - 4 to g + 4, none equal to g. `separator_map`: the entries of one row are distinct.
All inputs are finite; a program needn't handle non-finite values.
Results may differ from a plain program's by a relative error of at most 0.0001.
Values sent between devices are 32-bit elements; how exact they have to be, the bound alone decides.
No kernel may reach another device: no remote copies, remote signals or barrier semaphores. Data moves between devices by JAX's collectives and lax.ppermute only.
A program may use at most 64 MiB of HBM per device.

v0:
```python
import math

import jax
import jax.numpy as jnp
from jax import lax
from jax.sharding import PartitionSpec as P

HALO_BLOCKS = 4
SEP_GROUPS = 8


HIGHEST = lax.Precision.HIGHEST


def with_halo(shard, sides, width):
    for axis, dim in sides:
        size, length = (lax.axis_size(axis), shard.shape[dim])
        up = [(i, (i + 1) % size) for i in range(size - 1)]
        down = [(j, i) for i, j in up]
        last = lax.slice_in_dim(shard, length - width, length, axis=dim)
        first = lax.slice_in_dim(shard, 0, width, axis=dim)
        before = lax.ppermute(last, axis, up)
        after = lax.ppermute(first, axis, down)
        shard = jnp.concatenate([before, shard, after], axis=dim)
    return shard


def scale_coarse(summed, shift_rows, real_shift, imag_shift):
    real_gap = real_shift[:, None, None] - shift_rows[None, :, None]
    imag_gap = imag_shift[:, None, None]
    modulus = real_gap * real_gap + imag_gap * imag_gap
    real_part = summed[:, 0]
    imag_part = summed[:, 1]
    return jnp.stack(
        [
            (real_part * real_gap + imag_part * imag_gap) / modulus,
            (imag_part * real_gap - real_part * imag_gap) / modulus,
        ],
        axis=1,
    )


def shards(
    search_vectors,
    ritz_values,
    matrix_blocks,
    block_lists,
    inverses,
    panels,
    separator_map,
    separator_shift,
):
    row_count, width = search_vectors.shape
    block_count, degree_count, block_size, _ = matrix_blocks.shape
    node_count = lax.axis_size("node")
    col_count = width // node_count
    node_index = lax.axis_index("node")
    sub_index = lax.axis_index("sub")
    column_start = node_index * col_count
    local_index = block_lists - sub_index * block_count + HALO_BLOCKS
    padded = with_halo(search_vectors, (("sub", 0),), HALO_BLOCKS * block_size)
    picked = padded.reshape(block_count + 2 * HALO_BLOCKS, block_size, -1)[local_index]
    residual = (
        jnp.einsum("bkij,bkjm->bim", matrix_blocks, picked, precision=HIGHEST).reshape(
            row_count, -1
        )
        - search_vectors * ritz_values[None, :]
    )
    node_local = inverses.shape[0]
    total_nodes = node_local * node_count
    node_ids = (node_index * node_local + jnp.arange(node_local, dtype=jnp.int32)).astype(
        jnp.float32
    )
    angles = math.pi * (node_ids + 0.5) / total_nodes
    real_shift = jnp.cos(angles)
    imag_shift = jnp.sin(angles)
    res_blocks = residual.reshape(block_count, block_size, width)
    first_guess = jnp.einsum("ncbij,bjm->ncbim", inverses, res_blocks, precision=HIGHEST).reshape(
        node_local, 2, row_count, width
    )
    my_panel = panels[0]
    sep_count = my_panel.shape[0] // block_size
    partial_value = jnp.einsum("sr,ncrm->ncsm", my_panel, first_guess, precision=HIGHEST)
    one_hot = (
        separator_map[0][:, None] == jnp.arange(SEP_GROUPS, dtype=jnp.int32)[None, :]
    ).astype(jnp.float32)
    spread = jnp.einsum(
        "pg,ncpkm->ncgkm",
        one_hot,
        partial_value.reshape(node_local, 2, sep_count, block_size, width),
        precision=HIGHEST,
    ).reshape(node_local, 2, SEP_GROUPS * block_size, width)
    summed_all = lax.psum(spread, "sub")
    scaled = scale_coarse(summed_all, separator_shift, real_shift, imag_shift)
    picked_back = jnp.einsum(
        "pg,ncgkm->ncpkm",
        one_hot,
        scaled.reshape(node_local, 2, SEP_GROUPS, block_size, width),
        precision=HIGHEST,
    ).reshape(node_local, 2, sep_count * block_size, width)
    spread_back = jnp.einsum("sr,ncsm->ncrm", my_panel, picked_back, precision=HIGHEST).reshape(
        node_local, 2, block_count, block_size, width
    )
    products = jnp.einsum("ncbij,ndbjm->ncdbim", inverses, spread_back, precision=HIGHEST).reshape(
        node_local, 2, 2, row_count, width
    )
    sol_real = first_guess[:, 0] - (products[:, 0, 0] - products[:, 1, 1])
    sol_imag = first_guess[:, 1] - (products[:, 0, 1] + products[:, 1, 0])
    weight_real = 2.0 / total_nodes * real_shift
    weight_imag = 2.0 / total_nodes * imag_shift
    weighted = jnp.sum(
        weight_real[:, None, None] * sol_real - weight_imag[:, None, None] * sol_imag, axis=0
    )
    node_total = lax.psum_scatter(weighted, "node", scatter_dimension=1, tiled=True)
    updated = lax.dynamic_slice_in_dim(search_vectors, column_start, col_count, 1) - node_total
    squares = lax.psum(jnp.sum(updated * updated, axis=0), "sub")
    total_rows = row_count * lax.axis_size("sub")
    return updated * lax.rsqrt(squares / total_rows + 1e-06)[None, :]


def solution(mesh):
    return jax.shard_map(
        shards,
        mesh=mesh,
        in_specs=(
            P("sub", None),
            P(),
            P("sub", None, None, None),
            P("sub", None),
            P("node", None, "sub", None, None),
            P("sub", None, None),
            P("sub", None),
            P(),
        ),
        out_specs=P("sub", "node"),
        check_vma=False,
    )
```

profile of v0, /device:TPU:0, one launch (start us, length us, event | category | flops | bytes accessed | tf_op | source)
XLA Modules:
  0.0 625.0 jit_solution(13011423427141754346)
XLA Ops:
  6.5 2.5 fusion.40
  9.0 6.0 collective-permute-start
  15.0 1.3 collective-permute-start.1
  16.5 20.4 %collective-permute-done = f32[512,256]{1,0:T(8,128)} collective-permute-done((f32[512,256]{1,0:T(8,128)}, f32[512,256]{1,0:T(8,128)}, u32[]{:S(2)}, u32[]{:S(2)}) %collective-permute-start) | collective-permute-done | bytes 524320 | tf_op jit(solution)/shard_map/ppermute | solution.py:22
  36.9 4.3 collective-permute-done.1
  41.2 2.7 pad_maximum_fusion
  43.8 4.3 gather_fusion
  48.2 7.1 %fusion.41 = f32[8,256,128,1]{1,2,3,0:T(8,128)S(1)} fusion(f32[8,4,128,256]{3,2,1,0:T(8,128)} %bitcast.142, f32[8,4,128,128]{3,2,1,0:T(8,128)} %param.10), kind=kOutput, calls=%fused_computation.58 | convolution fusion | flops 1610612736 | bytes 7340032 | tf_op jit(solution)/shard_map/bkij,bkjm->bim/dot_general | solution.py:64
  55.5 3.5 convolution_bitcast_fusion.1
  59.4 2.0 copy-done.1
  61.4 14.6 %fusion.25 = f32[2,2,512,256]{2,3,1,0:T(8,128)} fusion(f32[2,2,1024,256]{3,2,1,0:T(8,128)S(1)} %bitcast.136, f32[1,512,1024]{2,1,0:T(8,128)S(1)} %copy-done.4), kind=kOutput, calls=%fused_computation.35 | convolution fusion | flops 6442450944 | bytes 8388608 | tf_op jit(solution)/shard_map/sr,ncrm->ncsm/dot_general | solution.py:83
  76.0 2.9 reshape.134
  79.0 4.1 copy.59
  83.1 3.8 convolution_bitcast_fusion
  86.9 3.3 copy.60
  90.9 365.5 %all-reduce.2.cloned.1.call-done = f32[2,2,1024,256]{3,2,1,0:T(8,128)} async-done(((f32[2,2,1024,256]{3,2,1,0:T(8,128)}), f32[2,2,1024,256]{3,2,1,0:T(8,128)}) %all-reduce.2.cloned.1.call-update) | async-done | bytes 4194320 | tf_op jit(solution)/shard_map/psum | solution.py:93
  456.4 3.0 add_divide_fusion
  459.4 1.2 copy.61
  460.6 1.2 copy.62
  461.9 2.1 fusion.28
  464.4 1.2 copy-done.5
  465.6 7.0 %fusion.19 = f32[2,2,256,1024]{3,2,1,0:T(8,128)S(1)} fusion(f32[2,2,512,256]{3,2,1,0:T(8,128)S(1)} %bitcast.146, f32[1,512,1024]{2,1,0:T(8,128)S(1)} %copy-done.5), kind=kOutput, calls=%fused_computation.27 | convolution fusion | flops 6442450944 | bytes 8388608 | tf_op jit(solution)/shard_map/sr,ncsm->ncrm/dot_general | solution.py:101
  473.7 7.8 %fusion.6 = f32[2,2,2,8,128,256]{5,4,1,2,3,0:T(8,128)S(1)} fusion(f32[2,2,8,128,256,1]{3,2,4,1,0,5:T(8,128)S(1)} %bitcast.140, f32[2,2,8,128,128]{4,3,2,1,0:T(8,128)S(1)} %copy-done), kind=kOutput, calls=%fused_computation.7 | convolution fusion | flops 3221225472 | bytes 14680064 | tf_op jit(solution)/shard_map/ncbij,ndbjm->ncdbim/dot_general | solution.py:104
  481.6 4.2 copy.67
  485.7 5.6 fusion.14
  491.3 2.5 copy.85
  493.9 20.6 %reduce-scatter.4.cloned.1.call-done = f32[64,1024]{1,0:T(8,128)} async-done(((f32[256,1024]{1,0:T(8,128)}), f32[64,1024]{1,0:T(8,128)}) %reduce-scatter.4.cloned.1.call-update) | async-done | bytes 262160
  514.5 2.0 copy.86
  516.5 1.3 multiply_reduce_fusion
  517.7 96.2 %psum.15 = f32[64]{0:T(128)S(1)} all-reduce(f32[64]{0:T(128)S(1)} %multiply_reduce_fusion), channel_id=1, replica_groups=mesh['sub'=32,'node'=4] {'sub'}, use_global_device_ids=true, to_apply=%region_4.0 | all-reduce | flops 64 | bytes 512 | tf_op jit(solution)/shard_map/psum | solution.py:116
  613.9 2.1 broadcast_multiply_fusion
  616.0 1.9 copy.72
  (35 shorter events, 3.1 us)
Async XLA Ops:
  6.5 48.9 %copy-start = (f32[2,2,8,128,128]{4,3,2,1,0:T(8,128)S(1)}, f32[2,2,8,128,128]{4,3,2,1,0:T(8,128)}, u32[]{:S(2)}) copy-start(f32[2,2,8,128,128]{4,3,2,1,0:T(8,128)} %param.12) | copy-start | bytes 6291460
  6.5 34.6 %copy-start.3 = (f32[1024,256]{1,0:T(8,128)S(1)}, f32[1024,256]{1,0:T(8,128)}, u32[]{:S(2)}) copy-start(f32[1024,256]{1,0:T(8,128)} %param.8) | copy-start | bytes 3145732
  6.5 9.7 %copy-start.8 = (s32[8,4]{0,1:T(4,128)S(1)}, s32[8,4]{0,1:T(4,128)}, u32[]{:S(2)}) copy-start(s32[8,4]{0,1:T(4,128)} %param.11) | copy-start | bytes 388
  6.5 449.9 %all-reduce.2.cloned.1.call-start = ((), (), s32[]{:S(2)}) async-start(), calls=%async_computation.1 | async-start | bytes 8388608 | tf_op jit(solution)/shard_map/psum | solution.py:93
  9.0 27.9 %collective-permute-start = (f32[512,256]{1,0:T(8,128)}, f32[512,256]{1,0:T(8,128)}, u32[]{:S(2)}, u32[]{:S(2)}) collective-permute-start(f32[512,256]{1,0:T(8,128)} %get-tuple-element.7), channel_id=1, source_target_pairs={{0,4},{4,8},{8,12},{12,16},{16,20},{20,24},{24,28},{28,32},{32,36}... | collective-permute-start | bytes 1572872 | tf_op jit(solution)/shard_map/ppermute | solution.py:22
  15.0 26.2 %collective-permute-start.1 = (f32[512,256]{1,0:T(8,128)}, f32[512,256]{1,0:T(8,128)}, u32[]{:S(2)}, u32[]{:S(2)}) collective-permute-start(f32[512,256]{1,0:T(8,128)} %get-tuple-element.8), channel_id=1, source_target_pairs={{4,0},{8,4},{12,8},{16,12},{20,16},{24,20},{28,24},{32,28},{36,32}... | collective-permute-start | bytes 1572872 | tf_op jit(solution)/shard_map/ppermute | solution.py:23
  48.2 7.1 %copy-start.9 = (f32[256]{0:T(256)S(1)}, f32[256]{0:T(256)}, u32[]{:S(2)}) copy-start(f32[256]{0:T(256)} %param.9) | copy-start | bytes 3076
  59.0 2.4 copy-start.4
  59.4 2.0 copy-start.1
  79.0 4.1 copy-start.7
  90.2 0.7 copy-start.6
  90.2 424.3 %reduce-scatter.4.cloned.1.call-start = ((), (), s32[]{:S(2)}) async-start(), calls=%async_computation.2 | async-start | bytes 1310720
  464.0 1.6 copy-start.5
  481.6 4.2 copy-start.2
Sparse Core Ops, SparseCore 0:
  90.3 366.0 all-reduce.1
  494.0 20.4 reduce-scatter.3
where the time goes:
time: 629 us; the launch traced here: 625 us
  waiting for transfers between devices  411 us (65%)
  blocking collectives  96.2 us (15%)
  matrix products  46 us (7%)
  local copies, waits for them, and re-layouts  36 us (6%)
  other arithmetic  14.9 us (2%)
  between operations  13.8 us (2%)
  starting transfers between devices  7.3 us (1%)
    psum x1, waiting for transfers between devices, shards(): summed_all = lax.psum(spread, 'sub')  365 us
    psum x1, blocking collectives, shards(): squares = lax.psum(jnp.sum(updated * updated, axis=0), 'sub')  96.2 us
    unnamed x3, waiting for transfers between devices  20.7 us
    ppermute x1, waiting for transfers between devices, with_halo(): before = lax.ppermute(last, axis, up)  20.4 us
    dot_general x1, matrix products, shards(): jnp.einsum('sr,ncrm->ncsm', my_panel, first_guess, precision=HIGHEST)  14.6 us
  transfers between devices with their start and end apart: 4, of which 4 were waited for; matrix products, arithmetic and copies ran while one was open for 0% of the time, Pallas kernels for 0%

commit v1 on v0

v1 whole, which is shorter than its diff:
```python
import functools
import math

import jax
import jax.numpy as jnp
import numpy as np
from jax import lax
from jax.experimental import pallas as pl
from jax.experimental.pallas import tpu as pltpu
from jax.sharding import PartitionSpec as P

BLK = 128
HALO = 4
GROUPS = 8
NODES = 8
LOCAL = 2
LANES = 128

F32 = jnp.float32
BF16 = jnp.bfloat16
VMEM = pl.BlockSpec(memory_space=pltpu.VMEM)
SMEM = pl.BlockSpec(memory_space=pltpu.SMEM)


def split(x):
    hi = x.astype(BF16)
    return hi, (x - hi.astype(F32)).astype(BF16)


def dot(a, b, dims=((1,), (0,))):
    return lax.dot_general(a, b, (dims, ((), ())), preferred_element_type=F32)


def dot3(a, b, dims=((1,), (0,))):
    return dot(a[0], b[0], dims) + (dot(a[0], b[1], dims) + dot(a[1], b[0], dims))


def halves(top, bottom):
    low = lax.broadcasted_iota(jnp.int32, top.shape, 1) < LANES // 2
    return (
        jnp.where(low, top, pltpu.roll(bottom, LANES // 2, 1)),
        jnp.where(low, pltpu.roll(top, LANES // 2, 1), bottom),
    )


def forward_kernel(
    place, lists, sep_map, own, near, far, ritz, mats, inverses, panel,
    residual, pieces, ext_hi, ext_lo, guess_hi, guess_lo,
):
    sub, core = place[0], place[1] % 2
    blocks = own.shape[0] // BLK
    for ref, start in ((near, core * 12), (own, HALO), (far, 12 - core * 12)):
        hi, lo = split(ref[...].reshape(-1, BLK, ref.shape[1]))
        ext_hi[pl.ds(start, hi.shape[0])] = hi
        ext_lo[pl.ds(start, hi.shape[0])] = lo
    for g in range(blocks):
        where = [lists[g, q] - sub * blocks + HALO for q in range(4)]
        rhs = [jnp.concatenate([e[w] for w in where], 0) for e in (ext_hi, ext_lo)]
        lhs = split(jnp.concatenate([mats[g, q] for q in range(4)], 1))
        rows = slice(g * BLK, (g + 1) * BLK)
        res = dot3(lhs, rhs) - own[rows, :] * ritz[...]
        residual[rows, :] = res
        r_hi, r_lo = split(res)
        d_hi, d_lo = split(
            jnp.concatenate([inverses[n, c, g] for n in range(LOCAL) for c in range(2)], 0)
        )
        guess = dot(
            jnp.concatenate([d_hi, d_lo, d_hi], 1), jnp.concatenate([r_hi, r_hi, r_lo], 0)
        )
        for k in range(2 * LOCAL):
            hi, lo = split(guess[k * BLK : (k + 1) * BLK])
            guess_hi[rows, k * 256 : (k + 1) * 256] = hi
            guess_lo[rows, k * 256 : (k + 1) * 256] = lo
    p_hi, p_lo = split(panel[0])
    for k in range(2 * LOCAL):
        cols = slice(k * 256, (k + 1) * 256)
        part = dot3((p_hi, p_lo), (guess_hi[:, cols], guess_lo[:, cols]))
        n, c = divmod(k, 2)
        for p in range(4):
            for h in range(2):
                row = ((c * 4 + p) * 2 + h) * 8
                tile = part[p * BLK : (p + 1) * BLK, h * LANES : (h + 1) * LANES]
                pieces[n * 16 : (n + 1) * 16, row : row + 8, :] = tile.reshape(16, 8, LANES)
    lane = lax.broadcasted_iota(jnp.int32, (8, LANES), 1)
    ids = jnp.zeros((8, LANES), jnp.int32)
    for p in range(4):
        ids = jnp.where(lane == p, sep_map[0, p], ids)
    pieces[:, 128:136, :] = jnp.broadcast_to(ids.astype(F32)[None], (32, 8, LANES))


def owner_kernel(place, maps, table, shift, received, back, total):
    sub = place[0]
    node = place[1] * LOCAL + sub // 16
    first_row = (sub % 16) * 8
    z_r, z_i, w_r, w_i = (table[node, k] for k in range(4))
    total[...] = jnp.zeros_like(total)

    def add(t, carry):
        for p in range(4):
            g = maps[t, p]
            for c in range(2):
                r = (c * 4 + p) * 16
                total[g, c] += received[t, r : r + 16, :]
        return carry

    lax.fori_loop(0, 32, add, 0, unroll=4)
    lane = lax.broadcasted_iota(jnp.int32, (8, LANES), 1)
    pick = lane == first_row + lax.broadcasted_iota(jnp.int32, (8, LANES), 0)
    for g in range(GROUPS):
        row = jnp.broadcast_to(shift[g : g + 1, :], (8, LANES))
        gap = z_r - jnp.sum(jnp.where(pick, row, 0.0), axis=1, keepdims=True)
        gap = jnp.concatenate([gap, gap], 0)
        modulus = gap * gap + z_i * z_i
        real, imag = total[g, 0], total[g, 1]
        c_r = (real * gap + imag * z_i) / modulus
        c_i = (imag * gap - real * z_i) / modulus
        total[g, 0] = w_r * c_r - w_i * c_i
        total[g, 1] = w_r * c_i + w_i * c_r

    def give(t, carry):
        for p in range(4):
            g = maps[t, p]
            for c in range(2):
                r = (c * 4 + p) * 16
                back[t, r : r + 16, :] = total[g, c]
        return carry

    lax.fori_loop(0, 32, give, 0, unroll=4)


def backward_kernel(
    place, table, picked, residual, inverses, panel, keep, send, x_hi, x_lo, v_hi, v_lo
):
    core = place[1] % 2
    for n in range(LOCAL):
        for c in range(2):
            for p in range(4):
                for h in range(2):
                    row = ((c * 4 + p) * 2 + h) * 8
                    tile = picked[n * 16 : (n + 1) * 16, row : row + 8, :].reshape(BLK, LANES)
                    hi, lo = split(tile)
                    col = (n * 2 + c) * 256 + h * LANES
                    x_hi[p * BLK : (p + 1) * BLK, col : col + LANES] = hi
                    x_lo[p * BLK : (p + 1) * BLK, col : col + LANES] = lo
    panels = split(panel[0])
    res = residual[...]
    blocks = residual.shape[0] // BLK
    for n in range(LOCAL):
        for c in range(2):
            k = n * 2 + c
            cols = slice(k * 256, (k + 1) * 256)
            corr = dot3(panels, (x_hi[:, cols], x_lo[:, cols]), ((0,), (0,)))
            weight = table[place[1] * LOCAL + n, 2 + c]
            value = res * weight - corr
            hi, lo = split(value if c == 0 else -value)
            v_hi[:, k] = hi.reshape(blocks, BLK, 256)
            v_lo[:, k] = lo.reshape(blocks, BLK, 256)
    for g in range(blocks):
        lhs = split(
            jnp.concatenate([inverses[n, c, g] for n in range(LOCAL) for c in range(2)], 1)
        )
        rhs = v_hi[g].reshape(4 * BLK, 256), v_lo[g].reshape(4 * BLK, 256)
        weighted = dot3(lhs, rhs)
        low, high = halves(weighted[:, :LANES], weighted[:, LANES:])
        rows = slice(g * BLK, (g + 1) * BLK)
        keep[rows, :] = jnp.where(core == 0, low, high)
        send[rows, :] = jnp.where(core == 0, high, low)


def pair_kernel(place, mine, theirs, keep, send):
    first = place[1] // 2 == 0
    half = mine.shape[0] // 2
    total = mine[...] + theirs[...]
    low, high = halves(total[:half], total[half:])
    keep[...] = jnp.where(first, low, high)
    send[...] = jnp.where(first, high, low)


def update_kernel(place, mine, theirs, vectors, update, squares):
    first, core = place[1] // 2 == 0, place[1] % 2
    half = mine.shape[0]
    mid = vectors.shape[1] // 2
    own = jnp.where(first, vectors[:, :mid], vectors[:, mid:])
    low, high = halves(own[:half], own[half:])
    new = jnp.where(core == 0, low, high) - (mine[...] + theirs[...])
    update[...] = new
    sums = jnp.sum(new * new, axis=0, keepdims=True)
    sums = sums + pltpu.roll(sums, LANES // 2, 1)
    squares[...] = jnp.broadcast_to(sums[None], squares.shape)


def scale_kernel(rows, update, squares, out):
    half = update.shape[0]
    factor = lax.rsqrt(jnp.sum(squares[...], axis=0) / rows + 1e-06)
    new = update[...] * factor
    out[:half, :] = new[:, : LANES // 2]
    out[half:, :] = pltpu.roll(new, LANES // 2, 1)[:, : LANES // 2]


def call(body, name, specs, shapes, scratch=()):
    return pl.pallas_call(
        body,
        name=name,
        in_specs=specs,
        out_specs=[VMEM] * len(shapes),
        out_shape=[jax.ShapeDtypeStruct(s, F32) for s in shapes],
        scratch_shapes=list(scratch),
        compiler_params=pltpu.CompilerParams(vmem_limit_bytes=50 << 20),
    )


def shards(
    search_vectors,
    ritz_values,
    matrix_blocks,
    block_lists,
    inverses,
    panels,
    separator_map,
    separator_shift,
):
    rows, width = search_vectors.shape
    subs, nodes = lax.axis_size("sub"), lax.axis_size("node")
    sub, node = lax.axis_index("sub"), lax.axis_index("node")
    place = jnp.stack([sub, node]).astype(jnp.int32)
    theta = math.pi * (np.arange(NODES) + 0.5) / NODES
    z = np.stack([np.cos(theta), np.sin(theta)], 1)
    table = jnp.asarray(np.concatenate([z, 2.0 * z / NODES], 1), F32)

    halo_rows = HALO * BLK
    edge = lax.dynamic_slice_in_dim(
        search_vectors, jnp.where(node % 2 == 0, rows - halo_rows, 0), halo_rows, 0
    )
    ring = []
    for t in range(subs):
        for n in range(nodes):
            d = t + 1 if n % 2 == 0 else t - 1
            if 0 <= d < subs:
                ring.append((t * nodes + n, d * nodes + n))
    swap_core = [(i, i ^ 1) for i in range(nodes)]
    swap_chip = [(i, i ^ 2) for i in range(nodes)]
    near = lax.ppermute(edge, ("sub", "node"), ring)
    far = lax.ppermute(near, "node", swap_core)

    residual, pieces = call(
        forward_kernel,
        "forward",
        [SMEM, SMEM, SMEM] + [VMEM] * 7,
        [(rows, width), (subs, 136, LANES)],
        [
            pltpu.VMEM((16, BLK, width), BF16),
            pltpu.VMEM((16, BLK, width), BF16),
            pltpu.VMEM((rows, 4 * width), BF16),
            pltpu.VMEM((rows, 4 * width), BF16),
        ],
    )(
        place, block_lists, separator_map, search_vectors, near, far,
        ritz_values[None, :], matrix_blocks, inverses, panels,
    )
    received = lax.all_to_all(pieces, "sub", 0, 0, tiled=True)
    maps = received[:, 128, :4].astype(jnp.int32)
    (back,) = call(
        owner_kernel,
        "owner",
        [SMEM, SMEM, SMEM, VMEM, VMEM],
        [(subs, 128, LANES)],
        [pltpu.VMEM((GROUPS, 2, 16, LANES), F32)],
    )(place, maps, table, separator_shift.reshape(GROUPS, LANES), received)
    picked = lax.all_to_all(back, "sub", 0, 0, tiled=True)
    keep, send = call(
        backward_kernel,
        "backward",
        [SMEM, SMEM] + [VMEM] * 4,
        [(rows, LANES), (rows, LANES)],
        [
            pltpu.VMEM((512, 4 * width), BF16),
            pltpu.VMEM((512, 4 * width), BF16),
            pltpu.VMEM((rows // BLK, 4, BLK, width), BF16),
            pltpu.VMEM((rows // BLK, 4, BLK, width), BF16),
        ],
    )(place, table, picked, residual, inverses, panels)
    theirs = lax.ppermute(send, "node", swap_core)
    keep, send = call(
        pair_kernel, "pair", [SMEM, VMEM, VMEM], [(rows // 2, LANES), (rows // 2, LANES)]
    )(place, keep, theirs)
    theirs = lax.ppermute(send, "node", swap_chip)
    update, squares = call(
        update_kernel,
        "update",
        [SMEM, VMEM, VMEM, VMEM],
        [(rows // 2, LANES), (subs, 1, LANES)],
    )(place, keep, theirs, search_vectors)
    gathered = lax.all_to_all(squares, "sub", 0, 0, tiled=True)
    (out,) = call(
        functools.partial(scale_kernel, rows * subs),
        "scale",
        [VMEM, VMEM],
        [(rows, width // nodes)],
    )(update, gathered)
    return out


def solution(mesh):
    return jax.shard_map(
        shards,
        mesh=mesh,
        in_specs=(
            P("sub", None),
            P(),
            P("sub", None, None, None),
            P("sub", None),
            P("node", None, "sub", None, None),
            P("sub", None, None),
            P("sub", None),
            P(),
        ),
        out_specs=P("sub", "node"),
        check_vma=False,
    )
```

time: 629 us -> 150 us (0.24)
  waiting for transfers between devices: 411 us -> 22.7 us
  matrix products: 46 us -> 0 us
  local copies, waits for them, and re-layouts: 36 us -> 6.64 us
  Pallas kernels: 0 us -> 23 us
  other arithmetic: 14.9 us -> 0.09 us
  between operations: 13.8 us -> 0.08 us
    psum x1 -> x0, waiting for transfers between devices: 365 us -> none  [shards(): summed_all = lax.psum(spread, 'sub')]
    psum x1 -> x0, blocking collectives: 96.2 us -> none  [shards(): squares = lax.psum(jnp.sum(updated * updated, axis=0), 'sub')]
    all_to_all x0 -> x3, blocking collectives: none -> 90.7 us  [the longest x1 44 us: shards(): received = lax.all_to_all(pieces, 'sub', 0, 0, tiled=True)]
    dot_general x7 -> x0, matrix products: 46 us -> none  [the longest x1 14.6 us: shards(): jnp.einsum('sr,ncrm->ncsm', my_panel, first_guess, precision=HIGHEST)]
    pallas_call x0 -> x6, Pallas kernels: none -> 23 us  [the longest x1 10.7 us: shards(): call(forward_kernel, 'forward', [SMEM, SMEM, SMEM] + [VMEM] * 7, [(rows,...]
    unnamed x3 -> x0, waiting for transfers between devices: 20.7 us -> none
    transpose x4 -> x0, local copies, waits for them, and re-layouts: 8.25 us -> none  [the longest x1 4.17 us: shards(): jnp.einsum('ncbij,ndbjm->ncdbim', inverses, spread_back, precision=HIGHEST)]
    reshape x2 -> x0, local copies, waits for them, and re-layouts: 7.08 us -> none  [shards(): partial_value.reshape(node_local, 2, sep_count, block_size, width)]
  transfers between devices with their start and end apart: 4 -> 4, of which waited for: 4 -> 4; matrix products, arithmetic and copies ran while one was open for 0% -> 1% of each run, Pallas kernels for 0% -> 0%
where the time goes in v1:
time: 150 us; the launch traced here: 149 us
  blocking collectives  90.7 us (60%)
  Pallas kernels  23 us (15%)
  waiting for transfers between devices  22.7 us (15%)
  local copies, waits for them, and re-layouts  6.64 us (4%)
  starting transfers between devices  6.06 us (4%)
    all_to_all x1, blocking collectives, shards(): received = lax.all_to_all(pieces, 'sub', 0, 0, tiled=True)  44 us
    all_to_all x1, blocking collectives, shards(): picked = lax.all_to_all(back, 'sub', 0, 0, tiled=True)  33.4 us
    all_to_all x1, blocking collectives, shards(): gathered = lax.all_to_all(squares, 'sub', 0, 0, tiled=True)  13.3 us
    ppermute x1, waiting for transfers between devices, shards(): near = lax.ppermute(edge, ('sub', 'node'), ring)  12 us
    pallas_call x1, Pallas kernels, shards(): call(forward_kernel, 'forward', [SMEM, SMEM, SMEM] + [VMEM] * 7, [(rows,...  10.7 us
    pallas_call x1, Pallas kernels, shards(): call(backward_kernel, 'backward', [SMEM, SMEM] + [VMEM] * 4, [(rows, LANE...  8.04 us
    ppermute x1, waiting for transfers between devices, shards(): theirs = lax.ppermute(send, 'node', swap_chip)  7.67 us
    ppermute x1, starting transfers between devices, shards(): near = lax.ppermute(edge, ('sub', 'node'), ring)  5.21 us
  transfers between devices with their start and end apart: 4, of which 4 were waited for; matrix products, arithmetic and copies ran while one was open for 1% of the time, Pallas kernels for 0%

profile of v1, /device:TPU:0, one launch (start us, length us, event | category | flops | bytes accessed | tf_op | source)
XLA Modules:
  0.0 149.2 jit_solution(2786945289403791712)
XLA Ops:
  0.0 1.1 constant_dynamic-slice_fusion
  1.1 5.2 %collective-permute-start = (f32[512,256]{1,0:T(8,128)S(1)}, f32[512,256]{1,0:T(8,128)S(1)}, u32[]{:S(2)}, u32[]{:S(2)}) collective-permute-start(f32[512,256]{1,0:T(8,128)S(1)} %constant_dynamic-slice_fusion), channel_id=1, source_target_pairs={{0,4},{2,6},{4,8},{5,1},{6,10},{7,3},{8,12},{9,5},{10,14},{11,7},{... | collective-permute-start | bytes 1572872 | tf_op jit(solution)/shard_map/ppermute | solution.py:242
  6.3 12.0 %collective-permute-done.near = f32[512,256]{1,0:T(8,128)S(1)} collective-permute-done((f32[512,256]{1,0:T(8,128)S(1)}, f32[512,256]{1,0:T(8,128)S(1)}, u32[]{:S(2)}, u32[]{:S(2)}) %collective-permute-start) | collective-permute-done | bytes 524320 | tf_op jit(solution)/shard_map/ppermute | solution.py:242
  18.3 0.0 collective-permute-start.1
  18.3 0.8 copy.14.lists
  19.1 0.1 pad_add_fusion.place
  19.2 1.1 collective-permute-done.1.far
  20.2 0.0 copy-start
  20.2 1.2 copy-done
  21.5 0.0 copy-start.4
  21.5 0.7 copy-done.4
  22.1 0.0 copy-start.5
  22.2 0.7 copy-done.5
  22.8 10.7 %forward.1 = (f32[1024,256]{1,0:T(8,128)S(1)}, f32[32,136,128]{2,1,0:T(8,128)}) custom-call(s32[2]{0:T(128)S(1)} %pad_add_fusion.place, s32[8,4]{1,0:T(8,128)S(1)} %copy.14.lists, s32[1,4]{1,0:T(1,128)S(1)} %copy-done.5, f32[1024,256]{1,0:T(8,128)S(1)} %copy-done, f32[512,256]{1,0:T(8,128)S(1)} %collective-permute-done.near, ...), custom_call_target="tpu_custom_call" | custom-call | tf_op jit(solution)/shard_map/forward/pallas_call | solution.py:245
  33.5 0.0 copy-start.2
  33.5 44.0 %all_to_all.15.received = f32[32,136,128]{2,1,0:T(8,128)S(1)} all-to-all(f32[32,136,128]{2,1,0:T(8,128)} %get-tuple-element.13), channel_id=1, replica_groups=mesh['sub'=32,'node'=4] {'sub'}, dimensions={0} | all-to-all | bytes 4456448 | tf_op jit(solution)/shard_map/all_to_all | solution.py:260
  77.5 1.3 copy-done.6
  78.9 0.0 copy-done.2
  78.9 0.0 copy-done.3
  78.9 2.5 %owner.1 = f32[32,128,128]{2,1,0:T(8,128)S(1)} custom-call(s32[2]{0:T(128)S(1)} %pad_add_fusion.place, s32[32,4]{1,0:T(8,128)S(1)} %bitcast.5, f32[8,4]{1,0:T(8,128)S(1)} %copy-done.2, f32[8,128]{1,0:T(8,128)S(1)} %bitcast.6, f32[32,136,128]{2,1,0:T(8,128)} %copy-done.6), custom_call_target="tpu_custom_call" | custom-call | tf_op jit(solution)/shard_map/owner/pallas_call | solution.py:262
  81.4 33.4 %all_to_all.16.picked = f32[32,128,128]{2,1,0:T(8,128)} all-to-all(f32[32,128,128]{2,1,0:T(8,128)S(1)} %owner.1), channel_id=1, replica_groups=mesh['sub'=32,'node'=4] {'sub'}, dimensions={0} | all-to-all | bytes 4194304 | tf_op jit(solution)/shard_map/all_to_all | solution.py:269
  114.8 8.0 %backward.1 = (f32[1024,128]{1,0:T(8,128)S(1)}, f32[1024,128]{1,0:T(8,128)S(1)}) custom-call(s32[2]{0:T(128)S(1)} %pad_add_fusion.place, f32[8,4]{1,0:T(8,128)S(1)} %copy-done.2, f32[32,128,128]{2,1,0:T(8,128)} %all_to_all.16.picked, f32[1024,256]{1,0:T(8,128)S(1)} %get-tuple-element.14.residual, f32[2,2,8,128,128]{4,3,2,1,0:T(8,128)} %inverses.3, ...), custom_call_target="tpu_custom_call" | custom-call | tf_op jit(solution)/shard_map/backward/pallas_call | solution.py:270
  122.8 0.1 collective-permute-start.2
  122.9 1.9 %collective-permute-done.2.theirs = f32[1024,128]{1,0:T(8,128)S(1)} collective-permute-done((f32[1024,128]{1,0:T(8,128)S(1)}, f32[1024,128]{1,0:T(8,128)S(1)}, u32[]{:S(2)}, u32[]{:S(2)}) %collective-permute-start.2) | collective-permute-done | bytes 524320 | tf_op jit(solution)/shard_map/ppermute | solution.py:282
  124.8 0.7 pair.1
  125.6 0.8 collective-permute-start.3
  126.3 7.7 %collective-permute-done.3.theirs = f32[512,128]{1,0:T(8,128)S(1)} collective-permute-done((f32[512,128]{1,0:T(8,128)S(1)}, f32[512,128]{1,0:T(8,128)S(1)}, u32[]{:S(2)}, u32[]{:S(2)}) %collective-permute-start.3) | collective-permute-done | bytes 262176 | tf_op jit(solution)/shard_map/ppermute | solution.py:286
  134.0 0.0 copy-done.1
  134.0 0.8 update.1
  134.8 13.3 %all_to_all.17.squares = f32[32,1,128]{2,1,0:T(1,128)S(1)} all-to-all(f32[32,1,128]{2,1,0:T(1,128)S(1)} %get-tuple-element.20), channel_id=1, replica_groups=mesh['sub'=32,'node'=4] {'sub'}, dimensions={0} | all-to-all | bytes 32768 | tf_op jit(solution)/shard_map/all_to_all | solution.py:293
  148.2 0.2 scale.1
  148.3 0.9 copy.17
  (4 shorter events, 0.0 us)
Async XLA Ops:
  1.1 17.3 %collective-permute-start = (f32[512,256]{1,0:T(8,128)S(1)}, f32[512,256]{1,0:T(8,128)S(1)}, u32[]{:S(2)}, u32[]{:S(2)}) collective-permute-start(f32[512,256]{1,0:T(8,128)S(1)} %constant_dynamic-slice_fusion), channel_id=1, source_target_pairs={{0,4},{2,6},{4,8},{5,1},{6,10},{7,3},{8,12},{9,5},{10,14},{11,7},{... | collective-permute-start | bytes 1572872 | tf_op jit(solution)/shard_map/ppermute | solution.py:242
  18.3 1.9 %collective-permute-start.1 = (f32[512,256]{1,0:T(8,128)S(1)}, f32[512,256]{1,0:T(8,128)S(1)}, u32[]{:S(2)}, u32[]{:S(2)}) collective-permute-start(f32[512,256]{1,0:T(8,128)S(1)} %collective-permute-done.near), channel_id=1, source_target_pairs={{0,1},{1,0},{2,3},{3,2},{4,5},{5,4},{6,7},{7,6},{8,9},{9,8},{10,11... | collective-permute-start | bytes 1572872 | tf_op jit(solution)/shard_map/ppermute | solution.py:243
  20.2 1.2 copy-start
  21.5 0.7 copy-start.4
  22.1 0.7 copy-start.5
  33.5 45.4 %copy-start.2 = (f32[8,4]{1,0:T(8,128)S(1)}, f32[8,4]{1,0:T(8,128)}, u32[]{:S(2)}) copy-start(f32[8,4]{1,0:T(8,128)} %constant.29.clone.table) | copy-start | bytes 388
  33.5 45.4 %copy-start.3 = (f32[1024]{0:T(1024)S(1)}, f32[1024]{0:T(1024)}, u32[]{:S(2)}) copy-start(f32[1024]{0:T(1024)} %param.16) | copy-start | bytes 12292
  77.5 1.4 copy-start.6
  114.8 19.2 %copy-start.1 = (f32[1024,256]{1,0:T(8,128)S(1)}, f32[1024,256]{1,0:T(8,128)}, u32[]{:S(2)}) copy-start(f32[1024,256]{1,0:T(8,128)} %vectors.1) | copy-start | bytes 3145732
  122.8 2.0 %collective-permute-start.2 = (f32[1024,128]{1,0:T(8,128)S(1)}, f32[1024,128]{1,0:T(8,128)S(1)}, u32[]{:S(2)}, u32[]{:S(2)}) collective-permute-start(f32[1024,128]{1,0:T(8,128)S(1)} %get-tuple-element.16), channel_id=1, source_target_pairs={{0,1},{1,0},{2,3},{3,2},{4,5},{5,4},{6,7},{7,6},{8,9},{9,8},{10,11... | collective-permute-start | bytes 1572872 | tf_op jit(solution)/shard_map/ppermute | solution.py:282
  125.6 8.4 %collective-permute-start.3 = (f32[512,128]{1,0:T(8,128)S(1)}, f32[512,128]{1,0:T(8,128)S(1)}, u32[]{:S(2)}, u32[]{:S(2)}) collective-permute-start(f32[512,128]{1,0:T(8,128)S(1)} %get-tuple-element.18), channel_id=1, source_target_pairs={{0,2},{1,3},{2,0},{3,1},{4,6},{5,7},{6,4},{7,5},{8,10},{9,11},{10,... | collective-permute-start | bytes 786440 | tf_op jit(solution)/shard_map/ppermute | solution.py:286

commit v2 on v1

--- a/solution.py
+++ b/solution.py
@@ -43,49 +43,74 @@
     )
 
 
+def prepare_kernel(
+    place, sep_map, table, own, ritz, mats, inverses, panel,
+    own_hi, own_lo, scaled, m_hi, m_lo, e_hi, e_lo, f_hi, f_lo, w_hi, w_lo, ids,
+):
+    node = place[1] * LOCAL
+    blocks, sep = own.shape[0] // BLK, panel.shape[1]
+    scaled[...] = own[...] * ritz[...]
+    parts = [(n, c) for n in range(LOCAL) for c in range(2)]
+    for g in range(blocks):
+        rows = slice(g * BLK, (g + 1) * BLK)
+        own_hi[g], own_lo[g] = split(own[rows, :])
+        m_hi[g], m_lo[g] = split(jnp.concatenate([mats[g, q] for q in range(4)], 1))
+        weighted = [inverses[n, 0, g] * table[node + n, 2] for n in range(LOCAL)]
+        weighted += [inverses[n, 1, g] * -table[node + n, 3] for n in range(LOCAL)]
+        w_hi[g], w_lo[g] = split(sum(weighted[1:], weighted[0]))
+        p_hi, p_lo = split(panel[0, :, rows])
+        d_hi, d_lo = split(jnp.concatenate([inverses[n, c, g] for n, c in parts], 1))
+        e = dot(
+            jnp.concatenate([p_hi, p_lo, p_hi], 1), jnp.concatenate([d_hi, d_hi, d_lo], 0)
+        )
+        d_hi, d_lo = split(
+            jnp.concatenate([-inverses[n, c, g] if c == 0 else inverses[n, c, g] for n, c in parts], 0)
+        )
+        f = dot(
+            jnp.concatenate([d_hi, d_lo, d_hi], 1),
+            jnp.concatenate([p_hi, p_hi, p_lo], 1),
+            ((1,), (1,)),
+        )
+        for k in range(2 * LOCAL):
+            span, block = slice(k * sep, (k + 1) * sep), slice(k * BLK, (k + 1) * BLK)
+            e_hi[span, rows], e_lo[span, rows] = split(e[:, block])
+            f_hi[rows, span], f_lo[rows, span] = split(f[block, :])
+    lane = lax.broadcasted_iota(jnp.int32, ids.shape, 1)
+    value = jnp.zeros(ids.shape, jnp.int32)
+    for p in range(4):
+        value = jnp.where(lane == p, sep_map[0, p], value)
+    ids[...] = value.astype(F32)
+
+
 def forward_kernel(
-    place, lists, sep_map, own, near, far, ritz, mats, inverses, panel,
-    residual, pieces, ext_hi, ext_lo, guess_hi, guess_lo,
+    place, lists, near, far, own_hi, own_lo, scaled, m_hi, m_lo, e_hi, e_lo, ids,
+    r_hi, r_lo, pieces, ext_hi, ext_lo,
 ):
     sub, core = place[0], place[1] % 2
-    blocks = own.shape[0] // BLK
-    for ref, start in ((near, core * 12), (own, HALO), (far, 12 - core * 12)):
-        hi, lo = split(ref[...].reshape(-1, BLK, ref.shape[1]))
-        ext_hi[pl.ds(start, hi.shape[0])] = hi
-        ext_lo[pl.ds(start, hi.shape[0])] = lo
+    blocks = own_hi.shape[0]
+    for ref, start in ((near, core * 12), (far, 12 - core * 12)):
+        hi, lo = split(ref[...].reshape(HALO, BLK, ref.shape[1]))
+        ext_hi[pl.ds(start, HALO)] = hi
+        ext_lo[pl.ds(start, HALO)] = lo
+    ext_hi[HALO : HALO + blocks] = own_hi[...]
+    ext_lo[HALO : HALO + blocks] = own_lo[...]
     for g in range(blocks):
-        where = [lists[g, q] - sub * blocks + HALO for q in range(4)]
+        where = [lists[q, g] - sub * blocks + HALO for q in range(4)]
         rhs = [jnp.concatenate([e[w] for w in where], 0) for e in (ext_hi, ext_lo)]
-        lhs = split(jnp.concatenate([mats[g, q] for q in range(4)], 1))
         rows = slice(g * BLK, (g + 1) * BLK)
-        res = dot3(lhs, rhs) - own[rows, :] * ritz[...]
-        residual[rows, :] = res
-        r_hi, r_lo = split(res)
-        d_hi, d_lo = split(
-            jnp.concatenate([inverses[n, c, g] for n in range(LOCAL) for c in range(2)], 0)
-        )
-        guess = dot(
-            jnp.concatenate([d_hi, d_lo, d_hi], 1), jnp.concatenate([r_hi, r_hi, r_lo], 0)
-        )
-        for k in range(2 * LOCAL):
-            hi, lo = split(guess[k * BLK : (k + 1) * BLK])
-            guess_hi[rows, k * 256 : (k + 1) * 256] = hi
-            guess_lo[rows, k * 256 : (k + 1) * 256] = lo
-    p_hi, p_lo = split(panel[0])
+        r_hi[rows, :], r_lo[rows, :] = split(dot3((m_hi[g], m_lo[g]), rhs) - scaled[rows, :])
+    sep = e_hi.shape[0] // (2 * LOCAL)
+    res = r_hi[...], r_lo[...]
     for k in range(2 * LOCAL):
-        cols = slice(k * 256, (k + 1) * 256)
-        part = dot3((p_hi, p_lo), (guess_hi[:, cols], guess_lo[:, cols]))
+        span = slice(k * sep, (k + 1) * sep)
+        part = dot3((e_hi[span, :], e_lo[span, :]), res)
         n, c = divmod(k, 2)
         for p in range(4):
             for h in range(2):
                 row = ((c * 4 + p) * 2 + h) * 8
                 tile = part[p * BLK : (p + 1) * BLK, h * LANES : (h + 1) * LANES]
                 pieces[n * 16 : (n + 1) * 16, row : row + 8, :] = tile.reshape(16, 8, LANES)
-    lane = lax.broadcasted_iota(jnp.int32, (8, LANES), 1)
-    ids = jnp.zeros((8, LANES), jnp.int32)
-    for p in range(4):
-        ids = jnp.where(lane == p, sep_map[0, p], ids)
-    pieces[:, 128:136, :] = jnp.broadcast_to(ids.astype(F32)[None], (32, 8, LANES))
+    pieces[:, 128:136, :] = jnp.broadcast_to(ids[...][None], (32, 8, LANES))
 
 
 def owner_kernel(place, maps, table, shift, received, back, total):
@@ -129,42 +154,31 @@
 
 
 def backward_kernel(
-    place, table, picked, residual, inverses, panel, keep, send, x_hi, x_lo, v_hi, v_lo
+    place, picked, f_hi, f_lo, r_hi, r_lo, w_hi, w_lo, keep, send, x_hi, x_lo
 ):
     core = place[1] % 2
-    for n in range(LOCAL):
-        for c in range(2):
-            for p in range(4):
-                for h in range(2):
-                    row = ((c * 4 + p) * 2 + h) * 8
-                    tile = picked[n * 16 : (n + 1) * 16, row : row + 8, :].reshape(BLK, LANES)
-                    hi, lo = split(tile)
-                    col = (n * 2 + c) * 256 + h * LANES
-                    x_hi[p * BLK : (p + 1) * BLK, col : col + LANES] = hi
-                    x_lo[p * BLK : (p + 1) * BLK, col : col + LANES] = lo
-    panels = split(panel[0])
-    res = residual[...]
-    blocks = residual.shape[0] // BLK
-    for n in range(LOCAL):
-        for c in range(2):
-            k = n * 2 + c
-            cols = slice(k * 256, (k + 1) * 256)
-            corr = dot3(panels, (x_hi[:, cols], x_lo[:, cols]), ((0,), (0,)))
-            weight = table[place[1] * LOCAL + n, 2 + c]
-            value = res * weight - corr
-            hi, lo = split(value if c == 0 else -value)
-            v_hi[:, k] = hi.reshape(blocks, BLK, 256)
-            v_lo[:, k] = lo.reshape(blocks, BLK, 256)
-    for g in range(blocks):
-        lhs = split(
-            jnp.concatenate([inverses[n, c, g] for n in range(LOCAL) for c in range(2)], 1)
-        )
-        rhs = v_hi[g].reshape(4 * BLK, 256), v_lo[g].reshape(4 * BLK, 256)
-        weighted = dot3(lhs, rhs)
-        low, high = halves(weighted[:, :LANES], weighted[:, LANES:])
-        rows = slice(g * BLK, (g + 1) * BLK)
-        keep[rows, :] = jnp.where(core == 0, low, high)
-        send[rows, :] = jnp.where(core == 0, high, low)
+    sep = f_hi.shape[1] // (2 * LOCAL)
+    for k in range(2 * LOCAL):
+        n, c = divmod(k, 2)
+        for p in range(4):
+            for h in range(2):
+                row = ((c * 4 + p) * 2 + h) * 8
+                tile = picked[n * 16 : (n + 1) * 16, row : row + 8, :].reshape(BLK, LANES)
+                rows = slice(k * sep + p * BLK, k * sep + (p + 1) * BLK)
+                cols = slice(h * LANES, (h + 1) * LANES)
+                x_hi[rows, cols], x_lo[rows, cols] = split(tile)
+    coarse = x_hi[...], x_lo[...]
+    for g in range(0, w_hi.shape[0], 2):
+        both = slice(g * BLK, (g + 2) * BLK)
+        back = dot3((f_hi[both, :], f_lo[both, :]), coarse)
+        for i in range(2):
+            rows = slice((g + i) * BLK, (g + i + 1) * BLK)
+            weighted = back[i * BLK : (i + 1) * BLK] + dot3(
+                (w_hi[g + i], w_lo[g + i]), (r_hi[rows, :], r_lo[rows, :])
+            )
+            low, high = halves(weighted[:, :LANES], weighted[:, LANES:])
+            keep[rows, :] = jnp.where(core == 0, low, high)
+            send[rows, :] = jnp.where(core == 0, high, low)
 
 
 def pair_kernel(place, mine, theirs, keep, send):
@@ -192,20 +206,22 @@
 def scale_kernel(rows, update, squares, out):
     half = update.shape[0]
     factor = lax.rsqrt(jnp.sum(squares[...], axis=0) / rows + 1e-06)
-    new = update[...] * factor
-    out[:half, :] = new[:, : LANES // 2]
-    out[half:, :] = pltpu.roll(new, LANES // 2, 1)[:, : LANES // 2]
-
-
-def call(body, name, specs, shapes, scratch=()):
+    new = (update[...] * factor).T
+    out[:, :half] = new[: LANES // 2]
+    out[:, half:] = new[LANES // 2 :]
+
+
+def call(body, name, specs, shapes, scratch=(), limit=16, flops=0):
+    shapes = [s if isinstance(s, jax.ShapeDtypeStruct) else jax.ShapeDtypeStruct(s, F32) for s in shapes]
     return pl.pallas_call(
         body,
         name=name,
         in_specs=specs,
         out_specs=[VMEM] * len(shapes),
-        out_shape=[jax.ShapeDtypeStruct(s, F32) for s in shapes],
+        out_shape=shapes,
         scratch_shapes=list(scratch),
-        compiler_params=pltpu.CompilerParams(vmem_limit_bytes=50 << 20),
+        cost_estimate=pl.CostEstimate(flops=flops, bytes_accessed=8 << 20, transcendentals=0),
+        compiler_params=pltpu.CompilerParams(vmem_limit_bytes=limit << 20),
     )
 
 
@@ -240,22 +256,38 @@
     swap_core = [(i, i ^ 1) for i in range(nodes)]
     swap_chip = [(i, i ^ 2) for i in range(nodes)]
     near = lax.ppermute(edge, ("sub", "node"), ring)
+    half = functools.partial(jax.ShapeDtypeStruct, dtype=BF16)
+    blocks, sep = rows // BLK, panels.shape[1]
+    prepared = call(
+        prepare_kernel,
+        "prepare",
+        [SMEM, SMEM, SMEM] + [VMEM] * 5,
+        [half((blocks, BLK, width))] * 2
+        + [(rows, width)]
+        + [half((blocks, BLK, 4 * BLK))] * 2
+        + [half((4 * sep, rows))] * 2
+        + [half((rows, 4 * sep))] * 2
+        + [half((blocks, BLK, BLK))] * 2
+        + [(8, LANES)],
+        limit=24,
+        flops=8 * 10**9,
+    )(
+        place, separator_map, table, search_vectors, ritz_values[None, :],
+        matrix_blocks, inverses, panels,
+    )
+    own_hi, own_lo, scaled, m_hi, m_lo, e_hi, e_lo, f_hi, f_lo, w_hi, w_lo, ids = prepared
+    near, ids = lax.optimization_barrier((near, ids))
     far = lax.ppermute(near, "node", swap_core)
-
-    residual, pieces = call(
+    r_hi, r_lo, pieces = call(
         forward_kernel,
         "forward",
-        [SMEM, SMEM, SMEM] + [VMEM] * 7,
-        [(rows, width), (subs, 136, LANES)],
-        [
-            pltpu.VMEM((16, BLK, width), BF16),
-            pltpu.VMEM((16, BLK, width), BF16),
-            pltpu.VMEM((rows, 4 * width), BF16),
-            pltpu.VMEM((rows, 4 * width), BF16),
-        ],
+        [SMEM, SMEM] + [VMEM] * 10,
+        [half((rows, width)), half((rows, width)), (subs, 136, LANES)],
+        [pltpu.VMEM((16, BLK, width), BF16)] * 2,
+        limit=16,
+        flops=4 * 10**9,
     )(
-        place, block_lists, separator_map, search_vectors, near, far,
-        ritz_values[None, :], matrix_blocks, inverses, panels,
+        place, block_lists.T, near, far, own_hi, own_lo, scaled, m_hi, m_lo, e_hi, e_lo, ids
     )
     received = lax.all_to_all(pieces, "sub", 0, 0, tiled=True)
     maps = received[:, 128, :4].astype(jnp.int32)
@@ -270,15 +302,12 @@
     keep, send = call(
         backward_kernel,
         "backward",
-        [SMEM, SMEM] + [VMEM] * 4,
+        [SMEM] + [VMEM] * 7,
         [(rows, LANES), (rows, LANES)],
-        [
-            pltpu.VMEM((512, 4 * width), BF16),
-            pltpu.VMEM((512, 4 * width), BF16),
-            pltpu.VMEM((rows // BLK, 4, BLK, width), BF16),
-            pltpu.VMEM((rows // BLK, 4, BLK, width), BF16),
-        ],
-    )(place, table, picked, residual, inverses, panels)
+        [pltpu.VMEM((4 * sep, width), BF16)] * 2,
+        limit=16,
+        flops=4 * 10**9,
+    )(place, picked, f_hi, f_lo, r_hi, r_lo, w_hi, w_lo)
     theirs = lax.ppermute(send, "node", swap_core)
     keep, send = call(
         pair_kernel, "pair", [SMEM, VMEM, VMEM], [(rows // 2, LANES), (rows // 2, LANES)]
@@ -295,9 +324,9 @@
         functools.partial(scale_kernel, rows * subs),
         "scale",
         [VMEM, VMEM],
-        [(rows, width // nodes)],
+        [(width // nodes, rows)],
     )(update, gathered)
-    return out
+    return out.T
 
 
 def solution(mesh):

time: 150 us -> 136 us (0.907)
  waiting for transfers between devices: 22.7 us -> 10.5 us
  blocking collectives: 90.7 us -> 87.7 us
  local copies, waits for them, and re-layouts: 6.64 us -> 9.11 us
  Pallas kernels: 23 us -> 21.2 us
    ppermute x1, waiting for transfers between devices: 12 us -> 0.01 us  [shards(): near = lax.ppermute(edge, ('sub', 'node'), ring)]
    all_to_all x1, blocking collectives: 44 us -> 40.6 us  [shards(): received = lax.all_to_all(pieces, 'sub', 0, 0, tiled=True)]
    unnamed x15 -> x22, local copies, waits for them, and re-layouts: 4.68 us -> 8.04 us
    pallas_call x2 -> x3, Pallas kernels: 18.7 us -> 16.9 us  [the longest x1 7.19 us: shards(): call(prepare_kernel, 'prepare', [SMEM, SMEM, SMEM] + [VMEM] * 5, [half((b...]
  transfers between devices with their start and end apart: 4 -> 4, of which waited for: 4 -> 3; matrix products, arithmetic and copies ran while one was open for 1% -> 0% of each run, Pallas kernels for 0% -> 5%
where the time goes in v2:
time: 136 us
  blocking collectives  87.7 us (64%)
  Pallas kernels  21.2 us (16%)
  waiting for transfers between devices  10.5 us (8%)
  local copies, waits for them, and re-layouts  9.11 us (7%)
  starting transfers between devices  7.08 us (5%)
    all_to_all x1, blocking collectives, shards(): received = lax.all_to_all(pieces, 'sub', 0, 0, tiled=True)  40.6 us
    all_to_all x1, blocking collectives, shards(): picked = lax.all_to_all(back, 'sub', 0, 0, tiled=True)  33.2 us
    all_to_all x1, blocking collectives, shards(): gathered = lax.all_to_all(squares, 'sub', 0, 0, tiled=True)  13.8 us
    unnamed x22, local copies, waits for them, and re-layouts  8.04 us
    pallas_call x1, Pallas kernels, shards(): call(prepare_kernel, 'prepare', [SMEM, SMEM, SMEM] + [VMEM] * 5, [half((b...  7.19 us
    ppermute x1, waiting for transfers between devices, shards(): theirs = lax.ppermute(send, 'node', swap_chip)  6.73 us
    ppermute x1, starting transfers between devices, shards(): near = lax.ppermute(edge, ('sub', 'node'), ring)  5.21 us
    pallas_call x1, Pallas kernels, shards(): call(forward_kernel, 'forward', [SMEM, SMEM] + [VMEM] * 10, [half((rows,...  5.19 us
  transfers between devices with their start and end apart: 4, of which 3 were waited for; matrix products, arithmetic and copies ran while one was open for 0% of the time, Pallas kernels for 5%

profile of v2, /device:TPU:0, one launch (start us, length us, event | category | flops | bytes accessed | tf_op | source)
XLA Modules:
  0.0 135.8 jit_solution(6566681806944539569)
XLA Ops:
  0.0 1.1 constant_dynamic-slice_fusion
  1.1 5.2 %collective-permute-start = (f32[512,256]{1,0:T(8,128)S(1)}, f32[512,256]{1,0:T(8,128)S(1)}, u32[]{:S(2)}, u32[]{:S(2)}) collective-permute-start(f32[512,256]{1,0:T(8,128)S(1)} %constant_dynamic-slice_fusion), channel_id=1, source_target_pairs={{0,4},{2,6},{4,8},{5,1},{6,10},{7,3},{8,12},{9,5},{10,14},{11,7},{... | collective-permute-start | bytes 1572872 | tf_op jit(solution)/shard_map/ppermute | solution.py:258
  6.3 0.1 pad_add_fusion.place
  6.4 1.2 copy-done
  7.6 0.7 copy-done.3
  8.3 1.6 %copy-done.5 = f32[8,4,128,128]{3,2,1,0:T(8,128)S(1)} copy-done((f32[8,4,128,128]{3,2,1,0:T(8,128)S(1)}, f32[8,4,128,128]{3,2,1,0:T(8,128)}, u32[]{:S(2)}) %copy-start.5) | copy-done | bytes 2097176
  9.9 1.6 %copy-done.6 = f32[2,2,8,128,128]{4,3,2,1,0:T(8,128)S(1)} copy-done((f32[2,2,8,128,128]{4,3,2,1,0:T(8,128)S(1)}, f32[2,2,8,128,128]{4,3,2,1,0:T(8,128)}, u32[]{:S(2)}) %copy-start.6) | copy-done | bytes 2097176
  11.5 1.6 %copy-done.7 = f32[1,512,1024]{2,1,0:T(8,128)S(1)} copy-done((f32[1,512,1024]{2,1,0:T(8,128)S(1)}, f32[1,512,1024]{2,1,0:T(8,128)}, u32[]{:S(2)}) %copy-start.7) | copy-done | bytes 2097176
  13.1 0.7 copy-done.9
  13.8 0.7 copy-done.10
  14.4 7.2 %prepare.1 = (bf16[8,128,256]{2,1,0:T(8,128)(2,1)S(1)}, bf16[8,128,256]{2,1,0:T(8,128)(2,1)S(1)}, f32[1024,256]{1,0:T(8,128)S(1)}, bf16[8,128,512]{2,1,0:T(8,128...) custom-call(s32[2]{0:T(128)S(1)} %pad_add_fusion.place, ...), custom_call_target="tpu_custom_call" | custom-call | flops 8000000000 | bytes 8388608 | tf_op jit(solution)/shard_map/prepare/pallas_call | solution.py:261
  21.6 0.0 collective-permute-done.near
  21.6 0.1 collective-permute-start.1
  21.7 1.9 %collective-permute-done.1.far = f32[512,256]{1,0:T(8,128)S(1)} collective-permute-done((f32[512,256]{1,0:T(8,128)S(1)}, f32[512,256]{1,0:T(8,128)S(1)}, u32[]{:S(2)}, u32[]{:S(2)}) %collective-permute-start.1) | collective-permute-done | bytes 524320 | tf_op jit(solution)/shard_map/ppermute | solution.py:280
  23.6 0.0 copy-done.8
  23.6 5.2 %forward.1 = (bf16[1024,256]{1,0:T(8,128)(2,1)S(1)}, bf16[1024,256]{1,0:T(8,128)(2,1)S(1)}, f32[32,136,128]{2,1,0:T(8,128)S(1)}) custom-call(s32[2]{0:T(128)S(1)} %pad_add_fusion.place, s32[4,8]{1,0:T(4,128)S(1)} %bitcast.9, f32[512,256]{1,0:T(8,128)S(1)} %collective-permute-done.near, f32[512,256]{1,0:T(8,128)S(1)} %collective-permute-done.1.far, ...), custom_call_target="tpu_custom_call" | custom-call | flops 4000000000 | bytes 8388608 | tf_op jit(solution)/shard_map/forward/pallas_call | solution.py:281
  28.8 0.0 copy-start.2
  28.8 0.0 copy-start.4
  28.8 40.6 %all_to_all.15.received = f32[32,136,128]{2,1,0:T(8,128)S(1)} all-to-all(f32[32,136,128]{2,1,0:T(8,128)S(1)} %get-tuple-element.38), channel_id=1, replica_groups=mesh['sub'=32,'node'=4] {'sub'}, dimensions={0} | all-to-all | bytes 4456448 | tf_op jit(solution)/shard_map/all_to_all | solution.py:292
  69.5 0.0 copy-done.2
  69.5 0.0 copy-done.4
  69.5 1.8 %owner.1 = f32[32,128,128]{2,1,0:T(8,128)S(1)} custom-call(s32[2]{0:T(128)S(1)} %pad_add_fusion.place, s32[32,4]{1,0:T(8,128)S(1)} %bitcast.7, f32[8,4]{1,0:T(8,128)S(1)} %copy-done.4, f32[8,128]{1,0:T(8,128)S(1)} %bitcast.8, f32[32,136,128]{2,1,0:T(8,128)S(1)} %all_to_all.15.received), custom_call_target="tpu_custom_call" | custom-call | bytes 8388608 | tf_op jit(solution)/shard_map/owner/pallas_call | solution.py:294
  71.3 33.2 %all_to_all.16.picked = f32[32,128,128]{2,1,0:T(8,128)S(1)} all-to-all(f32[32,128,128]{2,1,0:T(8,128)S(1)} %owner.1), channel_id=1, replica_groups=mesh['sub'=32,'node'=4] {'sub'}, dimensions={0} | all-to-all | bytes 4194304 | tf_op jit(solution)/shard_map/all_to_all | solution.py:301
  104.6 4.6 %backward.1 = (f32[1024,128]{1,0:T(8,128)S(1)}, f32[1024,128]{1,0:T(8,128)S(1)}) custom-call(s32[2]{0:T(128)S(1)} %pad_add_fusion.place, f32[32,128,128]{2,1,0:T(8,128)S(1)} %all_to_all.16.picked, bf16[1024,2048]{1,0:T(8,128)(2,1)S(1)} %get-tuple-element.39.f_hi, bf16[1024,2048]{1,0:T(8,128)(2,1)S(1)} %get-tuple-element.40.f_lo, ...), custom_call_target="tpu_custom_call" | custom-call | flops 4000000000 | bytes 8388608 | tf_op jit(solution)/shard_map/backward/pallas_call | solution.py:302
  109.1 0.1 collective-permute-start.2
  109.2 1.9 %collective-permute-done.2.theirs = f32[1024,128]{1,0:T(8,128)S(1)} collective-permute-done((f32[1024,128]{1,0:T(8,128)S(1)}, f32[1024,128]{1,0:T(8,128)S(1)}, u32[]{:S(2)}, u32[]{:S(2)}) %collective-permute-start.2) | collective-permute-done | bytes 524320 | tf_op jit(solution)/shard_map/ppermute | solution.py:311
  111.1 0.7 pair.1
  111.9 1.7 %collective-permute-start.3 = (f32[512,128]{1,0:T(8,128)S(1)}, f32[512,128]{1,0:T(8,128)S(1)}, u32[]{:S(2)}, u32[]{:S(2)}) collective-permute-start(f32[512,128]{1,0:T(8,128)S(1)} %get-tuple-element.48), channel_id=1, source_target_pairs={{0,2},{1,3},{2,0},{3,1},{4,6},{5,7},{6,4},{7,5},{8,10},{9,11},{10,... | collective-permute-start | bytes 786440 | tf_op jit(solution)/shard_map/ppermute | solution.py:315
  113.6 6.7 %collective-permute-done.3.theirs = f32[512,128]{1,0:T(8,128)S(1)} collective-permute-done((f32[512,128]{1,0:T(8,128)S(1)}, f32[512,128]{1,0:T(8,128)S(1)}, u32[]{:S(2)}, u32[]{:S(2)}) %collective-permute-start.3) | collective-permute-done | bytes 262176 | tf_op jit(solution)/shard_map/ppermute | solution.py:315
  120.3 0.8 update.1
  121.1 13.8 %all_to_all.17.squares = f32[32,1,128]{2,1,0:T(1,128)S(1)} all-to-all(f32[32,1,128]{2,1,0:T(1,128)S(1)} %get-tuple-element.50), channel_id=1, replica_groups=mesh['sub'=32,'node'=4] {'sub'}, dimensions={0} | all-to-all | bytes 32768 | tf_op jit(solution)/shard_map/all_to_all | solution.py:322
  135.0 0.9 scale.1
  (11 shorter events, 0.0 us)
Async XLA Ops:
  1.1 20.5 %collective-permute-start = (f32[512,256]{1,0:T(8,128)S(1)}, f32[512,256]{1,0:T(8,128)S(1)}, u32[]{:S(2)}, u32[]{:S(2)}) collective-permute-start(f32[512,256]{1,0:T(8,128)S(1)} %constant_dynamic-slice_fusion), channel_id=1, source_target_pairs={{0,4},{2,6},{4,8},{5,1},{6,10},{7,3},{8,12},{9,5},{10,14},{11,7},{... | collective-permute-start | bytes 1572872 | tf_op jit(solution)/shard_map/ppermute | solution.py:258
  6.4 1.2 copy-start
  7.6 0.7 copy-start.3
  8.3 1.6 %copy-start.5 = (f32[8,4,128,128]{3,2,1,0:T(8,128)S(1)}, f32[8,4,128,128]{3,2,1,0:T(8,128)}, u32[]{:S(2)}) copy-start(f32[8,4,128,128]{3,2,1,0:T(8,128)} %mats.1) | copy-start | bytes 6291460
  9.9 1.6 %copy-start.6 = (f32[2,2,8,128,128]{4,3,2,1,0:T(8,128)S(1)}, f32[2,2,8,128,128]{4,3,2,1,0:T(8,128)}, u32[]{:S(2)}) copy-start(f32[2,2,8,128,128]{4,3,2,1,0:T(8,128)} %inverses.1) | copy-start | bytes 6291460
  11.5 1.6 %copy-start.7 = (f32[1,512,1024]{2,1,0:T(8,128)S(1)}, f32[1,512,1024]{2,1,0:T(8,128)}, u32[]{:S(2)}) copy-start(f32[1,512,1024]{2,1,0:T(8,128)} %panel.1) | copy-start | bytes 6291460
  13.1 0.7 copy-start.9
  13.7 0.7 copy-start.10
  14.4 9.2 %copy-start.8 = (s32[8,4]{0,1:T(4,128)S(1)}, s32[8,4]{0,1:T(4,128)}, u32[]{:S(2)}) copy-start(s32[8,4]{0,1:T(4,128)} %param.12) | copy-start | bytes 388
  21.6 2.0 %collective-permute-start.1 = (f32[512,256]{1,0:T(8,128)S(1)}, f32[512,256]{1,0:T(8,128)S(1)}, u32[]{:S(2)}, u32[]{:S(2)}) collective-permute-start(f32[512,256]{1,0:T(8,128)S(1)} %collective-permute-done.near), channel_id=1, source_target_pairs={{0,1},{1,0},{2,3},{3,2},{4,5},{5,4},{6,7},{7,6},{8,9},{9,8},{10,11... | collective-permute-start | bytes 1572872 | tf_op jit(solution)/shard_map/ppermute | solution.py:280
  28.8 40.7 %copy-start.2 = (f32[1024]{0:T(1024)S(1)}, f32[1024]{0:T(1024)}, u32[]{:S(2)}) copy-start(f32[1024]{0:T(1024)} %param.16) | copy-start | bytes 12292
  28.8 40.7 %copy-start.4 = (f32[8,4]{1,0:T(8,128)S(1)}, f32[8,4]{1,0:T(8,128)}, u32[]{:S(2)}) copy-start(f32[8,4]{1,0:T(8,128)} %constant.29.clone.table) | copy-start | bytes 388
  104.6 15.7 %copy-start.1 = (f32[1024,256]{1,0:T(8,128)S(1)}, f32[1024,256]{1,0:T(8,128)}, u32[]{:S(2)}) copy-start(f32[1024,256]{1,0:T(8,128)} %vectors.1) | copy-start | bytes 3145732
  109.1 2.0 %collective-permute-start.2 = (f32[1024,128]{1,0:T(8,128)S(1)}, f32[1024,128]{1,0:T(8,128)S(1)}, u32[]{:S(2)}, u32[]{:S(2)}) collective-permute-start(f32[1024,128]{1,0:T(8,128)S(1)} %get-tuple-element.46), channel_id=1, source_target_pairs={{0,1},{1,0},{2,3},{3,2},{4,5},{5,4},{6,7},{7,6},{8,9},{9,8},{10,11... | collective-permute-start | bytes 1572872 | tf_op jit(solution)/shard_map/ppermute | solution.py:311
  111.9 8.4 %collective-permute-start.3 = (f32[512,128]{1,0:T(8,128)S(1)}, f32[512,128]{1,0:T(8,128)S(1)}, u32[]{:S(2)}, u32[]{:S(2)}) collective-permute-start(f32[512,128]{1,0:T(8,128)S(1)} %get-tuple-element.48), channel_id=1, source_target_pairs={{0,2},{1,3},{2,0},{3,1},{4,6},{5,7},{6,4},{7,5},{8,10},{9,11},{10,... | collective-permute-start | bytes 786440 | tf_op jit(solution)/shard_map/ppermute | solution.py:315

commit v3 on v2

--- a/solution.py
+++ b/solution.py
@@ -3,7 +3,6 @@
 
 import jax
 import jax.numpy as jnp
-import numpy as np
 from jax import lax
 from jax.experimental import pallas as pl
 from jax.experimental.pallas import tpu as pltpu
@@ -20,6 +19,11 @@
 BF16 = jnp.bfloat16
 VMEM = pl.BlockSpec(memory_space=pltpu.VMEM)
 SMEM = pl.BlockSpec(memory_space=pltpu.SMEM)
+HBM = pl.BlockSpec(memory_space=pltpu.HBM)
+
+THETA = [math.pi * (j + 0.5) / NODES for j in range(NODES)]
+Z_REAL, Z_IMAG = [math.cos(t) for t in THETA], [math.sin(t) for t in THETA]
+W_REAL, W_IMAG = [2.0 * v / NODES for v in Z_REAL], [2.0 * v / NODES for v in Z_IMAG]
 
 
 def split(x):
@@ -43,28 +47,64 @@
     )
 
 
+def constant(node, values):
+    out = jnp.float32(values[0])
+    for k in range(1, NODES):
+        out = jnp.where(node == k, jnp.float32(values[k]), out)
+    return out
+
+
 def prepare_kernel(
-    place, sep_map, table, own, ritz, mats, inverses, panel,
+    place, sep_map, own_hbm, ritz_hbm, mats_hbm, inverses_hbm, panel_hbm,
     own_hi, own_lo, scaled, m_hi, m_lo, e_hi, e_lo, f_hi, f_lo, w_hi, w_lo, ids,
+    own, ritz, mats, inverses, panel, ids_sem, ritz_sem, sems, map_copy,
 ):
     node = place[1] * LOCAL
-    blocks, sep = own.shape[0] // BLK, panel.shape[1]
-    scaled[...] = own[...] * ritz[...]
+    blocks, sep = own.shape[0] // BLK, panel.shape[0]
     parts = [(n, c) for n in range(LOCAL) for c in range(2)]
+    copies = []
     for g in range(blocks):
+        rows = pl.ds(g * BLK, BLK)
+        copies.append(
+            [
+                pltpu.make_async_copy(src, dst, sems.at[g, k])
+                for k, (src, dst) in enumerate(
+                    (
+                        (panel_hbm.at[0, :, rows], panel.at[:, rows]),
+                        (inverses_hbm.at[:, :, g], inverses.at[g]),
+                        (mats_hbm.at[g], mats.at[g]),
+                        (own_hbm.at[rows, :], own.at[rows, :]),
+                    )
+                )
+            ]
+        )
+    small = [
+        pltpu.make_async_copy(ritz_hbm, ritz, ritz_sem),
+        pltpu.make_async_copy(sep_map, map_copy, ids_sem),
+    ]
+    for copy in copies[0] + small + sum(copies[1:], []):
+        copy.start()
+    for copy in small:
+        copy.wait()
+    for g in range(blocks):
+        for copy in copies[g]:
+            copy.wait()
         rows = slice(g * BLK, (g + 1) * BLK)
+        scaled[rows, :] = own[rows, :] * ritz[...]
         own_hi[g], own_lo[g] = split(own[rows, :])
         m_hi[g], m_lo[g] = split(jnp.concatenate([mats[g, q] for q in range(4)], 1))
-        weighted = [inverses[n, 0, g] * table[node + n, 2] for n in range(LOCAL)]
-        weighted += [inverses[n, 1, g] * -table[node + n, 3] for n in range(LOCAL)]
+        weighted = []
+        for n in range(LOCAL):
+            weighted.append(inverses[g, n, 0] * constant(node + n, W_REAL))
+            weighted.append(inverses[g, n, 1] * -constant(node + n, W_IMAG))
         w_hi[g], w_lo[g] = split(sum(weighted[1:], weighted[0]))
-        p_hi, p_lo = split(panel[0, :, rows])
-        d_hi, d_lo = split(jnp.concatenate([inverses[n, c, g] for n, c in parts], 1))
+        p_hi, p_lo = split(panel[:, rows])
+        d_hi, d_lo = split(jnp.concatenate([inverses[g, n, c] for n, c in parts], 1))
         e = dot(
             jnp.concatenate([p_hi, p_lo, p_hi], 1), jnp.concatenate([d_hi, d_hi, d_lo], 0)
         )
         d_hi, d_lo = split(
-            jnp.concatenate([-inverses[n, c, g] if c == 0 else inverses[n, c, g] for n, c in parts], 0)
+            jnp.concatenate([-inverses[g, n, c] if c == 0 else inverses[g, n, c] for n, c in parts], 0)
         )
         f = dot(
             jnp.concatenate([d_hi, d_lo, d_hi], 1),
@@ -78,7 +118,7 @@
     lane = lax.broadcasted_iota(jnp.int32, ids.shape, 1)
     value = jnp.zeros(ids.shape, jnp.int32)
     for p in range(4):
-        value = jnp.where(lane == p, sep_map[0, p], value)
+        value = jnp.where(lane == p, map_copy[0, p], value)
     ids[...] = value.astype(F32)
 
 
@@ -113,11 +153,11 @@
     pieces[:, 128:136, :] = jnp.broadcast_to(ids[...][None], (32, 8, LANES))
 
 
-def owner_kernel(place, maps, table, shift, received, back, total):
+def owner_kernel(place, maps, shift, received, back, total):
     sub = place[0]
     node = place[1] * LOCAL + sub // 16
     first_row = (sub % 16) * 8
-    z_r, z_i, w_r, w_i = (table[node, k] for k in range(4))
+    z_r, z_i, w_r, w_i = (constant(node, v) for v in (Z_REAL, Z_IMAG, W_REAL, W_IMAG))
     total[...] = jnp.zeros_like(total)
 
     def add(t, carry):
@@ -239,9 +279,6 @@
     subs, nodes = lax.axis_size("sub"), lax.axis_size("node")
     sub, node = lax.axis_index("sub"), lax.axis_index("node")
     place = jnp.stack([sub, node]).astype(jnp.int32)
-    theta = math.pi * (np.arange(NODES) + 0.5) / NODES
-    z = np.stack([np.cos(theta), np.sin(theta)], 1)
-    table = jnp.asarray(np.concatenate([z, 2.0 * z / NODES], 1), F32)
 
     halo_rows = HALO * BLK
     edge = lax.dynamic_slice_in_dim(
@@ -261,7 +298,7 @@
     prepared = call(
         prepare_kernel,
         "prepare",
-        [SMEM, SMEM, SMEM] + [VMEM] * 5,
+        [SMEM] + [HBM] * 6,
         [half((blocks, BLK, width))] * 2
         + [(rows, width)]
         + [half((blocks, BLK, 4 * BLK))] * 2
@@ -269,11 +306,27 @@
         + [half((rows, 4 * sep))] * 2
         + [half((blocks, BLK, BLK))] * 2
         + [(8, LANES)],
+        [
+            pltpu.VMEM((rows, width), F32),
+            pltpu.VMEM((1, width), F32),
+            pltpu.VMEM(matrix_blocks.shape, F32),
+            pltpu.VMEM((blocks, LOCAL, 2, BLK, BLK), F32),
+            pltpu.VMEM((sep, rows), F32),
+            pltpu.SemaphoreType.DMA,
+            pltpu.SemaphoreType.DMA,
+            pltpu.SemaphoreType.DMA((blocks, 4)),
+            pltpu.SMEM(separator_map.shape, jnp.int32),
+        ],
         limit=24,
         flops=8 * 10**9,
     )(
-        place, separator_map, table, search_vectors, ritz_values[None, :],
-        matrix_blocks, inverses, panels,
+        place, *(
+            pltpu.with_memory_space_constraint(x, pltpu.HBM)
+            for x in (
+                separator_map, search_vectors, ritz_values[None, :],
+                matrix_blocks, inverses, panels,
+            )
+        )
     )
     own_hi, own_lo, scaled, m_hi, m_lo, e_hi, e_lo, f_hi, f_lo, w_hi, w_lo, ids = prepared
     near, ids = lax.optimization_barrier((near, ids))
@@ -294,10 +347,10 @@
     (back,) = call(
         owner_kernel,
         "owner",
-        [SMEM, SMEM, SMEM, VMEM, VMEM],
+        [SMEM, SMEM, VMEM, VMEM],
         [(subs, 128, LANES)],
         [pltpu.VMEM((GROUPS, 2, 16, LANES), F32)],
-    )(place, maps, table, separator_shift.reshape(GROUPS, LANES), received)
+    )(place, maps, separator_shift.reshape(GROUPS, LANES), received)
     picked = lax.all_to_all(back, "sub", 0, 0, tiled=True)
     keep, send = call(
         backward_kernel,

time: 136 us -> 135 us (level)
  local copies, waits for them, and re-layouts: 9.11 us -> 1.09 us
  Pallas kernels: 21.2 us -> 25.8 us
  blocking collectives: 87.7 us -> 90.3 us
    unnamed x22 -> x6, local copies, waits for them, and re-layouts: 8.04 us -> 0.01 us
    pallas_call x2, Pallas kernels: 9.02 us -> 13.5 us  [the longest x1 11.7 us: shards(): call(prepare_kernel, 'prepare', [SMEM] + [HBM] * 6, [half((blocks, BLK, w...]
    all_to_all x1, blocking collectives: 40.6 us -> 43.7 us  [shards(): received = lax.all_to_all(pieces, 'sub', 0, 0, tiled=True)]
  transfers between devices with their start and end apart: 4 -> 4, of which waited for: 3 -> 4; matrix products, arithmetic and copies ran while one was open for 0% -> 0% of each run, Pallas kernels for 5% -> 9%
where the time goes in v3:
time: 135 us
  blocking collectives  90.3 us (67%)
  Pallas kernels  25.8 us (19%)
  waiting for transfers between devices  11.7 us (9%)
  starting transfers between devices  6.06 us (4%)
    all_to_all x1, blocking collectives, shards(): received = lax.all_to_all(pieces, 'sub', 0, 0, tiled=True)  43.7 us
    all_to_all x1, blocking collectives, shards(): picked = lax.all_to_all(back, 'sub', 0, 0, tiled=True)  33.3 us
    all_to_all x1, blocking collectives, shards(): gathered = lax.all_to_all(squares, 'sub', 0, 0, tiled=True)  13.3 us
    pallas_call x1, Pallas kernels, shards(): call(prepare_kernel, 'prepare', [SMEM] + [HBM] * 6, [half((blocks, BLK, w...  11.7 us
    ppermute x1, waiting for transfers between devices, shards(): theirs = lax.ppermute(send, 'node', swap_chip)  7.67 us
    ppermute x1, starting transfers between devices, shards(): near = lax.ppermute(edge, ('sub', 'node'), ring)  5.21 us
    pallas_call x1, Pallas kernels, shards(): call(forward_kernel, 'forward', [SMEM, SMEM] + [VMEM] * 10, [half((rows,...  5.2 us
    pallas_call x1, Pallas kernels, shards(): call(backward_kernel, 'backward', [SMEM] + [VMEM] * 7, [(rows, LANES), (r...  4.62 us
  transfers between devices with their start and end apart: 4, of which 4 were waited for; matrix products, arithmetic and copies ran while one was open for 0% of the time, Pallas kernels for 9%

profile of v3, /device:TPU:0, one launch (start us, length us, event | category | flops | bytes accessed | tf_op | source)
XLA Modules:
  0.0 135.0 jit_solution(13399266787647817666)
XLA Ops:
  0.0 1.1 constant_dynamic-slice_fusion
  1.1 5.2 %collective-permute-start = (f32[512,256]{1,0:T(8,128)S(1)}, f32[512,256]{1,0:T(8,128)S(1)}, u32[]{:S(2)}, u32[]{:S(2)}) collective-permute-start(f32[512,256]{1,0:T(8,128)S(1)} %constant_dynamic-slice_fusion), channel_id=1, source_target_pairs={{0,4},{2,6},{4,8},{5,1},{6,10},{7,3},{8,12},{9,5},{10,14},{11,7},{... | collective-permute-start | bytes 1572872 | tf_op jit(solution)/shard_map/ppermute | solution.py:295
  6.3 0.1 pad_add_fusion.place
  6.4 0.0 copy-start.2
  6.4 11.7 %prepare.1 = (bf16[8,128,256]{2,1,0:T(8,128)(2,1)S(1)}, bf16[8,128,256]{2,1,0:T(8,128)(2,1)S(1)}, f32[1024,256]{1,0:T(8,128)S(1)}, bf16[8,128,512]{2,1,0:T(8,128...) custom-call(s32[2]{0:T(128)S(1)} %pad_add_fusion.place, ...), custom_call_target="tpu_custom_call" | custom-call | flops 8000000000 | bytes 8388608 | tf_op jit(solution)/shard_map/prepare/pallas_call | solution.py:298
  18.1 0.2 collective-permute-done.near
  18.3 0.0 collective-permute-start.1
  18.3 1.9 %collective-permute-done.1.far = f32[512,256]{1,0:T(8,128)S(1)} collective-permute-done((f32[512,256]{1,0:T(8,128)S(1)}, f32[512,256]{1,0:T(8,128)S(1)}, u32[]{:S(2)}, u32[]{:S(2)}) %collective-permute-start.1) | collective-permute-done | bytes 524320 | tf_op jit(solution)/shard_map/ppermute | solution.py:333
  20.2 0.0 copy-done.2
  20.2 5.2 %forward.1 = (bf16[1024,256]{1,0:T(8,128)(2,1)S(1)}, bf16[1024,256]{1,0:T(8,128)(2,1)S(1)}, f32[32,136,128]{2,1,0:T(8,128)S(1)}) custom-call(s32[2]{0:T(128)S(1)} %pad_add_fusion.place, s32[4,8]{1,0:T(4,128)S(1)} %bitcast.9, f32[512,256]{1,0:T(8,128)S(1)} %collective-permute-done.near, f32[512,256]{1,0:T(8,128)S(1)} %collective-permute-done.1.far, ...), custom_call_target="tpu_custom_call" | custom-call | flops 4000000000 | bytes 8388608 | tf_op jit(solution)/shard_map/forward/pallas_call | solution.py:334
  25.5 0.0 copy-start.1
  25.5 43.7 %all_to_all.15.received = f32[32,136,128]{2,1,0:T(8,128)S(1)} all-to-all(f32[32,136,128]{2,1,0:T(8,128)S(1)} %get-tuple-element.38), channel_id=1, replica_groups=mesh['sub'=32,'node'=4] {'sub'}, dimensions={0} | all-to-all | bytes 4456448 | tf_op jit(solution)/shard_map/all_to_all | solution.py:345
  69.1 0.0 copy-done.1
  69.2 1.8 %owner.1 = f32[32,128,128]{2,1,0:T(8,128)S(1)} custom-call(s32[2]{0:T(128)S(1)} %pad_add_fusion.place, s32[32,4]{1,0:T(8,128)S(1)} %bitcast.7, f32[8,128]{1,0:T(8,128)S(1)} %bitcast.8, f32[32,136,128]{2,1,0:T(8,128)S(1)} %all_to_all.15.received), custom_call_target="tpu_custom_call" | custom-call | bytes 8388608 | tf_op jit(solution)/shard_map/owner/pallas_call | solution.py:347
  70.9 33.3 %all_to_all.16.picked = f32[32,128,128]{2,1,0:T(8,128)S(1)} all-to-all(f32[32,128,128]{2,1,0:T(8,128)S(1)} %owner.1), channel_id=1, replica_groups=mesh['sub'=32,'node'=4] {'sub'}, dimensions={0} | all-to-all | bytes 4194304 | tf_op jit(solution)/shard_map/all_to_all | solution.py:354
  104.2 0.0 copy-start
  104.2 4.6 %backward.1 = (f32[1024,128]{1,0:T(8,128)S(1)}, f32[1024,128]{1,0:T(8,128)S(1)}) custom-call(s32[2]{0:T(128)S(1)} %pad_add_fusion.place, f32[32,128,128]{2,1,0:T(8,128)S(1)} %all_to_all.16.picked, bf16[1024,2048]{1,0:T(8,128)(2,1)S(1)} %get-tuple-element.39.f_hi, bf16[1024,2048]{1,0:T(8,128)(2,1)S(1)} %get-tuple-element.40.f_lo, ...), custom_call_target="tpu_custom_call" | custom-call | flops 4000000000 | bytes 8388608 | tf_op jit(solution)/shard_map/backward/pallas_call | solution.py:355
  108.8 0.1 collective-permute-start.2
  108.9 1.9 %collective-permute-done.2.theirs = f32[1024,128]{1,0:T(8,128)S(1)} collective-permute-done((f32[1024,128]{1,0:T(8,128)S(1)}, f32[1024,128]{1,0:T(8,128)S(1)}, u32[]{:S(2)}, u32[]{:S(2)}) %collective-permute-start.2) | collective-permute-done | bytes 524320 | tf_op jit(solution)/shard_map/ppermute | solution.py:364
  110.8 0.7 pair.1
  111.6 0.8 collective-permute-start.3
  112.3 7.7 %collective-permute-done.3.theirs = f32[512,128]{1,0:T(8,128)S(1)} collective-permute-done((f32[512,128]{1,0:T(8,128)S(1)}, f32[512,128]{1,0:T(8,128)S(1)}, u32[]{:S(2)}, u32[]{:S(2)}) %collective-permute-start.3) | collective-permute-done | bytes 262176 | tf_op jit(solution)/shard_map/ppermute | solution.py:368
  120.0 0.0 copy-done
  120.0 0.8 update.1
  120.8 13.3 %all_to_all.17.squares = f32[32,1,128]{2,1,0:T(1,128)S(1)} all-to-all(f32[32,1,128]{2,1,0:T(1,128)S(1)} %get-tuple-element.50), channel_id=1, replica_groups=mesh['sub'=32,'node'=4] {'sub'}, dimensions={0} | all-to-all | bytes 32768 | tf_op jit(solution)/shard_map/all_to_all | solution.py:375
  134.2 0.9 scale.1
  (1 shorter events, 0.0 us)
Async XLA Ops:
  1.1 17.3 %collective-permute-start = (f32[512,256]{1,0:T(8,128)S(1)}, f32[512,256]{1,0:T(8,128)S(1)}, u32[]{:S(2)}, u32[]{:S(2)}) collective-permute-start(f32[512,256]{1,0:T(8,128)S(1)} %constant_dynamic-slice_fusion), channel_id=1, source_target_pairs={{0,4},{2,6},{4,8},{5,1},{6,10},{7,3},{8,12},{9,5},{10,14},{11,7},{... | collective-permute-start | bytes 1572872 | tf_op jit(solution)/shard_map/ppermute | solution.py:295
  6.4 13.9 %copy-start.2 = (s32[8,4]{0,1:T(4,128)S(1)}, s32[8,4]{0,1:T(4,128)}, u32[]{:S(2)}) copy-start(s32[8,4]{0,1:T(4,128)} %param.11) | copy-start | bytes 388
  18.3 1.9 %collective-permute-start.1 = (f32[512,256]{1,0:T(8,128)S(1)}, f32[512,256]{1,0:T(8,128)S(1)}, u32[]{:S(2)}, u32[]{:S(2)}) collective-permute-start(f32[512,256]{1,0:T(8,128)S(1)} %collective-permute-done.near), channel_id=1, source_target_pairs={{0,1},{1,0},{2,3},{3,2},{4,5},{5,4},{6,7},{7,6},{8,9},{9,8},{10,11... | collective-permute-start | bytes 1572872 | tf_op jit(solution)/shard_map/ppermute | solution.py:333
  25.5 43.7 %copy-start.1 = (f32[1024]{0:T(1024)S(1)}, f32[1024]{0:T(1024)}, u32[]{:S(2)}) copy-start(f32[1024]{0:T(1024)} %param.15) | copy-start | bytes 12292
  104.2 15.8 %copy-start = (f32[1024,256]{1,0:T(8,128)S(1)}, f32[1024,256]{1,0:T(8,128)}, u32[]{:S(2)}) copy-start(f32[1024,256]{1,0:T(8,128)} %vectors.1) | copy-start | bytes 3145732
  108.8 2.0 %collective-permute-start.2 = (f32[1024,128]{1,0:T(8,128)S(1)}, f32[1024,128]{1,0:T(8,128)S(1)}, u32[]{:S(2)}, u32[]{:S(2)}) collective-permute-start(f32[1024,128]{1,0:T(8,128)S(1)} %get-tuple-element.46), channel_id=1, source_target_pairs={{0,1},{1,0},{2,3},{3,2},{4,5},{5,4},{6,7},{7,6},{8,9},{9,8},{10,11... | collective-permute-start | bytes 1572872 | tf_op jit(solution)/shard_map/ppermute | solution.py:364
  111.6 8.4 %collective-permute-start.3 = (f32[512,128]{1,0:T(8,128)S(1)}, f32[512,128]{1,0:T(8,128)S(1)}, u32[]{:S(2)}, u32[]{:S(2)}) collective-permute-start(f32[512,128]{1,0:T(8,128)S(1)} %get-tuple-element.48), channel_id=1, source_target_pairs={{0,2},{1,3},{2,0},{3,1},{4,6},{5,7},{6,4},{7,5},{8,10},{9,11},{10,... | collective-permute-start | bytes 786440 | tf_op jit(solution)/shard_map/ppermute | solution.py:368

commit v4 on v3

--- a/solution.py
+++ b/solution.py
@@ -57,42 +57,37 @@
 def prepare_kernel(
     place, sep_map, own_hbm, ritz_hbm, mats_hbm, inverses_hbm, panel_hbm,
     own_hi, own_lo, scaled, m_hi, m_lo, e_hi, e_lo, f_hi, f_lo, w_hi, w_lo, ids,
-    own, ritz, mats, inverses, panel, ids_sem, ritz_sem, sems, map_copy,
+    own, ritz, mats, inverses, panel, ids_sem, ritz_sem, mats_sem, panel_sem, sems, map_copy,
 ):
-    node = place[1] * LOCAL
+    node, core = place[1] * LOCAL, place[1] % 2
     blocks, sep = own.shape[0] // BLK, panel.shape[0]
+    per_core = blocks // 2
     parts = [(n, c) for n in range(LOCAL) for c in range(2)]
     copies = []
     for g in range(blocks):
         rows = pl.ds(g * BLK, BLK)
         copies.append(
-            [
-                pltpu.make_async_copy(src, dst, sems.at[g, k])
-                for k, (src, dst) in enumerate(
-                    (
-                        (panel_hbm.at[0, :, rows], panel.at[:, rows]),
-                        (inverses_hbm.at[:, :, g], inverses.at[g]),
-                        (mats_hbm.at[g], mats.at[g]),
-                        (own_hbm.at[rows, :], own.at[rows, :]),
-                    )
-                )
-            ]
+            (
+                pltpu.make_async_copy(inverses_hbm.at[:, :, g], inverses.at[g], sems.at[g, 0]),
+                pltpu.make_async_copy(own_hbm.at[rows, :], own.at[rows, :], sems.at[g, 1]),
+            )
         )
+    my_mats = pltpu.make_async_copy(
+        mats_hbm.at[pl.ds(core * per_core, per_core)], mats, mats_sem
+    )
+    whole_panel = pltpu.make_async_copy(panel_hbm.at[0], panel, panel_sem)
     small = [
         pltpu.make_async_copy(ritz_hbm, ritz, ritz_sem),
         pltpu.make_async_copy(sep_map, map_copy, ids_sem),
     ]
-    for copy in copies[0] + small + sum(copies[1:], []):
+    for copy in [whole_panel, *copies[0], *sum(copies[1:], ()), my_mats] + small:
         copy.start()
-    for copy in small:
-        copy.wait()
+    whole_panel.wait()
     for g in range(blocks):
         for copy in copies[g]:
             copy.wait()
         rows = slice(g * BLK, (g + 1) * BLK)
-        scaled[rows, :] = own[rows, :] * ritz[...]
         own_hi[g], own_lo[g] = split(own[rows, :])
-        m_hi[g], m_lo[g] = split(jnp.concatenate([mats[g, q] for q in range(4)], 1))
         weighted = []
         for n in range(LOCAL):
             weighted.append(inverses[g, n, 0] * constant(node + n, W_REAL))
@@ -111,10 +106,19 @@
             jnp.concatenate([p_hi, p_hi, p_lo], 1),
             ((1,), (1,)),
         )
+        side, first = divmod(g, per_core)
+        cols = slice(first * BLK, (first + 1) * BLK)
         for k in range(2 * LOCAL):
             span, block = slice(k * sep, (k + 1) * sep), slice(k * BLK, (k + 1) * BLK)
-            e_hi[span, rows], e_lo[span, rows] = split(e[:, block])
+            e_hi[side, span, cols], e_lo[side, span, cols] = split(e[:, block])
             f_hi[rows, span], f_lo[rows, span] = split(f[block, :])
+    for copy in small:
+        copy.wait()
+    my_mats.wait()
+    for g in range(per_core):
+        rows = pl.ds(pl.multiple_of((core * per_core + g) * BLK, BLK), BLK)
+        scaled[g] = own[rows, :] * ritz[...]
+        m_hi[g], m_lo[g] = split(jnp.concatenate([mats[g, q] for q in range(4)], 1))
     lane = lax.broadcasted_iota(jnp.int32, ids.shape, 1)
     value = jnp.zeros(ids.shape, jnp.int32)
     for p in range(4):
@@ -122,28 +126,43 @@
     ids[...] = value.astype(F32)
 
 
-def forward_kernel(
-    place, lists, near, far, own_hi, own_lo, scaled, m_hi, m_lo, e_hi, e_lo, ids,
-    r_hi, r_lo, pieces, ext_hi, ext_lo,
+def residual_kernel(
+    place, lists, halo, own_hi, own_lo, scaled, m_hi, m_lo, residual, r_hi, r_lo, ext_hi, ext_lo
 ):
     sub, core = place[0], place[1] % 2
-    blocks = own_hi.shape[0]
-    for ref, start in ((near, core * 12), (far, 12 - core * 12)):
-        hi, lo = split(ref[...].reshape(HALO, BLK, ref.shape[1]))
-        ext_hi[pl.ds(start, HALO)] = hi
-        ext_lo[pl.ds(start, HALO)] = lo
-    ext_hi[HALO : HALO + blocks] = own_hi[...]
-    ext_lo[HALO : HALO + blocks] = own_lo[...]
-    for g in range(blocks):
-        where = [lists[q, g] - sub * blocks + HALO for q in range(4)]
+    blocks, per_core = own_hi.shape[0], m_hi.shape[0]
+    hi, lo = split(halo[...].reshape(HALO, BLK, halo.shape[1]))
+    ext_hi[pl.ds(core * blocks, HALO)] = hi
+    ext_lo[pl.ds(core * blocks, HALO)] = lo
+    start = HALO - core * HALO
+    ext_hi[pl.ds(start, blocks)] = own_hi[...]
+    ext_lo[pl.ds(start, blocks)] = own_lo[...]
+    for g in range(per_core):
+        where = [lists[q, core * per_core + g] - sub * blocks + start for q in range(4)]
         rhs = [jnp.concatenate([e[w] for w in where], 0) for e in (ext_hi, ext_lo)]
         rows = slice(g * BLK, (g + 1) * BLK)
-        r_hi[rows, :], r_lo[rows, :] = split(dot3((m_hi[g], m_lo[g]), rhs) - scaled[rows, :])
-    sep = e_hi.shape[0] // (2 * LOCAL)
-    res = r_hi[...], r_lo[...]
+        res = dot3((m_hi[g], m_lo[g]), rhs) - scaled[g]
+        residual[rows, :] = res
+        r_hi[rows, :], r_lo[rows, :] = split(res)
+
+
+def mine_kernel(place, e_hi, e_lo, r_hi, r_lo, sums):
+    core = place[1] % 2
+    sums[...] = dot3((e_hi[core], e_lo[core]), (r_hi[...], r_lo[...]))
+
+
+def theirs_kernel(
+    place, sums, theirs, e_hi, e_lo, m_hi, m_lo, ids, r_hi, r_lo, pieces
+):
+    core = place[1] % 2
+    other = 1 - core
+    hi, lo = split(theirs[...])
+    r_hi[other], r_lo[other] = hi, lo
+    r_hi[core], r_lo[core] = m_hi[...], m_lo[...]
+    sep = e_hi.shape[1] // (2 * LOCAL)
     for k in range(2 * LOCAL):
         span = slice(k * sep, (k + 1) * sep)
-        part = dot3((e_hi[span, :], e_lo[span, :]), res)
+        part = sums[span, :] + dot3((e_hi[other, span, :], e_lo[other, span, :]), (hi, lo))
         n, c = divmod(k, 2)
         for p in range(4):
             for h in range(2):
@@ -193,11 +212,8 @@
     lax.fori_loop(0, 32, give, 0, unroll=4)
 
 
-def backward_kernel(
-    place, picked, f_hi, f_lo, r_hi, r_lo, w_hi, w_lo, keep, send, x_hi, x_lo
-):
-    core = place[1] % 2
-    sep = f_hi.shape[1] // (2 * LOCAL)
+def coarse_halves(picked, x_hi, x_lo):
+    sep = x_hi.shape[0] // (2 * LOCAL)
     for k in range(2 * LOCAL):
         n, c = divmod(k, 2)
         for p in range(4):
@@ -207,18 +223,33 @@
                 rows = slice(k * sep + p * BLK, k * sep + (p + 1) * BLK)
                 cols = slice(h * LANES, (h + 1) * LANES)
                 x_hi[rows, cols], x_lo[rows, cols] = split(tile)
-    coarse = x_hi[...], x_lo[...]
-    for g in range(0, w_hi.shape[0], 2):
-        both = slice(g * BLK, (g + 2) * BLK)
+
+
+def solve(side, core, coarse, f_hi, f_lo, r_hi, r_lo, w_hi, w_lo, keep, send):
+    per_side = w_hi.shape[0] // 2
+    for g in range(0, per_side, 2):
+        first = side * per_side + g
+        both = slice(first * BLK, (first + 2) * BLK)
         back = dot3((f_hi[both, :], f_lo[both, :]), coarse)
         for i in range(2):
             rows = slice((g + i) * BLK, (g + i + 1) * BLK)
             weighted = back[i * BLK : (i + 1) * BLK] + dot3(
-                (w_hi[g + i], w_lo[g + i]), (r_hi[rows, :], r_lo[rows, :])
+                (w_hi[first + i], w_lo[first + i]), (r_hi[side, rows, :], r_lo[side, rows, :])
             )
             low, high = halves(weighted[:, :LANES], weighted[:, LANES:])
             keep[rows, :] = jnp.where(core == 0, low, high)
             send[rows, :] = jnp.where(core == 0, high, low)
+
+
+def first_kernel(place, picked, f_hi, f_lo, r_hi, r_lo, w_hi, w_lo, keep, send, x_hi, x_lo):
+    coarse_halves(picked, x_hi, x_lo)
+    coarse = x_hi[...], x_lo[...]
+    solve(0, place[1] % 2, coarse, f_hi, f_lo, r_hi, r_lo, w_hi, w_lo, keep, send)
+
+
+def second_kernel(place, x_hi, x_lo, f_hi, f_lo, r_hi, r_lo, w_hi, w_lo, keep, send):
+    coarse = x_hi[...], x_lo[...]
+    solve(1, place[1] % 2, coarse, f_hi, f_lo, r_hi, r_lo, w_hi, w_lo, keep, send)
 
 
 def pair_kernel(place, mine, theirs, keep, send):
@@ -230,25 +261,32 @@
     send[...] = jnp.where(first, high, low)
 
 
-def update_kernel(place, mine, theirs, vectors, update, squares):
+def update_kernel(place, mine_a, theirs_a, mine_b, theirs_b, vectors, update, squares):
     first, core = place[1] // 2 == 0, place[1] % 2
-    half = mine.shape[0]
+    quarter = mine_a.shape[0]
     mid = vectors.shape[1] // 2
     own = jnp.where(first, vectors[:, :mid], vectors[:, mid:])
-    low, high = halves(own[:half], own[half:])
-    new = jnp.where(core == 0, low, high) - (mine[...] + theirs[...])
-    update[...] = new
-    sums = jnp.sum(new * new, axis=0, keepdims=True)
+    sums = jnp.zeros((1, LANES), F32)
+    for side, (mine, theirs) in enumerate(((mine_a, theirs_a), (mine_b, theirs_b))):
+        top = own[2 * side * quarter : (2 * side + 1) * quarter]
+        low, high = halves(top, own[(2 * side + 1) * quarter : (2 * side + 2) * quarter])
+        new = jnp.where(core == 0, low, high) - (mine[...] + theirs[...])
+        update[side * quarter : (side + 1) * quarter, :] = new
+        sums = sums + jnp.sum(new * new, axis=0, keepdims=True)
     sums = sums + pltpu.roll(sums, LANES // 2, 1)
     squares[...] = jnp.broadcast_to(sums[None], squares.shape)
 
 
 def scale_kernel(rows, update, squares, out):
-    half = update.shape[0]
+    quarter = update.shape[0] // 2
     factor = lax.rsqrt(jnp.sum(squares[...], axis=0) / rows + 1e-06)
     new = (update[...] * factor).T
-    out[:, :half] = new[: LANES // 2]
-    out[:, half:] = new[LANES // 2 :]
+    for side in range(2):
+        for h in range(2):
+            start = (2 * side + h) * quarter
+            out[:, start : start + quarter] = new[
+                h * (LANES // 2) : (h + 1) * (LANES // 2), side * quarter : (side + 1) * quarter
+            ]
 
 
 def call(body, name, specs, shapes, scratch=(), limit=16, flops=0):
@@ -292,29 +330,33 @@
                 ring.append((t * nodes + n, d * nodes + n))
     swap_core = [(i, i ^ 1) for i in range(nodes)]
     swap_chip = [(i, i ^ 2) for i in range(nodes)]
-    near = lax.ppermute(edge, ("sub", "node"), ring)
+    halo = lax.ppermute(edge, ("sub", "node"), ring)
+
     half = functools.partial(jax.ShapeDtypeStruct, dtype=BF16)
     blocks, sep = rows // BLK, panels.shape[1]
+    per_core = blocks // 2
     prepared = call(
         prepare_kernel,
         "prepare",
         [SMEM] + [HBM] * 6,
         [half((blocks, BLK, width))] * 2
-        + [(rows, width)]
-        + [half((blocks, BLK, 4 * BLK))] * 2
-        + [half((4 * sep, rows))] * 2
+        + [(per_core, BLK, width)]
+        + [half((per_core, BLK, 4 * BLK))] * 2
+        + [half((2, 4 * sep, rows // 2))] * 2
         + [half((rows, 4 * sep))] * 2
         + [half((blocks, BLK, BLK))] * 2
         + [(8, LANES)],
         [
             pltpu.VMEM((rows, width), F32),
             pltpu.VMEM((1, width), F32),
-            pltpu.VMEM(matrix_blocks.shape, F32),
+            pltpu.VMEM((per_core, 4, BLK, BLK), F32),
             pltpu.VMEM((blocks, LOCAL, 2, BLK, BLK), F32),
             pltpu.VMEM((sep, rows), F32),
             pltpu.SemaphoreType.DMA,
             pltpu.SemaphoreType.DMA,
-            pltpu.SemaphoreType.DMA((blocks, 4)),
+            pltpu.SemaphoreType.DMA,
+            pltpu.SemaphoreType.DMA,
+            pltpu.SemaphoreType.DMA((blocks, 2)),
             pltpu.SMEM(separator_map.shape, jnp.int32),
         ],
         limit=24,
@@ -329,19 +371,31 @@
         )
     )
     own_hi, own_lo, scaled, m_hi, m_lo, e_hi, e_lo, f_hi, f_lo, w_hi, w_lo, ids = prepared
-    near, ids = lax.optimization_barrier((near, ids))
-    far = lax.ppermute(near, "node", swap_core)
+    halo, ids = lax.optimization_barrier((halo, ids))
+    residual, mine_hi, mine_lo = call(
+        residual_kernel,
+        "residual",
+        [SMEM, SMEM] + [VMEM] * 6,
+        [(rows // 2, width)] + [half((rows // 2, width))] * 2,
+        [pltpu.VMEM((blocks + HALO, BLK, width), BF16)] * 2,
+        flops=10**9,
+    )(place, block_lists.T, halo, own_hi, own_lo, scaled, m_hi, m_lo)
+    theirs = lax.ppermute(residual, "node", swap_core)
+    (sums,) = call(
+        mine_kernel,
+        "mine",
+        [SMEM] + [VMEM] * 4,
+        [(4 * sep, width)],
+        flops=4 * 10**9,
+    )(place, e_hi, e_lo, mine_hi, mine_lo)
+    theirs, sums = lax.optimization_barrier((theirs, sums))
     r_hi, r_lo, pieces = call(
-        forward_kernel,
-        "forward",
-        [SMEM, SMEM] + [VMEM] * 10,
-        [half((rows, width)), half((rows, width)), (subs, 136, LANES)],
-        [pltpu.VMEM((16, BLK, width), BF16)] * 2,
-        limit=16,
+        theirs_kernel,
+        "theirs",
+        [SMEM] + [VMEM] * 7,
+        [half((2, rows // 2, width))] * 2 + [(subs, 136, LANES)],
         flops=4 * 10**9,
-    )(
-        place, block_lists.T, near, far, own_hi, own_lo, scaled, m_hi, m_lo, e_hi, e_lo, ids
-    )
+    )(place, sums, theirs, e_hi, e_lo, mine_hi, mine_lo, ids)
     received = lax.all_to_all(pieces, "sub", 0, 0, tiled=True)
     maps = received[:, 128, :4].astype(jnp.int32)
     (back,) = call(
@@ -352,26 +406,35 @@
         [pltpu.VMEM((GROUPS, 2, 16, LANES), F32)],
     )(place, maps, separator_shift.reshape(GROUPS, LANES), received)
     picked = lax.all_to_all(back, "sub", 0, 0, tiled=True)
-    keep, send = call(
-        backward_kernel,
-        "backward",
+    operators = (f_hi, f_lo, r_hi, r_lo, w_hi, w_lo)
+    keep_a, send_a, x_hi, x_lo = call(
+        first_kernel,
+        "first",
         [SMEM] + [VMEM] * 7,
-        [(rows, LANES), (rows, LANES)],
-        [pltpu.VMEM((4 * sep, width), BF16)] * 2,
-        limit=16,
-        flops=4 * 10**9,
-    )(place, picked, f_hi, f_lo, r_hi, r_lo, w_hi, w_lo)
-    theirs = lax.ppermute(send, "node", swap_core)
-    keep, send = call(
-        pair_kernel, "pair", [SMEM, VMEM, VMEM], [(rows // 2, LANES), (rows // 2, LANES)]
-    )(place, keep, theirs)
-    theirs = lax.ppermute(send, "node", swap_chip)
+        [(rows // 2, LANES)] * 2 + [half((4 * sep, width))] * 2,
+        flops=2 * 10**9,
+    )(place, picked, *operators)
+    theirs_a = lax.ppermute(send_a, "node", swap_core)
+    keep_b, send_b = call(
+        second_kernel,
+        "second",
+        [SMEM] + [VMEM] * 8,
+        [(rows // 2, LANES)] * 2,
+        flops=2 * 10**9,
+    )(place, x_hi, x_lo, *operators)
+    theirs_a, send_b = lax.optimization_barrier((theirs_a, send_b))
+    theirs_b = lax.ppermute(send_b, "node", swap_core)
+    pair = call(pair_kernel, "pair", [SMEM, VMEM, VMEM], [(rows // 4, LANES)] * 2)
+    keep_a, send_a = pair(place, keep_a, theirs_a)
+    theirs_a = lax.ppermute(send_a, "node", swap_chip)
+    keep_b, send_b = pair(place, keep_b, theirs_b)
+    theirs_b = lax.ppermute(send_b, "node", swap_chip)
     update, squares = call(
         update_kernel,
         "update",
-        [SMEM, VMEM, VMEM, VMEM],
+        [SMEM] + [VMEM] * 5,
         [(rows // 2, LANES), (subs, 1, LANES)],
-    )(place, keep, theirs, search_vectors)
+    )(place, keep_a, theirs_a, keep_b, theirs_b, search_vectors)
     gathered = lax.all_to_all(squares, "sub", 0, 0, tiled=True)
     (out,) = call(
         functools.partial(scale_kernel, rows * subs),

time: 135 us -> 135 us (level)
  waiting for transfers between devices: 11.7 us -> 7.17 us
  starting transfers between devices: 6.06 us -> 8.13 us
    ppermute x4 -> x6, waiting for transfers between devices: 11.7 us -> 7.17 us  [the longest x1 3.57 us: shards(): theirs_a = lax.ppermute(send_a, 'node', swap_chip)]
    pallas_call x4 -> x8, Pallas kernels: 11.4 us -> 13.6 us  [the longest x1 2.65 us: shards(): call(first_kernel, 'first', [SMEM] + [VMEM] * 7, [(rows // 2, LANES)] * 2...]
    ppermute x4 -> x6, starting transfers between devices: 6.06 us -> 8.13 us  [the longest x1 5.21 us: shards(): halo = lax.ppermute(edge, ('sub', 'node'), ring)]
    pallas_call x1, Pallas kernels: 11.7 us -> 10.2 us  [shards(): call(prepare_kernel, 'prepare', [SMEM] + [HBM] * 6, [half((blocks, BLK, w...]
  transfers between devices with their start and end apart: 4 -> 6, of which waited for: 4 -> 3; matrix products, arithmetic and copies ran while one was open for 0% -> 0% of each run, Pallas kernels for 9% -> 12%
where the time goes in v4:
time: 135 us; the launch traced here: 134 us
  blocking collectives  91.3 us (68%)
  Pallas kernels  26.5 us (20%)
  starting transfers between devices  8.13 us (6%)
  waiting for transfers between devices  7.17 us (5%)
    all_to_all x1, blocking collectives, shards(): received = lax.all_to_all(pieces, 'sub', 0, 0, tiled=True)  44 us
    all_to_all x1, blocking collectives, shards(): picked = lax.all_to_all(back, 'sub', 0, 0, tiled=True)  34 us
    all_to_all x1, blocking collectives, shards(): gathered = lax.all_to_all(squares, 'sub', 0, 0, tiled=True)  13.3 us
    pallas_call x1, Pallas kernels, shards(): call(prepare_kernel, 'prepare', [SMEM] + [HBM] * 6, [half((blocks, BLK, w...  10.2 us
    ppermute x1, starting transfers between devices, shards(): halo = lax.ppermute(edge, ('sub', 'node'), ring)  5.21 us
    ppermute x1, waiting for transfers between devices, shards(): theirs_a = lax.ppermute(send_a, 'node', swap_chip)  3.57 us
  transfers between devices with their start and end apart: 6, of which 3 were waited for; matrix products, arithmetic and copies ran while one was open for 0% of the time, Pallas kernels for 12%

profile of v4, /device:TPU:0, one launch (start us, length us, event | category | flops | bytes accessed | tf_op | source)
XLA Modules:
  0.0 134.4 jit_solution(7879277891325004997)
XLA Ops:
  0.0 1.1 constant_dynamic-slice_fusion
  1.1 5.2 %collective-permute-start = (f32[512,256]{1,0:T(8,128)S(1)}, f32[512,256]{1,0:T(8,128)S(1)}, u32[]{:S(2)}, u32[]{:S(2)}) collective-permute-start(f32[512,256]{1,0:T(8,128)S(1)} %constant_dynamic-slice_fusion), channel_id=1, source_target_pairs={{0,4},{2,6},{4,8},{5,1},{6,10},{7,3},{8,12},{9,5},{10,14},{11,7},{... | collective-permute-start | bytes 1572872 | tf_op jit(solution)/shard_map/ppermute | solution.py:333
  6.3 0.1 pad_add_fusion.place
  6.4 10.2 %prepare.1 = (bf16[8,128,256]{2,1,0:T(8,128)(2,1)S(1)}, bf16[8,128,256]{2,1,0:T(8,128)(2,1)S(1)}, f32[4,128,256]{2,1,0:T(8,128)S(1)}, bf16[4,128,512]{2,1,0:T(8,...) custom-call(s32[2]{0:T(128)S(1)} %pad_add_fusion.place, ...), custom_call_target="tpu_custom_call" | custom-call | flops 8000000000 | bytes 8388608 | tf_op jit(solution)/shard_map/prepare/pallas_call | solution.py:338
  16.6 1.7 %collective-permute-done.halo = f32[512,256]{1,0:T(8,128)S(1)} collective-permute-done((f32[512,256]{1,0:T(8,128)S(1)}, f32[512,256]{1,0:T(8,128)S(1)}, u32[]{:S(2)}, u32[]{:S(2)}) %collective-permute-start) | collective-permute-done | bytes 524320 | tf_op jit(solution)/shard_map/ppermute | solution.py:333
  18.3 0.0 copy-done.2
  18.3 1.3 residual.1
  19.7 0.1 collective-permute-start.1
  19.8 2.4 %mine.1.sums = f32[2048,256]{1,0:T(8,128)S(1)} custom-call(s32[2]{0:T(128)S(1)} %pad_add_fusion.place, bf16[2,2048,512]{2,1,0:T(8,128)(2,1)S(1)} %get-tuple-element.49.e_hi, bf16[2,2048,512]{2,1,0:T(8,128)(2,1)S(1)} %get-tuple-element.50.e_lo, bf16[512,256]{1,0:T(8,128)(2,1)S(1)} %get-tuple-element.51.r_hi.m_hi, bf16[512,256]{1,0:T(8,128)(2,1)S(1)} %get-tuple-element.52.r_lo.m_lo), custom_call_target="tpu_custom_call" | custom-call | flops 4000000000 | bytes 8388608 | tf_op jit(solution)/shard_map/mine/pallas_call | solution.py:384
  22.2 0.0 collective-permute-done.1.theirs
  22.2 2.4 %theirs.1 = (bf16[2,512,256]{2,1,0:T(8,128)(2,1)S(1)}, bf16[2,512,256]{2,1,0:T(8,128)(2,1)S(1)}, f32[32,136,128]{2,1,0:T(8,128)S(1)}) custom-call(s32[2]{0:T(128)S(1)} %pad_add_fusion.place, f32[2048,256]{1,0:T(8,128)S(1)} %mine.1.sums, f32[512,256]{1,0:T(8,128)S(1)} %collective-permute-done.1.theirs, bf16[2,2048,512]{2,1,0:T(8,128)(2,1)S(1)} %get-tuple-element.49.e_hi, ...), custom_call_target="tpu_custom_call" | custom-call | flops 4000000000 | bytes 8388608 | tf_op jit(solution)/shard_map/theirs/pallas_call | solution.py:392
  24.6 0.0 copy-start.1
  24.6 44.0 %all_to_all.15.received = f32[32,136,128]{2,1,0:T(8,128)S(1)} all-to-all(f32[32,136,128]{2,1,0:T(8,128)S(1)} %get-tuple-element.56), channel_id=1, replica_groups=mesh['sub'=32,'node'=4] {'sub'}, dimensions={0} | all-to-all | bytes 4456448 | tf_op jit(solution)/shard_map/all_to_all | solution.py:399
  68.6 0.0 copy-done.1
  68.6 1.8 %owner.1 = f32[32,128,128]{2,1,0:T(8,128)S(1)} custom-call(s32[2]{0:T(128)S(1)} %pad_add_fusion.place, s32[32,4]{1,0:T(8,128)S(1)} %bitcast.7, f32[8,128]{1,0:T(8,128)S(1)} %bitcast.8, f32[32,136,128]{2,1,0:T(8,128)S(1)} %all_to_all.15.received), custom_call_target="tpu_custom_call" | custom-call | bytes 8388608 | tf_op jit(solution)/shard_map/owner/pallas_call | solution.py:401
  70.4 34.0 %all_to_all.16.picked = f32[32,128,128]{2,1,0:T(8,128)S(1)} all-to-all(f32[32,128,128]{2,1,0:T(8,128)S(1)} %owner.1), channel_id=1, replica_groups=mesh['sub'=32,'node'=4] {'sub'}, dimensions={0} | all-to-all | bytes 4194304 | tf_op jit(solution)/shard_map/all_to_all | solution.py:408
  104.4 2.7 %first.1 = (f32[512,128]{1,0:T(8,128)S(1)}, f32[512,128]{1,0:T(8,128)S(1)}, bf16[2048,256]{1,0:T(8,128)(2,1)S(1)}, bf16[2048,256]{1,0:T(8,128)(2,1)S(1)}) custom-call(s32[2]{0:T(128)S(1)} %pad_add_fusion.place, f32[32,128,128]{2,1,0:T(8,128)S(1)} %all_to_all.16.picked, bf16[1024,2048]{1,0:T(8,128)(2,1)S(1)} %get-tuple-element.57.f_hi, ...), custom_call_target="tpu_custom_call" | custom-call | flops 2000000000 | bytes 8388608 | tf_op jit(solution)/shard_map/first/pallas_call | solution.py:410
  107.1 0.1 collective-permute-start.2
  107.2 0.0 copy-start
  107.2 2.6 %second.1 = (f32[512,128]{1,0:T(8,128)S(1)}, f32[512,128]{1,0:T(8,128)S(1)}) custom-call(s32[2]{0:T(128)S(1)} %pad_add_fusion.place, bf16[2048,256]{1,0:T(8,128)(2,1)S(1)} %get-tuple-element.65.x_hi, bf16[2048,256]{1,0:T(8,128)(2,1)S(1)} %get-tuple-element.66.x_lo, bf16[1024,2048]{1,0:T(8,128)(2,1)S(1)} %get-tuple-element.57.f_hi, ...), custom_call_target="tpu_custom_call" | custom-call | flops 2000000000 | bytes 8388608 | tf_op jit(solution)/shard_map/second/pallas_call | solution.py:418
  109.8 0.0 collective-permute-done.2.theirs
  109.8 0.6 collective-permute-start.4
  110.4 0.7 pair.2
  111.1 1.2 collective-permute-start.3
  112.3 0.0 collective-permute-done.4.theirs
  112.3 0.7 pair.3
  112.9 1.0 collective-permute-start.5
  113.9 3.6 %collective-permute-done.3.theirs_a = f32[256,128]{1,0:T(8,128)S(1)} collective-permute-done((f32[256,128]{1,0:T(8,128)S(1)}, f32[256,128]{1,0:T(8,128)S(1)}, u32[]{:S(2)}, u32[]{:S(2)}) %collective-permute-start.3) | collective-permute-done | bytes 131104 | tf_op jit(solution)/shard_map/ppermute | solution.py:429
  117.5 1.9 %collective-permute-done.5.theirs_b = f32[256,128]{1,0:T(8,128)S(1)} collective-permute-done((f32[256,128]{1,0:T(8,128)S(1)}, f32[256,128]{1,0:T(8,128)S(1)}, u32[]{:S(2)}, u32[]{:S(2)}) %collective-permute-start.5) | collective-permute-done | bytes 131104 | tf_op jit(solution)/shard_map/ppermute | solution.py:431
  119.4 0.8 update.1
  120.2 13.3 %all_to_all.17.squares = f32[32,1,128]{2,1,0:T(1,128)S(1)} all-to-all(f32[32,1,128]{2,1,0:T(1,128)S(1)} %get-tuple-element.76), channel_id=1, replica_groups=mesh['sub'=32,'node'=4] {'sub'}, dimensions={0} | all-to-all | bytes 32768 | tf_op jit(solution)/shard_map/all_to_all | solution.py:438
  133.6 0.9 scale.1
  (3 shorter events, 0.0 us)
Async XLA Ops:
  1.1 17.3 %collective-permute-start = (f32[512,256]{1,0:T(8,128)S(1)}, f32[512,256]{1,0:T(8,128)S(1)}, u32[]{:S(2)}, u32[]{:S(2)}) collective-permute-start(f32[512,256]{1,0:T(8,128)S(1)} %constant_dynamic-slice_fusion), channel_id=1, source_target_pairs={{0,4},{2,6},{4,8},{5,1},{6,10},{7,3},{8,12},{9,5},{10,14},{11,7},{... | collective-permute-start | bytes 1572872 | tf_op jit(solution)/shard_map/ppermute | solution.py:333
  6.4 12.0 %copy-start.2 = (s32[8,4]{0,1:T(4,128)S(1)}, s32[8,4]{0,1:T(4,128)}, u32[]{:S(2)}) copy-start(s32[8,4]{0,1:T(4,128)} %param.11) | copy-start | bytes 388
  19.7 2.5 %collective-permute-start.1 = (f32[512,256]{1,0:T(8,128)S(1)}, f32[512,256]{1,0:T(8,128)S(1)}, u32[]{:S(2)}, u32[]{:S(2)}) collective-permute-start(f32[512,256]{1,0:T(8,128)S(1)} %get-tuple-element.48), channel_id=1, source_target_pairs={{0,1},{1,0},{2,3},{3,2},{4,5},{5,4},{6,7},{7,6},{8,9},{9,8},{10,11... | collective-permute-start | bytes 1572872 | tf_op jit(solution)/shard_map/ppermute | solution.py:383
  24.6 44.0 %copy-start.1 = (f32[1024]{0:T(1024)S(1)}, f32[1024]{0:T(1024)}, u32[]{:S(2)}) copy-start(f32[1024]{0:T(1024)} %param.15) | copy-start | bytes 12292
  107.1 2.7 %collective-permute-start.2 = (f32[512,128]{1,0:T(8,128)S(1)}, f32[512,128]{1,0:T(8,128)S(1)}, u32[]{:S(2)}, u32[]{:S(2)}) collective-permute-start(f32[512,128]{1,0:T(8,128)S(1)} %get-tuple-element.64), channel_id=1, source_target_pairs={{0,1},{1,0},{2,3},{3,2},{4,5},{5,4},{6,7},{7,6},{8,9},{9,8},{10,11... | collective-permute-start | bytes 786440 | tf_op jit(solution)/shard_map/ppermute | solution.py:417
  107.2 12.2 %copy-start = (f32[1024,256]{1,0:T(8,128)S(1)}, f32[1024,256]{1,0:T(8,128)}, u32[]{:S(2)}) copy-start(f32[1024,256]{1,0:T(8,128)} %vectors.1) | copy-start | bytes 3145732
  109.8 2.4 %collective-permute-start.4 = (f32[512,128]{1,0:T(8,128)S(1)}, f32[512,128]{1,0:T(8,128)S(1)}, u32[]{:S(2)}, u32[]{:S(2)}) collective-permute-start(f32[512,128]{1,0:T(8,128)S(1)} %get-tuple-element.72), channel_id=1, source_target_pairs={{0,1},{1,0},{2,3},{3,2},{4,5},{5,4},{6,7},{7,6},{8,9},{9,8},{10,11... | collective-permute-start | bytes 786440 | tf_op jit(solution)/shard_map/ppermute | solution.py:426
  111.1 6.4 %collective-permute-start.3 = (f32[256,128]{1,0:T(8,128)S(1)}, f32[256,128]{1,0:T(8,128)S(1)}, u32[]{:S(2)}, u32[]{:S(2)}) collective-permute-start(f32[256,128]{1,0:T(8,128)S(1)} %get-tuple-element.70), channel_id=1, source_target_pairs={{0,2},{1,3},{2,0},{3,1},{4,6},{5,7},{6,4},{7,5},{8,10},{9,11},{10,... | collective-permute-start | bytes 393224 | tf_op jit(solution)/shard_map/ppermute | solution.py:429
  112.9 6.4 %collective-permute-start.5 = (f32[256,128]{1,0:T(8,128)S(1)}, f32[256,128]{1,0:T(8,128)S(1)}, u32[]{:S(2)}, u32[]{:S(2)}) collective-permute-start(f32[256,128]{1,0:T(8,128)S(1)} %get-tuple-element.74), channel_id=1, source_target_pairs={{0,2},{1,3},{2,0},{3,1},{4,6},{5,7},{6,4},{7,5},{8,10},{9,11},{10,... | collective-permute-start | bytes 393224 | tf_op jit(solution)/shard_map/ppermute | solution.py:431

commit v5 on v4

--- a/solution.py
+++ b/solution.py
@@ -56,7 +56,7 @@
 
 def prepare_kernel(
     place, sep_map, own_hbm, ritz_hbm, mats_hbm, inverses_hbm, panel_hbm,
-    own_hi, own_lo, scaled, m_hi, m_lo, e_hi, e_lo, f_hi, f_lo, w_hi, w_lo, ids,
+    own_hi, own_lo, scaled, m_hi, m_lo, e_hi, e_lo, f_hi, f_lo, w_hi, w_lo, ids, columns,
     own, ritz, mats, inverses, panel, ids_sem, ritz_sem, mats_sem, panel_sem, sems, map_copy,
 ):
     node, core = place[1] * LOCAL, place[1] % 2
@@ -106,8 +106,8 @@
             jnp.concatenate([p_hi, p_hi, p_lo], 1),
             ((1,), (1,)),
         )
-        side, first = divmod(g, per_core)
-        cols = slice(first * BLK, (first + 1) * BLK)
+        side, nth = divmod(g, per_core)
+        cols = slice(nth * BLK, (nth + 1) * BLK)
         for k in range(2 * LOCAL):
             span, block = slice(k * sep, (k + 1) * sep), slice(k * BLK, (k + 1) * BLK)
             e_hi[side, span, cols], e_lo[side, span, cols] = split(e[:, block])
@@ -115,6 +115,14 @@
     for copy in small:
         copy.wait()
     my_mats.wait()
+    first, mid, quarter = place[1] // 2 == 0, own.shape[1] // 2, own.shape[0] // 4
+    for side in range(2):
+        top, bottom = (
+            jnp.where(first, own[rows, :mid], own[rows, mid:])
+            for rows in (slice(k * quarter, (k + 1) * quarter) for k in (2 * side, 2 * side + 1))
+        )
+        low, high = halves(top, bottom)
+        columns[side] = jnp.where(core == 0, low, high)
     for g in range(per_core):
         rows = pl.ds(pl.multiple_of((core * per_core + g) * BLK, BLK), BLK)
         scaled[g] = own[rows, :] * ritz[...]
@@ -227,18 +235,23 @@
 
 def solve(side, core, coarse, f_hi, f_lo, r_hi, r_lo, w_hi, w_lo, keep, send):
     per_side = w_hi.shape[0] // 2
+    quarters = []
     for g in range(0, per_side, 2):
         first = side * per_side + g
         both = slice(first * BLK, (first + 2) * BLK)
         back = dot3((f_hi[both, :], f_lo[both, :]), coarse)
+        local = []
         for i in range(2):
             rows = slice((g + i) * BLK, (g + i + 1) * BLK)
-            weighted = back[i * BLK : (i + 1) * BLK] + dot3(
-                (w_hi[first + i], w_lo[first + i]), (r_hi[side, rows, :], r_lo[side, rows, :])
+            local.append(
+                dot3((w_hi[first + i], w_lo[first + i]), (r_hi[side, rows, :], r_lo[side, rows, :]))
             )
-            low, high = halves(weighted[:, :LANES], weighted[:, LANES:])
-            keep[rows, :] = jnp.where(core == 0, low, high)
-            send[rows, :] = jnp.where(core == 0, high, low)
+        quarters.append(back + jnp.concatenate(local, 0))
+    for chip in range(2):
+        cols = slice(chip * LANES, (chip + 1) * LANES)
+        low, high = halves(quarters[0][:, cols], quarters[1][:, cols])
+        keep[chip] = jnp.where(core == 0, low, high)
+        send[chip] = jnp.where(core == 0, high, low)
 
 
 def first_kernel(place, picked, f_hi, f_lo, r_hi, r_lo, w_hi, w_lo, keep, send, x_hi, x_lo):
@@ -252,41 +265,14 @@
     solve(1, place[1] % 2, coarse, f_hi, f_lo, r_hi, r_lo, w_hi, w_lo, keep, send)
 
 
-def pair_kernel(place, mine, theirs, keep, send):
-    first = place[1] // 2 == 0
-    half = mine.shape[0] // 2
-    total = mine[...] + theirs[...]
-    low, high = halves(total[:half], total[half:])
-    keep[...] = jnp.where(first, low, high)
-    send[...] = jnp.where(first, high, low)
-
-
-def update_kernel(place, mine_a, theirs_a, mine_b, theirs_b, vectors, update, squares):
-    first, core = place[1] // 2 == 0, place[1] % 2
-    quarter = mine_a.shape[0]
-    mid = vectors.shape[1] // 2
-    own = jnp.where(first, vectors[:, :mid], vectors[:, mid:])
-    sums = jnp.zeros((1, LANES), F32)
-    for side, (mine, theirs) in enumerate(((mine_a, theirs_a), (mine_b, theirs_b))):
-        top = own[2 * side * quarter : (2 * side + 1) * quarter]
-        low, high = halves(top, own[(2 * side + 1) * quarter : (2 * side + 2) * quarter])
-        new = jnp.where(core == 0, low, high) - (mine[...] + theirs[...])
-        update[side * quarter : (side + 1) * quarter, :] = new
-        sums = sums + jnp.sum(new * new, axis=0, keepdims=True)
-    sums = sums + pltpu.roll(sums, LANES // 2, 1)
-    squares[...] = jnp.broadcast_to(sums[None], squares.shape)
-
-
-def scale_kernel(rows, update, squares, out):
-    quarter = update.shape[0] // 2
+def scale_kernel(rows, update_a, update_b, squares, out):
+    quarter = update_a.shape[0]
     factor = lax.rsqrt(jnp.sum(squares[...], axis=0) / rows + 1e-06)
-    new = (update[...] * factor).T
-    for side in range(2):
+    for side, update in enumerate((update_a, update_b)):
+        new = (update[...] * factor).T
         for h in range(2):
             start = (2 * side + h) * quarter
-            out[:, start : start + quarter] = new[
-                h * (LANES // 2) : (h + 1) * (LANES // 2), side * quarter : (side + 1) * quarter
-            ]
+            out[:, start : start + quarter] = new[h * (LANES // 2) : (h + 1) * (LANES // 2)]
 
 
 def call(body, name, specs, shapes, scratch=(), limit=16, flops=0):
@@ -345,7 +331,7 @@
         + [half((2, 4 * sep, rows // 2))] * 2
         + [half((rows, 4 * sep))] * 2
         + [half((blocks, BLK, BLK))] * 2
-        + [(8, LANES)],
+        + [(8, LANES), (2, rows // 4, LANES)],
         [
             pltpu.VMEM((rows, width), F32),
             pltpu.VMEM((1, width), F32),
@@ -370,7 +356,7 @@
             )
         )
     )
-    own_hi, own_lo, scaled, m_hi, m_lo, e_hi, e_lo, f_hi, f_lo, w_hi, w_lo, ids = prepared
+    own_hi, own_lo, scaled, m_hi, m_lo, e_hi, e_lo, f_hi, f_lo, w_hi, w_lo, ids, columns = prepared
     halo, ids = lax.optimization_barrier((halo, ids))
     residual, mine_hi, mine_lo = call(
         residual_kernel,
@@ -411,7 +397,7 @@
         first_kernel,
         "first",
         [SMEM] + [VMEM] * 7,
-        [(rows // 2, LANES)] * 2 + [half((4 * sep, width))] * 2,
+        [(2, rows // 4, LANES)] * 2 + [half((4 * sep, width))] * 2,
         flops=2 * 10**9,
     )(place, picked, *operators)
     theirs_a = lax.ppermute(send_a, "node", swap_core)
@@ -419,29 +405,32 @@
         second_kernel,
         "second",
         [SMEM] + [VMEM] * 8,
-        [(rows // 2, LANES)] * 2,
+        [(2, rows // 4, LANES)] * 2,
         flops=2 * 10**9,
     )(place, x_hi, x_lo, *operators)
     theirs_a, send_b = lax.optimization_barrier((theirs_a, send_b))
     theirs_b = lax.ppermute(send_b, "node", swap_core)
-    pair = call(pair_kernel, "pair", [SMEM, VMEM, VMEM], [(rows // 4, LANES)] * 2)
-    keep_a, send_a = pair(place, keep_a, theirs_a)
-    theirs_a = lax.ppermute(send_a, "node", swap_chip)
-    keep_b, send_b = pair(place, keep_b, theirs_b)
-    theirs_b = lax.ppermute(send_b, "node", swap_chip)
-    update, squares = call(
-        update_kernel,
-        "update",
-        [SMEM] + [VMEM] * 5,
-        [(rows // 2, LANES), (subs, 1, LANES)],
-    )(place, keep_a, theirs_a, keep_b, theirs_b, search_vectors)
+    chip = node // 2
+
+    def both(index, keep, theirs):
+        return lax.dynamic_index_in_dim(keep, index, 0, False) + lax.dynamic_index_in_dim(
+            theirs, index, 0, False
+        )
+
+    far_a = lax.ppermute(both(1 - chip, keep_a, theirs_a), "node", swap_chip)
+    far_b = lax.ppermute(both(1 - chip, keep_b, theirs_b), "node", swap_chip)
+    update_a = columns[0] - (both(chip, keep_a, theirs_a) + far_a)
+    update_b = columns[1] - (both(chip, keep_b, theirs_b) + far_b)
+    sums = jnp.sum(update_a * update_a, axis=0) + jnp.sum(update_b * update_b, axis=0)
+    sums = sums + jnp.roll(sums, LANES // 2)
+    squares = jnp.broadcast_to(sums[None, None], (subs, 1, LANES))
     gathered = lax.all_to_all(squares, "sub", 0, 0, tiled=True)
     (out,) = call(
         functools.partial(scale_kernel, rows * subs),
         "scale",
-        [VMEM, VMEM],
+        [VMEM, VMEM, VMEM],
         [(width // nodes, rows)],
-    )(update, gathered)
+    )(update_a, update_b, gathered)
     return out.T
 
 

time: 135 us -> 133 us (0.985)
  Pallas kernels: 26.5 us -> 24.6 us
    pallas_call x6 -> x3, Pallas kernels: 8.35 us -> 6.18 us  [the longest x1 2.66 us: shards(): call(first_kernel, 'first', [SMEM] + [VMEM] * 7, [(2, rows // 4, LANES)]...]
where the time goes in v5:
time: 133 us
  blocking collectives  91.3 us (69%)
  Pallas kernels  24.6 us (18%)
  starting transfers between devices  8.29 us (6%)
  waiting for transfers between devices  7.46 us (6%)
    all_to_all x1, blocking collectives, shards(): received = lax.all_to_all(pieces, 'sub', 0, 0, tiled=True)  44 us
    all_to_all x1, blocking collectives, shards(): picked = lax.all_to_all(back, 'sub', 0, 0, tiled=True)  34 us
    all_to_all x1, blocking collectives, shards(): gathered = lax.all_to_all(squares, 'sub', 0, 0, tiled=True)  13.3 us
    pallas_call x1, Pallas kernels, shards(): call(prepare_kernel, 'prepare', [SMEM] + [HBM] * 6, [half((blocks, BLK, w...  10.5 us
    ppermute x1, starting transfers between devices, shards(): halo = lax.ppermute(edge, ('sub', 'node'), ring)  5.21 us
    ppermute x1, waiting for transfers between devices, shards(): far_a = lax.ppermute(both(1 - chip, keep_a, theirs_a), 'node', swap_chip)  4.09 us
  transfers between devices with their start and end apart: 6, of which 3 were waited for; matrix products, arithmetic and copies ran while one was open for 0% of the time, Pallas kernels for 12%

profile of v5, /device:TPU:0, one launch (start us, length us, event | category | flops | bytes accessed | tf_op | source)
XLA Modules:
  0.0 133.2 jit_solution(6954033675338812827)
XLA Ops:
  0.0 1.1 constant_dynamic-slice_fusion
  1.1 5.2 %collective-permute-start = (f32[512,256]{1,0:T(8,128)S(1)}, f32[512,256]{1,0:T(8,128)S(1)}, u32[]{:S(2)}, u32[]{:S(2)}) collective-permute-start(f32[512,256]{1,0:T(8,128)S(1)} %constant_dynamic-slice_fusion), channel_id=1, source_target_pairs={{0,4},{2,6},{4,8},{5,1},{6,10},{7,3},{8,12},{9,5},{10,14},{11,7},{... | collective-permute-start | bytes 1572872 | tf_op jit(solution)/shard_map/ppermute | solution.py:319
  6.3 0.1 pad_add_fusion.place
  6.4 0.0 copy-start.1
  6.4 10.5 %prepare.1 = (bf16[8,128,256]{2,1,0:T(8,128)(2,1)S(1)}, bf16[8,128,256]{2,1,0:T(8,128)(2,1)S(1)}, f32[4,128,256]{2,1,0:T(8,128)S(1)}, bf16[4,128,512]{2,1,0:T(8,...) custom-call(s32[2]{0:T(128)S(1)} %pad_add_fusion.place, ...), custom_call_target="tpu_custom_call" | custom-call | flops 8000000000 | bytes 8388608 | tf_op jit(solution)/shard_map/prepare/pallas_call | solution.py:324
  16.9 1.5 %collective-permute-done.halo = f32[512,256]{1,0:T(8,128)S(1)} collective-permute-done((f32[512,256]{1,0:T(8,128)S(1)}, f32[512,256]{1,0:T(8,128)S(1)}, u32[]{:S(2)}, u32[]{:S(2)}) %collective-permute-start) | collective-permute-done | bytes 524320 | tf_op jit(solution)/shard_map/ppermute | solution.py:319
  18.3 0.0 copy-done.1
  18.3 1.3 %residual.1 = (f32[512,256]{1,0:T(8,128)S(1)}, bf16[512,256]{1,0:T(8,128)(2,1)S(1)}, bf16[512,256]{1,0:T(8,128)(2,1)S(1)}) custom-call(s32[2]{0:T(128)S(1)} %pad_add_fusion.place, s32[4,8]{1,0:T(4,128)S(1)} %bitcast.29, f32[512,256]{1,0:T(8,128)S(1)} %collective-permute-done.halo, bf16[8,128,256]{2,1,0:T(8,128)(2,1)S(1)} %get-tuple-element.39.own_hi, ...), custom_call_target="tpu_custom_call" | custom-call | flops 1000000000 | bytes 8388608 | tf_op jit(solution)/shard_map/residual/pallas_call | solution.py:361
  19.7 0.1 collective-permute-start.1
  19.8 2.4 %mine.1.sums = f32[2048,256]{1,0:T(8,128)S(1)} custom-call(s32[2]{0:T(128)S(1)} %pad_add_fusion.place, bf16[2,2048,512]{2,1,0:T(8,128)(2,1)S(1)} %get-tuple-element.45.e_hi, bf16[2,2048,512]{2,1,0:T(8,128)(2,1)S(1)} %get-tuple-element.46.e_lo, bf16[512,256]{1,0:T(8,128)(2,1)S(1)} %get-tuple-element.47.r_hi.m_hi, bf16[512,256]{1,0:T(8,128)(2,1)S(1)} %get-tuple-element.48.r_lo.m_lo), custom_call_target="tpu_custom_call" | custom-call | flops 4000000000 | bytes 8388608 | tf_op jit(solution)/shard_map/mine/pallas_call | solution.py:370
  22.2 0.0 collective-permute-done.1.theirs
  22.2 2.4 %theirs.1 = (bf16[2,512,256]{2,1,0:T(8,128)(2,1)S(1)}, bf16[2,512,256]{2,1,0:T(8,128)(2,1)S(1)}, f32[32,136,128]{2,1,0:T(8,128)S(1)}) custom-call(s32[2]{0:T(128)S(1)} %pad_add_fusion.place, f32[2048,256]{1,0:T(8,128)S(1)} %mine.1.sums, f32[512,256]{1,0:T(8,128)S(1)} %collective-permute-done.1.theirs, bf16[2,2048,512]{2,1,0:T(8,128)(2,1)S(1)} %get-tuple-element.45.e_hi, ...), custom_call_target="tpu_custom_call" | custom-call | flops 4000000000 | bytes 8388608 | tf_op jit(solution)/shard_map/theirs/pallas_call | solution.py:378
  24.6 0.0 copy-start
  24.6 44.0 %all_to_all.15.received = f32[32,136,128]{2,1,0:T(8,128)S(1)} all-to-all(f32[32,136,128]{2,1,0:T(8,128)S(1)} %get-tuple-element.52), channel_id=1, replica_groups=mesh['sub'=32,'node'=4] {'sub'}, dimensions={0} | all-to-all | bytes 4456448 | tf_op jit(solution)/shard_map/all_to_all | solution.py:385
  68.6 0.0 copy-done
  68.6 1.8 %owner.1 = f32[32,128,128]{2,1,0:T(8,128)S(1)} custom-call(s32[2]{0:T(128)S(1)} %pad_add_fusion.place, s32[32,4]{1,0:T(8,128)S(1)} %bitcast.27, f32[8,128]{1,0:T(8,128)S(1)} %bitcast.28, f32[32,136,128]{2,1,0:T(8,128)S(1)} %all_to_all.15.received), custom_call_target="tpu_custom_call" | custom-call | bytes 8388608 | tf_op jit(solution)/shard_map/owner/pallas_call | solution.py:387
  70.4 34.0 %all_to_all.16.picked = f32[32,128,128]{2,1,0:T(8,128)S(1)} all-to-all(f32[32,128,128]{2,1,0:T(8,128)S(1)} %owner.1), channel_id=1, replica_groups=mesh['sub'=32,'node'=4] {'sub'}, dimensions={0} | all-to-all | bytes 4194304 | tf_op jit(solution)/shard_map/all_to_all | solution.py:394
  104.4 2.7 %first.1 = (f32[2,256,128]{2,1,0:T(8,128)S(1)}, f32[2,256,128]{2,1,0:T(8,128)S(1)}, bf16[2048,256]{1,0:T(8,128)(2,1)S(1)}, bf16[2048,256]{1,0:T(8,128)(2,1)S(1)}) custom-call(s32[2]{0:T(128)S(1)} %pad_add_fusion.place, f32[32,128,128]{2,1,0:T(8,128)S(1)} %all_to_all.16.picked, bf16[1024,2048]{1,0:T(8,128)(2,1)S(1)} %get-tuple-element.53.f_hi, ...), custom_call_target="tpu_custom_call" | custom-call | flops 2000000000 | bytes 8388608 | tf_op jit(solution)/shard_map/first/pallas_call | solution.py:396
  107.1 0.1 collective-permute-start.2
  107.2 2.6 %second.1 = (f32[2,256,128]{2,1,0:T(8,128)S(1)}, f32[2,256,128]{2,1,0:T(8,128)S(1)}) custom-call(s32[2]{0:T(128)S(1)} %pad_add_fusion.place, bf16[2048,256]{1,0:T(8,128)(2,1)S(1)} %get-tuple-element.61.x_hi, bf16[2048,256]{1,0:T(8,128)(2,1)S(1)} %get-tuple-element.62.x_lo, bf16[1024,2048]{1,0:T(8,128)(2,1)S(1)} %get-tuple-element.53.f_hi, ...), custom_call_target="tpu_custom_call" | custom-call | flops 2000000000 | bytes 8388608 | tf_op jit(solution)/shard_map/second/pallas_call | solution.py:404
  109.8 0.0 collective-permute-done.2
  109.8 0.6 collective-permute-start.4
  110.4 1.2 collective-permute-start.3
  111.6 0.0 collective-permute-done.4
  111.6 1.2 collective-permute-start.5
  112.8 4.1 %collective-permute-done.3 = f32[256,128]{1,0:T(8,128)S(1)} collective-permute-done((f32[256,128]{1,0:T(8,128)S(1)}, f32[256,128]{1,0:T(8,128)S(1)}, u32[]{:S(2)}, u32[]{:S(2)}) %collective-permute-start.3) | collective-permute-done | bytes 131104 | tf_op jit(solution)/shard_map/ppermute | solution.py:420
  116.8 1.9 %collective-permute-done.5 = f32[256,128]{1,0:T(8,128)S(1)} collective-permute-done((f32[256,128]{1,0:T(8,128)S(1)}, f32[256,128]{1,0:T(8,128)S(1)}, u32[]{:S(2)}, u32[]{:S(2)}) %collective-permute-start.5) | collective-permute-done | bytes 131104 | tf_op jit(solution)/shard_map/ppermute | solution.py:421
  118.7 0.1 multiply_reduce_fusion
  118.8 0.1 fusion.4
  118.9 0.1 maximum_add_fusion
  119.0 13.3 %all_to_all.17.squares = f32[32,1,128]{2,1,0:T(1,128)S(1)} all-to-all(f32[32,1,128]{2,1,0:T(1,128)S(1)} %broadcast_in_dim.10), channel_id=1, replica_groups=mesh['sub'=32,'node'=4] {'sub'}, dimensions={0} | all-to-all | bytes 32768 | tf_op jit(solution)/shard_map/all_to_all | solution.py:427
  132.3 0.9 scale.1
  (5 shorter events, 0.1 us)
Async XLA Ops:
  1.1 17.3 %collective-permute-start = (f32[512,256]{1,0:T(8,128)S(1)}, f32[512,256]{1,0:T(8,128)S(1)}, u32[]{:S(2)}, u32[]{:S(2)}) collective-permute-start(f32[512,256]{1,0:T(8,128)S(1)} %constant_dynamic-slice_fusion), channel_id=1, source_target_pairs={{0,4},{2,6},{4,8},{5,1},{6,10},{7,3},{8,12},{9,5},{10,14},{11,7},{... | collective-permute-start | bytes 1572872 | tf_op jit(solution)/shard_map/ppermute | solution.py:319
  6.4 12.0 %copy-start.1 = (s32[8,4]{0,1:T(4,128)S(1)}, s32[8,4]{0,1:T(4,128)}, u32[]{:S(2)}) copy-start(s32[8,4]{0,1:T(4,128)} %param.11) | copy-start | bytes 388
  19.7 2.5 %collective-permute-start.1 = (f32[512,256]{1,0:T(8,128)S(1)}, f32[512,256]{1,0:T(8,128)S(1)}, u32[]{:S(2)}, u32[]{:S(2)}) collective-permute-start(f32[512,256]{1,0:T(8,128)S(1)} %get-tuple-element.44), channel_id=1, source_target_pairs={{0,1},{1,0},{2,3},{3,2},{4,5},{5,4},{6,7},{7,6},{8,9},{9,8},{10,11... | collective-permute-start | bytes 1572872 | tf_op jit(solution)/shard_map/ppermute | solution.py:369
  24.6 44.0 %copy-start = (f32[1024]{0:T(1024)S(1)}, f32[1024]{0:T(1024)}, u32[]{:S(2)}) copy-start(f32[1024]{0:T(1024)} %param.15) | copy-start | bytes 12292
  107.1 2.7 %collective-permute-start.2 = (f32[2,256,128]{2,1,0:T(8,128)S(1)}, f32[2,256,128]{2,1,0:T(8,128)S(1)}, u32[]{:S(2)}, u32[]{:S(2)}) collective-permute-start(f32[2,256,128]{2,1,0:T(8,128)S(1)} %get-tuple-element.60), channel_id=1, source_target_pairs={{0,1},{1,0},{2,3},{3,2},{4,5},{5,4},{6,7},{7,6},{8,9},{9,8},{10,11... | collective-permute-start | bytes 786440 | tf_op jit(solution)/shard_map/ppermute | solution.py:403
  109.8 1.8 %collective-permute-start.4 = (f32[2,256,128]{2,1,0:T(8,128)S(1)}, f32[2,256,128]{2,1,0:T(8,128)S(1)}, u32[]{:S(2)}, u32[]{:S(2)}) collective-permute-start(f32[2,256,128]{2,1,0:T(8,128)S(1)} %get-tuple-element.66), channel_id=1, source_target_pairs={{0,1},{1,0},{2,3},{3,2},{4,5},{5,4},{6,7},{7,6},{8,9},{9,8},{10,11... | collective-permute-start | bytes 786440 | tf_op jit(solution)/shard_map/ppermute | solution.py:412
  110.4 6.4 %collective-permute-start.3 = (f32[256,128]{1,0:T(8,128)S(1)}, f32[256,128]{1,0:T(8,128)S(1)}, u32[]{:S(2)}, u32[]{:S(2)}) collective-permute-start(f32[256,128]{1,0:T(8,128)S(1)} %add_bitcast_fusion.1), channel_id=1, source_target_pairs={{0,2},{1,3},{2,0},{3,1},{4,6},{5,7},{6,4},{7,5},{8,10},{9,11},{10,... | collective-permute-start | bytes 393224 | tf_op jit(solution)/shard_map/ppermute | solution.py:420
  111.6 7.1 %collective-permute-start.5 = (f32[256,128]{1,0:T(8,128)S(1)}, f32[256,128]{1,0:T(8,128)S(1)}, u32[]{:S(2)}, u32[]{:S(2)}) collective-permute-start(f32[256,128]{1,0:T(8,128)S(1)} %add_bitcast_fusion), channel_id=1, source_target_pairs={{0,2},{1,3},{2,0},{3,1},{4,6},{5,7},{6,4},{7,5},{8,10},{9,11},{10,... | collective-permute-start | bytes 393224 | tf_op jit(solution)/shard_map/ppermute | solution.py:421

commit v6 on v5

--- a/solution.py
+++ b/solution.py
@@ -174,7 +174,7 @@
         n, c = divmod(k, 2)
         for p in range(4):
             for h in range(2):
-                row = ((c * 4 + p) * 2 + h) * 8
+                row = ((p * 2 + c) * 2 + h) * 8
                 tile = part[p * BLK : (p + 1) * BLK, h * LANES : (h + 1) * LANES]
                 pieces[n * 16 : (n + 1) * 16, row : row + 8, :] = tile.reshape(16, 8, LANES)
     pieces[:, 128:136, :] = jnp.broadcast_to(ids[...][None], (32, 8, LANES))
@@ -188,11 +188,10 @@
     total[...] = jnp.zeros_like(total)
 
     def add(t, carry):
-        for p in range(4):
-            g = maps[t, p]
-            for c in range(2):
-                r = (c * 4 + p) * 16
-                total[g, c] += received[t, r : r + 16, :]
+        groups = [maps[t, p] for p in range(4)]
+        sums = [total[g] + received[t, p * 32 : (p + 1) * 32, :] for p, g in enumerate(groups)]
+        for g, value in zip(groups, sums):
+            total[g] = value
         return carry
 
     lax.fori_loop(0, 32, add, 0, unroll=4)
@@ -203,18 +202,15 @@
         gap = z_r - jnp.sum(jnp.where(pick, row, 0.0), axis=1, keepdims=True)
         gap = jnp.concatenate([gap, gap], 0)
         modulus = gap * gap + z_i * z_i
-        real, imag = total[g, 0], total[g, 1]
+        real, imag = total[g, :16], total[g, 16:]
         c_r = (real * gap + imag * z_i) / modulus
         c_i = (imag * gap - real * z_i) / modulus
-        total[g, 0] = w_r * c_r - w_i * c_i
-        total[g, 1] = w_r * c_i + w_i * c_r
+        total[g, :16] = w_r * c_r - w_i * c_i
+        total[g, 16:] = w_r * c_i + w_i * c_r
 
     def give(t, carry):
         for p in range(4):
-            g = maps[t, p]
-            for c in range(2):
-                r = (c * 4 + p) * 16
-                back[t, r : r + 16, :] = total[g, c]
+            back[t, p * 32 : (p + 1) * 32, :] = total[maps[t, p]]
         return carry
 
     lax.fori_loop(0, 32, give, 0, unroll=4)
@@ -226,7 +222,7 @@
         n, c = divmod(k, 2)
         for p in range(4):
             for h in range(2):
-                row = ((c * 4 + p) * 2 + h) * 8
+                row = ((p * 2 + c) * 2 + h) * 8
                 tile = picked[n * 16 : (n + 1) * 16, row : row + 8, :].reshape(BLK, LANES)
                 rows = slice(k * sep + p * BLK, k * sep + (p + 1) * BLK)
                 cols = slice(h * LANES, (h + 1) * LANES)
@@ -389,7 +385,7 @@
         "owner",
         [SMEM, SMEM, VMEM, VMEM],
         [(subs, 128, LANES)],
-        [pltpu.VMEM((GROUPS, 2, 16, LANES), F32)],
+        [pltpu.VMEM((GROUPS, 32, LANES), F32)],
     )(place, maps, separator_shift.reshape(GROUPS, LANES), received)
     picked = lax.all_to_all(back, "sub", 0, 0, tiled=True)
     operators = (f_hi, f_lo, r_hi, r_lo, w_hi, w_lo)

time: 133 us -> 133 us (level)
  no operation moved by 1% of the time
where the time goes in v6:
time: 133 us
  blocking collectives  91.3 us (69%)
  Pallas kernels  24.3 us (18%)
  starting transfers between devices  8.3 us (6%)
  waiting for transfers between devices  7.44 us (6%)
    all_to_all x1, blocking collectives, shards(): received = lax.all_to_all(pieces, 'sub', 0, 0, tiled=True)  44 us
    all_to_all x1, blocking collectives, shards(): picked = lax.all_to_all(back, 'sub', 0, 0, tiled=True)  34 us
    all_to_all x1, blocking collectives, shards(): gathered = lax.all_to_all(squares, 'sub', 0, 0, tiled=True)  13.3 us
    pallas_call x1, Pallas kernels, shards(): call(prepare_kernel, 'prepare', [SMEM] + [HBM] * 6, [half((blocks, BLK, w...  10.5 us
    ppermute x1, starting transfers between devices, shards(): halo = lax.ppermute(edge, ('sub', 'node'), ring)  5.21 us
    ppermute x1, waiting for transfers between devices, shards(): far_a = lax.ppermute(both(1 - chip, keep_a, theirs_a), 'node', swap_chip)  4.07 us
  transfers between devices with their start and end apart: 6, of which 3 were waited for; matrix products, arithmetic and copies ran while one was open for 0% of the time, Pallas kernels for 12%

profile of v6, /device:TPU:0, one launch (start us, length us, event | category | flops | bytes accessed | tf_op | source)
XLA Modules:
  0.0 133.0 jit_solution(9917177025939011516)
XLA Ops:
  0.0 1.1 constant_dynamic-slice_fusion
  1.1 5.2 %collective-permute-start = (f32[512,256]{1,0:T(8,128)S(1)}, f32[512,256]{1,0:T(8,128)S(1)}, u32[]{:S(2)}, u32[]{:S(2)}) collective-permute-start(f32[512,256]{1,0:T(8,128)S(1)} %constant_dynamic-slice_fusion), channel_id=1, source_target_pairs={{0,4},{2,6},{4,8},{5,1},{6,10},{7,3},{8,12},{9,5},{10,14},{11,7},{... | collective-permute-start | bytes 1572872 | tf_op jit(solution)/shard_map/ppermute | solution.py:315
  6.3 0.1 pad_add_fusion.place
  6.4 0.0 copy-start.1
  6.4 10.5 %prepare.1 = (bf16[8,128,256]{2,1,0:T(8,128)(2,1)S(1)}, bf16[8,128,256]{2,1,0:T(8,128)(2,1)S(1)}, f32[4,128,256]{2,1,0:T(8,128)S(1)}, bf16[4,128,512]{2,1,0:T(8,...) custom-call(s32[2]{0:T(128)S(1)} %pad_add_fusion.place, ...), custom_call_target="tpu_custom_call" | custom-call | flops 8000000000 | bytes 8388608 | tf_op jit(solution)/shard_map/prepare/pallas_call | solution.py:320
  16.9 1.5 %collective-permute-done.halo = f32[512,256]{1,0:T(8,128)S(1)} collective-permute-done((f32[512,256]{1,0:T(8,128)S(1)}, f32[512,256]{1,0:T(8,128)S(1)}, u32[]{:S(2)}, u32[]{:S(2)}) %collective-permute-start) | collective-permute-done | bytes 524320 | tf_op jit(solution)/shard_map/ppermute | solution.py:315
  18.3 0.0 copy-done.1
  18.3 1.3 %residual.1 = (f32[512,256]{1,0:T(8,128)S(1)}, bf16[512,256]{1,0:T(8,128)(2,1)S(1)}, bf16[512,256]{1,0:T(8,128)(2,1)S(1)}) custom-call(s32[2]{0:T(128)S(1)} %pad_add_fusion.place, s32[4,8]{1,0:T(4,128)S(1)} %bitcast.29, f32[512,256]{1,0:T(8,128)S(1)} %collective-permute-done.halo, bf16[8,128,256]{2,1,0:T(8,128)(2,1)S(1)} %get-tuple-element.39.own_hi, ...), custom_call_target="tpu_custom_call" | custom-call | flops 1000000000 | bytes 8388608 | tf_op jit(solution)/shard_map/residual/pallas_call | solution.py:357
  19.7 0.1 collective-permute-start.1
  19.8 2.4 %mine.1.sums = f32[2048,256]{1,0:T(8,128)S(1)} custom-call(s32[2]{0:T(128)S(1)} %pad_add_fusion.place, bf16[2,2048,512]{2,1,0:T(8,128)(2,1)S(1)} %get-tuple-element.45.e_hi, bf16[2,2048,512]{2,1,0:T(8,128)(2,1)S(1)} %get-tuple-element.46.e_lo, bf16[512,256]{1,0:T(8,128)(2,1)S(1)} %get-tuple-element.47.r_hi.m_hi, bf16[512,256]{1,0:T(8,128)(2,1)S(1)} %get-tuple-element.48.r_lo.m_lo), custom_call_target="tpu_custom_call" | custom-call | flops 4000000000 | bytes 8388608 | tf_op jit(solution)/shard_map/mine/pallas_call | solution.py:366
  22.2 0.0 collective-permute-done.1.theirs
  22.2 2.4 %theirs.1 = (bf16[2,512,256]{2,1,0:T(8,128)(2,1)S(1)}, bf16[2,512,256]{2,1,0:T(8,128)(2,1)S(1)}, f32[32,136,128]{2,1,0:T(8,128)S(1)}) custom-call(s32[2]{0:T(128)S(1)} %pad_add_fusion.place, f32[2048,256]{1,0:T(8,128)S(1)} %mine.1.sums, f32[512,256]{1,0:T(8,128)S(1)} %collective-permute-done.1.theirs, bf16[2,2048,512]{2,1,0:T(8,128)(2,1)S(1)} %get-tuple-element.45.e_hi, ...), custom_call_target="tpu_custom_call" | custom-call | flops 4000000000 | bytes 8388608 | tf_op jit(solution)/shard_map/theirs/pallas_call | solution.py:374
  24.6 0.0 copy-start
  24.6 44.0 %all_to_all.15.received = f32[32,136,128]{2,1,0:T(8,128)S(1)} all-to-all(f32[32,136,128]{2,1,0:T(8,128)S(1)} %get-tuple-element.52), channel_id=1, replica_groups=mesh['sub'=32,'node'=4] {'sub'}, dimensions={0} | all-to-all | bytes 4456448 | tf_op jit(solution)/shard_map/all_to_all | solution.py:381
  68.6 0.0 copy-done
  68.6 1.6 %owner.1 = f32[32,128,128]{2,1,0:T(8,128)S(1)} custom-call(s32[2]{0:T(128)S(1)} %pad_add_fusion.place, s32[32,4]{1,0:T(8,128)S(1)} %bitcast.27, f32[8,128]{1,0:T(8,128)S(1)} %bitcast.28, f32[32,136,128]{2,1,0:T(8,128)S(1)} %all_to_all.15.received), custom_call_target="tpu_custom_call" | custom-call | bytes 8388608 | tf_op jit(solution)/shard_map/owner/pallas_call | solution.py:383
  70.2 34.0 %all_to_all.16.picked = f32[32,128,128]{2,1,0:T(8,128)S(1)} all-to-all(f32[32,128,128]{2,1,0:T(8,128)S(1)} %owner.1), channel_id=1, replica_groups=mesh['sub'=32,'node'=4] {'sub'}, dimensions={0} | all-to-all | bytes 4194304 | tf_op jit(solution)/shard_map/all_to_all | solution.py:390
  104.2 2.6 %first.1 = (f32[2,256,128]{2,1,0:T(8,128)S(1)}, f32[2,256,128]{2,1,0:T(8,128)S(1)}, bf16[2048,256]{1,0:T(8,128)(2,1)S(1)}, bf16[2048,256]{1,0:T(8,128)(2,1)S(1)}) custom-call(s32[2]{0:T(128)S(1)} %pad_add_fusion.place, f32[32,128,128]{2,1,0:T(8,128)S(1)} %all_to_all.16.picked, bf16[1024,2048]{1,0:T(8,128)(2,1)S(1)} %get-tuple-element.53.f_hi, ...), custom_call_target="tpu_custom_call" | custom-call | flops 2000000000 | bytes 8388608 | tf_op jit(solution)/shard_map/first/pallas_call | solution.py:392
  106.8 0.1 collective-permute-start.2
  106.9 2.6 %second.1 = (f32[2,256,128]{2,1,0:T(8,128)S(1)}, f32[2,256,128]{2,1,0:T(8,128)S(1)}) custom-call(s32[2]{0:T(128)S(1)} %pad_add_fusion.place, bf16[2048,256]{1,0:T(8,128)(2,1)S(1)} %get-tuple-element.61.x_hi, bf16[2048,256]{1,0:T(8,128)(2,1)S(1)} %get-tuple-element.62.x_lo, bf16[1024,2048]{1,0:T(8,128)(2,1)S(1)} %get-tuple-element.53.f_hi, ...), custom_call_target="tpu_custom_call" | custom-call | flops 2000000000 | bytes 8388608 | tf_op jit(solution)/shard_map/second/pallas_call | solution.py:400
  109.6 0.0 collective-permute-done.2
  109.6 0.6 collective-permute-start.4
  110.2 1.2 collective-permute-start.3
  111.4 0.0 collective-permute-done.4
  111.4 1.2 collective-permute-start.5
  112.5 4.1 %collective-permute-done.3 = f32[256,128]{1,0:T(8,128)S(1)} collective-permute-done((f32[256,128]{1,0:T(8,128)S(1)}, f32[256,128]{1,0:T(8,128)S(1)}, u32[]{:S(2)}, u32[]{:S(2)}) %collective-permute-start.3) | collective-permute-done | bytes 131104 | tf_op jit(solution)/shard_map/ppermute | solution.py:416
  116.6 1.9 %collective-permute-done.5 = f32[256,128]{1,0:T(8,128)S(1)} collective-permute-done((f32[256,128]{1,0:T(8,128)S(1)}, f32[256,128]{1,0:T(8,128)S(1)}, u32[]{:S(2)}, u32[]{:S(2)}) %collective-permute-start.5) | collective-permute-done | bytes 131104 | tf_op jit(solution)/shard_map/ppermute | solution.py:417
  118.5 0.1 multiply_reduce_fusion
  118.6 0.1 fusion.4
  118.7 0.1 maximum_add_fusion
  118.7 13.3 %all_to_all.17.squares = f32[32,1,128]{2,1,0:T(1,128)S(1)} all-to-all(f32[32,1,128]{2,1,0:T(1,128)S(1)} %broadcast_in_dim.10), channel_id=1, replica_groups=mesh['sub'=32,'node'=4] {'sub'}, dimensions={0} | all-to-all | bytes 32768 | tf_op jit(solution)/shard_map/all_to_all | solution.py:423
  132.1 0.9 scale.1
  (5 shorter events, 0.1 us)
Async XLA Ops:
  1.1 17.3 %collective-permute-start = (f32[512,256]{1,0:T(8,128)S(1)}, f32[512,256]{1,0:T(8,128)S(1)}, u32[]{:S(2)}, u32[]{:S(2)}) collective-permute-start(f32[512,256]{1,0:T(8,128)S(1)} %constant_dynamic-slice_fusion), channel_id=1, source_target_pairs={{0,4},{2,6},{4,8},{5,1},{6,10},{7,3},{8,12},{9,5},{10,14},{11,7},{... | collective-permute-start | bytes 1572872 | tf_op jit(solution)/shard_map/ppermute | solution.py:315
  6.4 12.0 %copy-start.1 = (s32[8,4]{0,1:T(4,128)S(1)}, s32[8,4]{0,1:T(4,128)}, u32[]{:S(2)}) copy-start(s32[8,4]{0,1:T(4,128)} %param.11) | copy-start | bytes 388
  19.7 2.5 %collective-permute-start.1 = (f32[512,256]{1,0:T(8,128)S(1)}, f32[512,256]{1,0:T(8,128)S(1)}, u32[]{:S(2)}, u32[]{:S(2)}) collective-permute-start(f32[512,256]{1,0:T(8,128)S(1)} %get-tuple-element.44), channel_id=1, source_target_pairs={{0,1},{1,0},{2,3},{3,2},{4,5},{5,4},{6,7},{7,6},{8,9},{9,8},{10,11... | collective-permute-start | bytes 1572872 | tf_op jit(solution)/shard_map/ppermute | solution.py:365
  24.6 44.0 %copy-start = (f32[1024]{0:T(1024)S(1)}, f32[1024]{0:T(1024)}, u32[]{:S(2)}) copy-start(f32[1024]{0:T(1024)} %param.15) | copy-start | bytes 12292
  106.8 2.7 %collective-permute-start.2 = (f32[2,256,128]{2,1,0:T(8,128)S(1)}, f32[2,256,128]{2,1,0:T(8,128)S(1)}, u32[]{:S(2)}, u32[]{:S(2)}) collective-permute-start(f32[2,256,128]{2,1,0:T(8,128)S(1)} %get-tuple-element.60), channel_id=1, source_target_pairs={{0,1},{1,0},{2,3},{3,2},{4,5},{5,4},{6,7},{7,6},{8,9},{9,8},{10,11... | collective-permute-start | bytes 786440 | tf_op jit(solution)/shard_map/ppermute | solution.py:399
  109.6 1.8 %collective-permute-start.4 = (f32[2,256,128]{2,1,0:T(8,128)S(1)}, f32[2,256,128]{2,1,0:T(8,128)S(1)}, u32[]{:S(2)}, u32[]{:S(2)}) collective-permute-start(f32[2,256,128]{2,1,0:T(8,128)S(1)} %get-tuple-element.66), channel_id=1, source_target_pairs={{0,1},{1,0},{2,3},{3,2},{4,5},{5,4},{6,7},{7,6},{8,9},{9,8},{10,11... | collective-permute-start | bytes 786440 | tf_op jit(solution)/shard_map/ppermute | solution.py:408
  110.2 6.4 %collective-permute-start.3 = (f32[256,128]{1,0:T(8,128)S(1)}, f32[256,128]{1,0:T(8,128)S(1)}, u32[]{:S(2)}, u32[]{:S(2)}) collective-permute-start(f32[256,128]{1,0:T(8,128)S(1)} %add_bitcast_fusion.1), channel_id=1, source_target_pairs={{0,2},{1,3},{2,0},{3,1},{4,6},{5,7},{6,4},{7,5},{8,10},{9,11},{10,... | collective-permute-start | bytes 393224 | tf_op jit(solution)/shard_map/ppermute | solution.py:416
  111.4 7.1 %collective-permute-start.5 = (f32[256,128]{1,0:T(8,128)S(1)}, f32[256,128]{1,0:T(8,128)S(1)}, u32[]{:S(2)}, u32[]{:S(2)}) collective-permute-start(f32[256,128]{1,0:T(8,128)S(1)} %add_bitcast_fusion), channel_id=1, source_target_pairs={{0,2},{1,3},{2,0},{3,1},{4,6},{5,7},{6,4},{7,5},{8,10},{9,11},{10,... | collective-permute-start | bytes 393224 | tf_op jit(solution)/shard_map/ppermute | solution.py:417

commit v7 on v6

--- a/solution.py
+++ b/solution.py
@@ -59,7 +59,7 @@
     own_hi, own_lo, scaled, m_hi, m_lo, e_hi, e_lo, f_hi, f_lo, w_hi, w_lo, ids, columns,
     own, ritz, mats, inverses, panel, ids_sem, ritz_sem, mats_sem, panel_sem, sems, map_copy,
 ):
-    node, core = place[1] * LOCAL, place[1] % 2
+    node, core, side_of = place[1] * LOCAL, place[1] % 2, place[2]
     blocks, sep = own.shape[0] // BLK, panel.shape[0]
     per_core = blocks // 2
     parts = [(n, c) for n in range(LOCAL) for c in range(2)]
@@ -73,7 +73,7 @@
             )
         )
     my_mats = pltpu.make_async_copy(
-        mats_hbm.at[pl.ds(core * per_core, per_core)], mats, mats_sem
+        mats_hbm.at[pl.ds(side_of * per_core, per_core)], mats, mats_sem
     )
     whole_panel = pltpu.make_async_copy(panel_hbm.at[0], panel, panel_sem)
     small = [
@@ -124,7 +124,7 @@
         low, high = halves(top, bottom)
         columns[side] = jnp.where(core == 0, low, high)
     for g in range(per_core):
-        rows = pl.ds(pl.multiple_of((core * per_core + g) * BLK, BLK), BLK)
+        rows = pl.ds(pl.multiple_of((side_of * per_core + g) * BLK, BLK), BLK)
         scaled[g] = own[rows, :] * ritz[...]
         m_hi[g], m_lo[g] = split(jnp.concatenate([mats[g, q] for q in range(4)], 1))
     lane = lax.broadcasted_iota(jnp.int32, ids.shape, 1)
@@ -137,16 +137,16 @@
 def residual_kernel(
     place, lists, halo, own_hi, own_lo, scaled, m_hi, m_lo, residual, r_hi, r_lo, ext_hi, ext_lo
 ):
-    sub, core = place[0], place[1] % 2
+    sub, side = place[0], place[2]
     blocks, per_core = own_hi.shape[0], m_hi.shape[0]
     hi, lo = split(halo[...].reshape(HALO, BLK, halo.shape[1]))
-    ext_hi[pl.ds(core * blocks, HALO)] = hi
-    ext_lo[pl.ds(core * blocks, HALO)] = lo
-    start = HALO - core * HALO
+    ext_hi[pl.ds(side * blocks, HALO)] = hi
+    ext_lo[pl.ds(side * blocks, HALO)] = lo
+    start = HALO - side * HALO
     ext_hi[pl.ds(start, blocks)] = own_hi[...]
     ext_lo[pl.ds(start, blocks)] = own_lo[...]
     for g in range(per_core):
-        where = [lists[q, core * per_core + g] - sub * blocks + start for q in range(4)]
+        where = [lists[q, side * per_core + g] - sub * blocks + start for q in range(4)]
         rhs = [jnp.concatenate([e[w] for w in where], 0) for e in (ext_hi, ext_lo)]
         rows = slice(g * BLK, (g + 1) * BLK)
         res = dot3((m_hi[g], m_lo[g]), rhs) - scaled[g]
@@ -155,18 +155,18 @@
 
 
 def mine_kernel(place, e_hi, e_lo, r_hi, r_lo, sums):
-    core = place[1] % 2
-    sums[...] = dot3((e_hi[core], e_lo[core]), (r_hi[...], r_lo[...]))
+    side = place[2]
+    sums[...] = dot3((e_hi[side], e_lo[side]), (r_hi[...], r_lo[...]))
 
 
 def theirs_kernel(
     place, sums, theirs, e_hi, e_lo, m_hi, m_lo, ids, r_hi, r_lo, pieces
 ):
-    core = place[1] % 2
-    other = 1 - core
+    side = place[2]
+    other = 1 - side
     hi, lo = split(theirs[...])
     r_hi[other], r_lo[other] = hi, lo
-    r_hi[core], r_lo[core] = m_hi[...], m_lo[...]
+    r_hi[side], r_lo[side] = m_hi[...], m_lo[...]
     sep = e_hi.shape[1] // (2 * LOCAL)
     for k in range(2 * LOCAL):
         span = slice(k * sep, (k + 1) * sep)
@@ -298,18 +298,19 @@
     rows, width = search_vectors.shape
     subs, nodes = lax.axis_size("sub"), lax.axis_size("node")
     sub, node = lax.axis_index("sub"), lax.axis_index("node")
-    place = jnp.stack([sub, node]).astype(jnp.int32)
+    side = (node + sub) % 2
+    place = jnp.stack([sub, node, side]).astype(jnp.int32)
 
     halo_rows = HALO * BLK
     edge = lax.dynamic_slice_in_dim(
-        search_vectors, jnp.where(node % 2 == 0, rows - halo_rows, 0), halo_rows, 0
+        search_vectors, jnp.where(side == 0, rows - halo_rows, 0), halo_rows, 0
     )
     ring = []
     for t in range(subs):
         for n in range(nodes):
-            d = t + 1 if n % 2 == 0 else t - 1
+            d = t + 1 if (n + t) % 2 == 0 else t - 1
             if 0 <= d < subs:
-                ring.append((t * nodes + n, d * nodes + n))
+                ring.append((t * nodes + n, d * nodes + (n ^ 3)))
     swap_core = [(i, i ^ 1) for i in range(nodes)]
     swap_chip = [(i, i ^ 2) for i in range(nodes)]
     halo = lax.ppermute(edge, ("sub", "node"), ring)

time: 133 us -> 131 us (0.985)
  blocking collectives: 91.3 us -> 88.4 us
    all_to_all x1, blocking collectives: 44 us -> 41.2 us  [shards(): received = lax.all_to_all(pieces, 'sub', 0, 0, tiled=True)]
where the time goes in v7:
time: 131 us; the launch traced here: 130 us
  blocking collectives  88.4 us (67%)
  Pallas kernels  24.4 us (19%)
  starting transfers between devices  8.79 us (7%)
  waiting for transfers between devices  7.29 us (6%)
    all_to_all x1, blocking collectives, shards(): received = lax.all_to_all(pieces, 'sub', 0, 0, tiled=True)  41.2 us
    all_to_all x1, blocking collectives, shards(): picked = lax.all_to_all(back, 'sub', 0, 0, tiled=True)  33.5 us
    all_to_all x1, blocking collectives, shards(): gathered = lax.all_to_all(squares, 'sub', 0, 0, tiled=True)  13.7 us
    pallas_call x1, Pallas kernels, shards(): call(prepare_kernel, 'prepare', [SMEM] + [HBM] * 6, [half((blocks, BLK, w...  10.5 us
    ppermute x1, starting transfers between devices, shards(): halo = lax.ppermute(edge, ('sub', 'node'), ring)  4.47 us
    ppermute x1, waiting for transfers between devices, shards(): far_a = lax.ppermute(both(1 - chip, keep_a, theirs_a), 'node', swap_chip)  3.69 us
    pallas_call x1, Pallas kernels, shards(): call(first_kernel, 'first', [SMEM] + [VMEM] * 7, [(2, rows // 4, LANES)]...  2.64 us
    pallas_call x1, Pallas kernels, shards(): call(second_kernel, 'second', [SMEM] + [VMEM] * 8, [(2, rows // 4, LANES)...  2.63 us
  transfers between devices with their start and end apart: 6, of which 3 were waited for; matrix products, arithmetic and copies ran while one was open for 0% of the time, Pallas kernels for 12%

profile of v7, /device:TPU:0, one launch (start us, length us, event | category | flops | bytes accessed | tf_op | source)
XLA Modules:
  0.0 130.4 jit_solution(4254294265196099438)
XLA Ops:
  0.0 1.1 constant_dynamic-slice_fusion
  1.1 4.5 %collective-permute-start = (f32[512,256]{1,0:T(8,128)S(1)}, f32[512,256]{1,0:T(8,128)S(1)}, u32[]{:S(2)}, u32[]{:S(2)}) collective-permute-start(f32[512,256]{1,0:T(8,128)S(1)} %constant_dynamic-slice_fusion), channel_id=1, source_target_pairs={{0,7},{2,5},{4,3},{5,10},{6,1},{7,8},{8,15},{9,6},{10,13},{11,4},{... | collective-permute-start | bytes 1572872 | tf_op jit(solution)/shard_map/ppermute | solution.py:316
  5.6 0.1 pad_add_fusion.place
  5.6 0.0 copy-start.1
  5.6 10.5 %prepare.1 = (bf16[8,128,256]{2,1,0:T(8,128)(2,1)S(1)}, bf16[8,128,256]{2,1,0:T(8,128)(2,1)S(1)}, f32[4,128,256]{2,1,0:T(8,128)S(1)}, bf16[4,128,512]{2,1,0:T(8,...) custom-call(s32[3]{0:T(128)S(1)} %pad_add_fusion.place, ...), custom_call_target="tpu_custom_call" | custom-call | flops 8000000000 | bytes 8388608 | tf_op jit(solution)/shard_map/prepare/pallas_call | solution.py:321
  16.1 1.7 %collective-permute-done.halo = f32[512,256]{1,0:T(8,128)S(1)} collective-permute-done((f32[512,256]{1,0:T(8,128)S(1)}, f32[512,256]{1,0:T(8,128)S(1)}, u32[]{:S(2)}, u32[]{:S(2)}) %collective-permute-start) | collective-permute-done | bytes 524320 | tf_op jit(solution)/shard_map/ppermute | solution.py:316
  17.8 0.0 copy-done.1
  17.8 1.4 %residual.1 = (f32[512,256]{1,0:T(8,128)S(1)}, bf16[512,256]{1,0:T(8,128)(2,1)S(1)}, bf16[512,256]{1,0:T(8,128)(2,1)S(1)}) custom-call(s32[3]{0:T(128)S(1)} %pad_add_fusion.place, s32[4,8]{1,0:T(4,128)S(1)} %bitcast.30, f32[512,256]{1,0:T(8,128)S(1)} %collective-permute-done.halo, bf16[8,128,256]{2,1,0:T(8,128)(2,1)S(1)} %get-tuple-element.39.own_hi, ...), custom_call_target="tpu_custom_call" | custom-call | flops 1000000000 | bytes 8388608 | tf_op jit(solution)/shard_map/residual/pallas_call | solution.py:358
  19.2 0.9 collective-permute-start.1
  20.1 2.4 %mine.1.sums = f32[2048,256]{1,0:T(8,128)S(1)} custom-call(s32[3]{0:T(128)S(1)} %pad_add_fusion.place, bf16[2,2048,512]{2,1,0:T(8,128)(2,1)S(1)} %get-tuple-element.45.e_hi, bf16[2,2048,512]{2,1,0:T(8,128)(2,1)S(1)} %get-tuple-element.46.e_lo, bf16[512,256]{1,0:T(8,128)(2,1)S(1)} %get-tuple-element.47.r_hi.m_hi, bf16[512,256]{1,0:T(8,128)(2,1)S(1)} %get-tuple-element.48.r_lo.m_lo), custom_call_target="tpu_custom_call" | custom-call | flops 4000000000 | bytes 8388608 | tf_op jit(solution)/shard_map/mine/pallas_call | solution.py:367
  22.6 0.0 collective-permute-done.1.theirs
  22.6 2.4 %theirs.1 = (bf16[2,512,256]{2,1,0:T(8,128)(2,1)S(1)}, bf16[2,512,256]{2,1,0:T(8,128)(2,1)S(1)}, f32[32,136,128]{2,1,0:T(8,128)S(1)}) custom-call(s32[3]{0:T(128)S(1)} %pad_add_fusion.place, f32[2048,256]{1,0:T(8,128)S(1)} %mine.1.sums, f32[512,256]{1,0:T(8,128)S(1)} %collective-permute-done.1.theirs, bf16[2,2048,512]{2,1,0:T(8,128)(2,1)S(1)} %get-tuple-element.45.e_hi, ...), custom_call_target="tpu_custom_call" | custom-call | flops 4000000000 | bytes 8388608 | tf_op jit(solution)/shard_map/theirs/pallas_call | solution.py:375
  25.0 0.0 copy-start
  25.0 41.2 %all_to_all.15.received = f32[32,136,128]{2,1,0:T(8,128)S(1)} all-to-all(f32[32,136,128]{2,1,0:T(8,128)S(1)} %get-tuple-element.52), channel_id=1, replica_groups=mesh['sub'=32,'node'=4] {'sub'}, dimensions={0} | all-to-all | bytes 4456448 | tf_op jit(solution)/shard_map/all_to_all | solution.py:382
  66.2 0.0 copy-done
  66.2 1.5 %owner.1 = f32[32,128,128]{2,1,0:T(8,128)S(1)} custom-call(s32[3]{0:T(128)S(1)} %pad_add_fusion.place, s32[32,4]{1,0:T(8,128)S(1)} %bitcast.28, f32[8,128]{1,0:T(8,128)S(1)} %bitcast.29, f32[32,136,128]{2,1,0:T(8,128)S(1)} %all_to_all.15.received), custom_call_target="tpu_custom_call" | custom-call | bytes 8388608 | tf_op jit(solution)/shard_map/owner/pallas_call | solution.py:384
  67.8 33.5 %all_to_all.16.picked = f32[32,128,128]{2,1,0:T(8,128)S(1)} all-to-all(f32[32,128,128]{2,1,0:T(8,128)S(1)} %owner.1), channel_id=1, replica_groups=mesh['sub'=32,'node'=4] {'sub'}, dimensions={0} | all-to-all | bytes 4194304 | tf_op jit(solution)/shard_map/all_to_all | solution.py:391
  101.3 2.6 %first.1 = (f32[2,256,128]{2,1,0:T(8,128)S(1)}, f32[2,256,128]{2,1,0:T(8,128)S(1)}, bf16[2048,256]{1,0:T(8,128)(2,1)S(1)}, bf16[2048,256]{1,0:T(8,128)(2,1)S(1)}) custom-call(s32[3]{0:T(128)S(1)} %pad_add_fusion.place, f32[32,128,128]{2,1,0:T(8,128)S(1)} %all_to_all.16.picked, bf16[1024,2048]{1,0:T(8,128)(2,1)S(1)} %get-tuple-element.53.f_hi, ...), custom_call_target="tpu_custom_call" | custom-call | flops 2000000000 | bytes 8388608 | tf_op jit(solution)/shard_map/first/pallas_call | solution.py:393
  103.9 0.1 collective-permute-start.2
  104.0 2.6 %second.1 = (f32[2,256,128]{2,1,0:T(8,128)S(1)}, f32[2,256,128]{2,1,0:T(8,128)S(1)}) custom-call(s32[3]{0:T(128)S(1)} %pad_add_fusion.place, bf16[2048,256]{1,0:T(8,128)(2,1)S(1)} %get-tuple-element.61.x_hi, bf16[2048,256]{1,0:T(8,128)(2,1)S(1)} %get-tuple-element.62.x_lo, bf16[1024,2048]{1,0:T(8,128)(2,1)S(1)} %get-tuple-element.53.f_hi, ...), custom_call_target="tpu_custom_call" | custom-call | flops 2000000000 | bytes 8388608 | tf_op jit(solution)/shard_map/second/pallas_call | solution.py:401
  106.6 0.0 collective-permute-done.2
  106.7 0.6 collective-permute-start.4
  107.2 1.6 %collective-permute-start.3 = (f32[256,128]{1,0:T(8,128)S(1)}, f32[256,128]{1,0:T(8,128)S(1)}, u32[]{:S(2)}, u32[]{:S(2)}) collective-permute-start(f32[256,128]{1,0:T(8,128)S(1)} %add_bitcast_fusion.1), channel_id=1, source_target_pairs={{0,2},{1,3},{2,0},{3,1},{4,6},{5,7},{6,4},{7,5},{8,10},{9,11},{10,... | collective-permute-start | bytes 393224 | tf_op jit(solution)/shard_map/ppermute | solution.py:417
  108.8 0.0 collective-permute-done.4
  108.8 1.2 collective-permute-start.5
  110.0 3.7 %collective-permute-done.3 = f32[256,128]{1,0:T(8,128)S(1)} collective-permute-done((f32[256,128]{1,0:T(8,128)S(1)}, f32[256,128]{1,0:T(8,128)S(1)}, u32[]{:S(2)}, u32[]{:S(2)}) %collective-permute-start.3) | collective-permute-done | bytes 131104 | tf_op jit(solution)/shard_map/ppermute | solution.py:417
  113.7 1.9 %collective-permute-done.5 = f32[256,128]{1,0:T(8,128)S(1)} collective-permute-done((f32[256,128]{1,0:T(8,128)S(1)}, f32[256,128]{1,0:T(8,128)S(1)}, u32[]{:S(2)}, u32[]{:S(2)}) %collective-permute-start.5) | collective-permute-done | bytes 131104 | tf_op jit(solution)/shard_map/ppermute | solution.py:418
  115.6 0.1 multiply_reduce_fusion
  115.7 0.1 fusion.4
  115.7 0.1 maximum_add_fusion
  115.8 13.7 %all_to_all.17.squares = f32[32,1,128]{2,1,0:T(1,128)S(1)} all-to-all(f32[32,1,128]{2,1,0:T(1,128)S(1)} %broadcast_in_dim.10), channel_id=1, replica_groups=mesh['sub'=32,'node'=4] {'sub'}, dimensions={0} | all-to-all | bytes 32768 | tf_op jit(solution)/shard_map/all_to_all | solution.py:424
  129.5 0.9 scale.1
  (5 shorter events, 0.1 us)
Async XLA Ops:
  1.1 16.7 %collective-permute-start = (f32[512,256]{1,0:T(8,128)S(1)}, f32[512,256]{1,0:T(8,128)S(1)}, u32[]{:S(2)}, u32[]{:S(2)}) collective-permute-start(f32[512,256]{1,0:T(8,128)S(1)} %constant_dynamic-slice_fusion), channel_id=1, source_target_pairs={{0,7},{2,5},{4,3},{5,10},{6,1},{7,8},{8,15},{9,6},{10,13},{11,4},{... | collective-permute-start | bytes 1572872 | tf_op jit(solution)/shard_map/ppermute | solution.py:316
  5.6 12.2 %copy-start.1 = (s32[8,4]{0,1:T(4,128)S(1)}, s32[8,4]{0,1:T(4,128)}, u32[]{:S(2)}) copy-start(s32[8,4]{0,1:T(4,128)} %param.11) | copy-start | bytes 388
  19.2 3.4 %collective-permute-start.1 = (f32[512,256]{1,0:T(8,128)S(1)}, f32[512,256]{1,0:T(8,128)S(1)}, u32[]{:S(2)}, u32[]{:S(2)}) collective-permute-start(f32[512,256]{1,0:T(8,128)S(1)} %get-tuple-element.44), channel_id=1, source_target_pairs={{0,1},{1,0},{2,3},{3,2},{4,5},{5,4},{6,7},{7,6},{8,9},{9,8},{10,11... | collective-permute-start | bytes 1572872 | tf_op jit(solution)/shard_map/ppermute | solution.py:366
  25.0 41.2 %copy-start = (f32[1024]{0:T(1024)S(1)}, f32[1024]{0:T(1024)}, u32[]{:S(2)}) copy-start(f32[1024]{0:T(1024)} %param.15) | copy-start | bytes 12292
  103.9 2.7 %collective-permute-start.2 = (f32[2,256,128]{2,1,0:T(8,128)S(1)}, f32[2,256,128]{2,1,0:T(8,128)S(1)}, u32[]{:S(2)}, u32[]{:S(2)}) collective-permute-start(f32[2,256,128]{2,1,0:T(8,128)S(1)} %get-tuple-element.60), channel_id=1, source_target_pairs={{0,1},{1,0},{2,3},{3,2},{4,5},{5,4},{6,7},{7,6},{8,9},{9,8},{10,11... | collective-permute-start | bytes 786440 | tf_op jit(solution)/shard_map/ppermute | solution.py:400
  106.7 2.2 %collective-permute-start.4 = (f32[2,256,128]{2,1,0:T(8,128)S(1)}, f32[2,256,128]{2,1,0:T(8,128)S(1)}, u32[]{:S(2)}, u32[]{:S(2)}) collective-permute-start(f32[2,256,128]{2,1,0:T(8,128)S(1)} %get-tuple-element.66), channel_id=1, source_target_pairs={{0,1},{1,0},{2,3},{3,2},{4,5},{5,4},{6,7},{7,6},{8,9},{9,8},{10,11... | collective-permute-start | bytes 786440 | tf_op jit(solution)/shard_map/ppermute | solution.py:409
  107.2 6.4 %collective-permute-start.3 = (f32[256,128]{1,0:T(8,128)S(1)}, f32[256,128]{1,0:T(8,128)S(1)}, u32[]{:S(2)}, u32[]{:S(2)}) collective-permute-start(f32[256,128]{1,0:T(8,128)S(1)} %add_bitcast_fusion.1), channel_id=1, source_target_pairs={{0,2},{1,3},{2,0},{3,1},{4,6},{5,7},{6,4},{7,5},{8,10},{9,11},{10,... | collective-permute-start | bytes 393224 | tf_op jit(solution)/shard_map/ppermute | solution.py:417
  108.8 6.7 %collective-permute-start.5 = (f32[256,128]{1,0:T(8,128)S(1)}, f32[256,128]{1,0:T(8,128)S(1)}, u32[]{:S(2)}, u32[]{:S(2)}) collective-permute-start(f32[256,128]{1,0:T(8,128)S(1)} %add_bitcast_fusion), channel_id=1, source_target_pairs={{0,2},{1,3},{2,0},{3,1},{4,6},{5,7},{6,4},{7,5},{8,10},{9,11},{10,... | collective-permute-start | bytes 393224 | tf_op jit(solution)/shard_map/ppermute | solution.py:418

commit v8 on v7

--- a/solution.py
+++ b/solution.py
@@ -303,14 +303,14 @@
 
     halo_rows = HALO * BLK
     edge = lax.dynamic_slice_in_dim(
-        search_vectors, jnp.where(side == 0, rows - halo_rows, 0), halo_rows, 0
+        search_vectors, jnp.where(side == 1, rows - halo_rows, 0), halo_rows, 0
     )
     ring = []
     for t in range(subs):
         for n in range(nodes):
-            d = t + 1 if (n + t) % 2 == 0 else t - 1
+            d = t + 1 if (n + t) % 2 == 1 else t - 1
             if 0 <= d < subs:
-                ring.append((t * nodes + n, d * nodes + (n ^ 3)))
+                ring.append((t * nodes + n, d * nodes + (n ^ 2)))
     swap_core = [(i, i ^ 1) for i in range(nodes)]
     swap_chip = [(i, i ^ 2) for i in range(nodes)]
     halo = lax.ppermute(edge, ("sub", "node"), ring)

time: 131 us -> 130 us (level)
  waiting for transfers between devices: 7.29 us -> 5.58 us
    ppermute x1, starting transfers between devices: 0.93 us -> 5.53 us  [shards(): theirs = lax.ppermute(residual, 'node', swap_core)]
    ppermute x1, starting transfers between devices: 4.47 us -> 0.69 us  [shards(): halo = lax.ppermute(edge, ('sub', 'node'), ring)]
    ppermute x1, waiting for transfers between devices: 1.7 us -> 0.01 us  [shards(): halo = lax.ppermute(edge, ('sub', 'node'), ring)]
  transfers between devices with their start and end apart: 6 -> 6, of which waited for: 3 -> 2; matrix products, arithmetic and copies ran while one was open for 0% -> 0% of each run, Pallas kernels for 12% -> 12%
where the time goes in v8:
time: 130 us
  blocking collectives  88.7 us (68%)
  Pallas kernels  24.4 us (19%)
  starting transfers between devices  9.61 us (7%)
  waiting for transfers between devices  5.58 us (4%)
    all_to_all x1, blocking collectives, shards(): received = lax.all_to_all(pieces, 'sub', 0, 0, tiled=True)  41.5 us
    all_to_all x1, blocking collectives, shards(): picked = lax.all_to_all(back, 'sub', 0, 0, tiled=True)  33.5 us
    all_to_all x1, blocking collectives, shards(): gathered = lax.all_to_all(squares, 'sub', 0, 0, tiled=True)  13.7 us
    pallas_call x1, Pallas kernels, shards(): call(prepare_kernel, 'prepare', [SMEM] + [HBM] * 6, [half((blocks, BLK, w...  10.5 us
    ppermute x1, starting transfers between devices, shards(): theirs = lax.ppermute(residual, 'node', swap_core)  5.53 us
    ppermute x1, waiting for transfers between devices, shards(): far_a = lax.ppermute(both(1 - chip, keep_a, theirs_a), 'node', swap_chip)  3.68 us
    pallas_call x1, Pallas kernels, shards(): call(first_kernel, 'first', [SMEM] + [VMEM] * 7, [(2, rows // 4, LANES)]...  2.65 us
    pallas_call x1, Pallas kernels, shards(): call(second_kernel, 'second', [SMEM] + [VMEM] * 8, [(2, rows // 4, LANES)...  2.64 us
  transfers between devices with their start and end apart: 6, of which 2 were waited for; matrix products, arithmetic and copies ran while one was open for 0% of the time, Pallas kernels for 12%

profile of v8, /device:TPU:0, one launch (start us, length us, event | category | flops | bytes accessed | tf_op | source)
XLA Modules:
  0.0 129.8 jit_solution(5349201970027881396)
XLA Ops:
  0.0 1.1 constant_dynamic-slice_fusion
  1.1 0.7 collective-permute-start
  1.8 0.1 pad_add_fusion.place
  1.9 0.0 copy-start.1
  1.9 10.5 %prepare.1 = (bf16[8,128,256]{2,1,0:T(8,128)(2,1)S(1)}, bf16[8,128,256]{2,1,0:T(8,128)(2,1)S(1)}, f32[4,128,256]{2,1,0:T(8,128)S(1)}, bf16[4,128,512]{2,1,0:T(8,...) custom-call(s32[3]{0:T(128)S(1)} %pad_add_fusion.place, ...), custom_call_target="tpu_custom_call" | custom-call | flops 8000000000 | bytes 8388608 | tf_op jit(solution)/shard_map/prepare/pallas_call | solution.py:321
  12.3 0.0 collective-permute-done.halo
  12.4 0.0 copy-done.1
  12.4 1.4 %residual.1 = (f32[512,256]{1,0:T(8,128)S(1)}, bf16[512,256]{1,0:T(8,128)(2,1)S(1)}, bf16[512,256]{1,0:T(8,128)(2,1)S(1)}) custom-call(s32[3]{0:T(128)S(1)} %pad_add_fusion.place, s32[4,8]{1,0:T(4,128)S(1)} %bitcast.30, f32[512,256]{1,0:T(8,128)S(1)} %collective-permute-done.halo, bf16[8,128,256]{2,1,0:T(8,128)(2,1)S(1)} %get-tuple-element.39.own_hi, ...), custom_call_target="tpu_custom_call" | custom-call | flops 1000000000 | bytes 8388608 | tf_op jit(solution)/shard_map/residual/pallas_call | solution.py:358
  13.7 5.5 %collective-permute-start.1 = (f32[512,256]{1,0:T(8,128)S(1)}, f32[512,256]{1,0:T(8,128)S(1)}, u32[]{:S(2)}, u32[]{:S(2)}) collective-permute-start(f32[512,256]{1,0:T(8,128)S(1)} %get-tuple-element.44), channel_id=1, source_target_pairs={{0,1},{1,0},{2,3},{3,2},{4,5},{5,4},{6,7},{7,6},{8,9},{9,8},{10,11... | collective-permute-start | bytes 1572872 | tf_op jit(solution)/shard_map/ppermute | solution.py:366
  19.3 2.4 %mine.1.sums = f32[2048,256]{1,0:T(8,128)S(1)} custom-call(s32[3]{0:T(128)S(1)} %pad_add_fusion.place, bf16[2,2048,512]{2,1,0:T(8,128)(2,1)S(1)} %get-tuple-element.45.e_hi, bf16[2,2048,512]{2,1,0:T(8,128)(2,1)S(1)} %get-tuple-element.46.e_lo, bf16[512,256]{1,0:T(8,128)(2,1)S(1)} %get-tuple-element.47.r_hi.m_hi, bf16[512,256]{1,0:T(8,128)(2,1)S(1)} %get-tuple-element.48.r_lo.m_lo), custom_call_target="tpu_custom_call" | custom-call | flops 4000000000 | bytes 8388608 | tf_op jit(solution)/shard_map/mine/pallas_call | solution.py:367
  21.7 0.0 collective-permute-done.1.theirs
  21.7 2.4 %theirs.1 = (bf16[2,512,256]{2,1,0:T(8,128)(2,1)S(1)}, bf16[2,512,256]{2,1,0:T(8,128)(2,1)S(1)}, f32[32,136,128]{2,1,0:T(8,128)S(1)}) custom-call(s32[3]{0:T(128)S(1)} %pad_add_fusion.place, f32[2048,256]{1,0:T(8,128)S(1)} %mine.1.sums, f32[512,256]{1,0:T(8,128)S(1)} %collective-permute-done.1.theirs, bf16[2,2048,512]{2,1,0:T(8,128)(2,1)S(1)} %get-tuple-element.45.e_hi, ...), custom_call_target="tpu_custom_call" | custom-call | flops 4000000000 | bytes 8388608 | tf_op jit(solution)/shard_map/theirs/pallas_call | solution.py:375
  24.1 0.0 copy-start
  24.1 41.5 %all_to_all.15.received = f32[32,136,128]{2,1,0:T(8,128)S(1)} all-to-all(f32[32,136,128]{2,1,0:T(8,128)S(1)} %get-tuple-element.52), channel_id=1, replica_groups=mesh['sub'=32,'node'=4] {'sub'}, dimensions={0} | all-to-all | bytes 4456448 | tf_op jit(solution)/shard_map/all_to_all | solution.py:382
  65.6 0.0 copy-done
  65.6 1.5 %owner.1 = f32[32,128,128]{2,1,0:T(8,128)S(1)} custom-call(s32[3]{0:T(128)S(1)} %pad_add_fusion.place, s32[32,4]{1,0:T(8,128)S(1)} %bitcast.28, f32[8,128]{1,0:T(8,128)S(1)} %bitcast.29, f32[32,136,128]{2,1,0:T(8,128)S(1)} %all_to_all.15.received), custom_call_target="tpu_custom_call" | custom-call | bytes 8388608 | tf_op jit(solution)/shard_map/owner/pallas_call | solution.py:384
  67.2 33.5 %all_to_all.16.picked = f32[32,128,128]{2,1,0:T(8,128)S(1)} all-to-all(f32[32,128,128]{2,1,0:T(8,128)S(1)} %owner.1), channel_id=1, replica_groups=mesh['sub'=32,'node'=4] {'sub'}, dimensions={0} | all-to-all | bytes 4194304 | tf_op jit(solution)/shard_map/all_to_all | solution.py:391
  100.7 2.6 %first.1 = (f32[2,256,128]{2,1,0:T(8,128)S(1)}, f32[2,256,128]{2,1,0:T(8,128)S(1)}, bf16[2048,256]{1,0:T(8,128)(2,1)S(1)}, bf16[2048,256]{1,0:T(8,128)(2,1)S(1)}) custom-call(s32[3]{0:T(128)S(1)} %pad_add_fusion.place, f32[32,128,128]{2,1,0:T(8,128)S(1)} %all_to_all.16.picked, bf16[1024,2048]{1,0:T(8,128)(2,1)S(1)} %get-tuple-element.53.f_hi, ...), custom_call_target="tpu_custom_call" | custom-call | flops 2000000000 | bytes 8388608 | tf_op jit(solution)/shard_map/first/pallas_call | solution.py:393
  103.3 0.1 collective-permute-start.2
  103.4 2.6 %second.1 = (f32[2,256,128]{2,1,0:T(8,128)S(1)}, f32[2,256,128]{2,1,0:T(8,128)S(1)}) custom-call(s32[3]{0:T(128)S(1)} %pad_add_fusion.place, bf16[2048,256]{1,0:T(8,128)(2,1)S(1)} %get-tuple-element.61.x_hi, bf16[2048,256]{1,0:T(8,128)(2,1)S(1)} %get-tuple-element.62.x_lo, bf16[1024,2048]{1,0:T(8,128)(2,1)S(1)} %get-tuple-element.53.f_hi, ...), custom_call_target="tpu_custom_call" | custom-call | flops 2000000000 | bytes 8388608 | tf_op jit(solution)/shard_map/second/pallas_call | solution.py:401
  106.1 0.0 collective-permute-done.2
  106.1 0.6 collective-permute-start.4
  106.7 1.6 %collective-permute-start.3 = (f32[256,128]{1,0:T(8,128)S(1)}, f32[256,128]{1,0:T(8,128)S(1)}, u32[]{:S(2)}, u32[]{:S(2)}) collective-permute-start(f32[256,128]{1,0:T(8,128)S(1)} %add_bitcast_fusion.1), channel_id=1, source_target_pairs={{0,2},{1,3},{2,0},{3,1},{4,6},{5,7},{6,4},{7,5},{8,10},{9,11},{10,... | collective-permute-start | bytes 393224 | tf_op jit(solution)/shard_map/ppermute | solution.py:417
  108.3 0.0 collective-permute-done.4
  108.3 1.2 collective-permute-start.5
  109.4 3.7 %collective-permute-done.3 = f32[256,128]{1,0:T(8,128)S(1)} collective-permute-done((f32[256,128]{1,0:T(8,128)S(1)}, f32[256,128]{1,0:T(8,128)S(1)}, u32[]{:S(2)}, u32[]{:S(2)}) %collective-permute-start.3) | collective-permute-done | bytes 131104 | tf_op jit(solution)/shard_map/ppermute | solution.py:417
  113.1 1.9 %collective-permute-done.5 = f32[256,128]{1,0:T(8,128)S(1)} collective-permute-done((f32[256,128]{1,0:T(8,128)S(1)}, f32[256,128]{1,0:T(8,128)S(1)}, u32[]{:S(2)}, u32[]{:S(2)}) %collective-permute-start.5) | collective-permute-done | bytes 131104 | tf_op jit(solution)/shard_map/ppermute | solution.py:418
  115.0 0.1 multiply_reduce_fusion
  115.1 0.1 fusion.4
  115.2 0.1 maximum_add_fusion
  115.3 13.7 %all_to_all.17.squares = f32[32,1,128]{2,1,0:T(1,128)S(1)} all-to-all(f32[32,1,128]{2,1,0:T(1,128)S(1)} %broadcast_in_dim.10), channel_id=1, replica_groups=mesh['sub'=32,'node'=4] {'sub'}, dimensions={0} | all-to-all | bytes 32768 | tf_op jit(solution)/shard_map/all_to_all | solution.py:424
  129.0 0.9 scale.1
  (5 shorter events, 0.1 us)
Async XLA Ops:
  1.1 11.3 %collective-permute-start = (f32[512,256]{1,0:T(8,128)S(1)}, f32[512,256]{1,0:T(8,128)S(1)}, u32[]{:S(2)}, u32[]{:S(2)}) collective-permute-start(f32[512,256]{1,0:T(8,128)S(1)} %constant_dynamic-slice_fusion), channel_id=1, source_target_pairs={{1,7},{3,5},{4,10},{5,3},{6,8},{7,1},{8,6},{9,15},{10,4},{11,13},{... | collective-permute-start | bytes 1572872 | tf_op jit(solution)/shard_map/ppermute | solution.py:316
  1.9 10.5 %copy-start.1 = (s32[8,4]{0,1:T(4,128)S(1)}, s32[8,4]{0,1:T(4,128)}, u32[]{:S(2)}) copy-start(s32[8,4]{0,1:T(4,128)} %param.11) | copy-start | bytes 388
  13.7 8.0 %collective-permute-start.1 = (f32[512,256]{1,0:T(8,128)S(1)}, f32[512,256]{1,0:T(8,128)S(1)}, u32[]{:S(2)}, u32[]{:S(2)}) collective-permute-start(f32[512,256]{1,0:T(8,128)S(1)} %get-tuple-element.44), channel_id=1, source_target_pairs={{0,1},{1,0},{2,3},{3,2},{4,5},{5,4},{6,7},{7,6},{8,9},{9,8},{10,11... | collective-permute-start | bytes 1572872 | tf_op jit(solution)/shard_map/ppermute | solution.py:366
  24.1 41.5 %copy-start = (f32[1024]{0:T(1024)S(1)}, f32[1024]{0:T(1024)}, u32[]{:S(2)}) copy-start(f32[1024]{0:T(1024)} %param.15) | copy-start | bytes 12292
  103.3 2.7 %collective-permute-start.2 = (f32[2,256,128]{2,1,0:T(8,128)S(1)}, f32[2,256,128]{2,1,0:T(8,128)S(1)}, u32[]{:S(2)}, u32[]{:S(2)}) collective-permute-start(f32[2,256,128]{2,1,0:T(8,128)S(1)} %get-tuple-element.60), channel_id=1, source_target_pairs={{0,1},{1,0},{2,3},{3,2},{4,5},{5,4},{6,7},{7,6},{8,9},{9,8},{10,11... | collective-permute-start | bytes 786440 | tf_op jit(solution)/shard_map/ppermute | solution.py:400
  106.1 2.2 %collective-permute-start.4 = (f32[2,256,128]{2,1,0:T(8,128)S(1)}, f32[2,256,128]{2,1,0:T(8,128)S(1)}, u32[]{:S(2)}, u32[]{:S(2)}) collective-permute-start(f32[2,256,128]{2,1,0:T(8,128)S(1)} %get-tuple-element.66), channel_id=1, source_target_pairs={{0,1},{1,0},{2,3},{3,2},{4,5},{5,4},{6,7},{7,6},{8,9},{9,8},{10,11... | collective-permute-start | bytes 786440 | tf_op jit(solution)/shard_map/ppermute | solution.py:409
  106.7 6.4 %collective-permute-start.3 = (f32[256,128]{1,0:T(8,128)S(1)}, f32[256,128]{1,0:T(8,128)S(1)}, u32[]{:S(2)}, u32[]{:S(2)}) collective-permute-start(f32[256,128]{1,0:T(8,128)S(1)} %add_bitcast_fusion.1), channel_id=1, source_target_pairs={{0,2},{1,3},{2,0},{3,1},{4,6},{5,7},{6,4},{7,5},{8,10},{9,11},{10,... | collective-permute-start | bytes 393224 | tf_op jit(solution)/shard_map/ppermute | solution.py:417
  108.3 6.7 %collective-permute-start.5 = (f32[256,128]{1,0:T(8,128)S(1)}, f32[256,128]{1,0:T(8,128)S(1)}, u32[]{:S(2)}, u32[]{:S(2)}) collective-permute-start(f32[256,128]{1,0:T(8,128)S(1)} %add_bitcast_fusion), channel_id=1, source_target_pairs={{0,2},{1,3},{2,0},{3,1},{4,6},{5,7},{6,4},{7,5},{8,10},{9,11},{10,... | collective-permute-start | bytes 393224 | tf_op jit(solution)/shard_map/ppermute | solution.py:418

commit v9 on v8

--- a/solution.py
+++ b/solution.py
@@ -298,7 +298,7 @@
     rows, width = search_vectors.shape
     subs, nodes = lax.axis_size("sub"), lax.axis_size("node")
     sub, node = lax.axis_index("sub"), lax.axis_index("node")
-    side = (node + sub) % 2
+    side = (node + sub + 1) % 2
     place = jnp.stack([sub, node, side]).astype(jnp.int32)
 
     halo_rows = HALO * BLK
@@ -308,7 +308,7 @@
     ring = []
     for t in range(subs):
         for n in range(nodes):
-            d = t + 1 if (n + t) % 2 == 1 else t - 1
+            d = t + 1 if (n + t) % 2 == 0 else t - 1
             if 0 <= d < subs:
                 ring.append((t * nodes + n, d * nodes + (n ^ 2)))
     swap_core = [(i, i ^ 1) for i in range(nodes)]

time: 130 us -> 133 us (1.023)
  waiting for transfers between devices: 5.58 us -> 7.67 us
    ppermute x1, starting transfers between devices: 5.53 us -> 0.09 us  [shards(): theirs = lax.ppermute(residual, 'node', swap_core)]
    ppermute x1, starting transfers between devices: 0.69 us -> 5.01 us  [shards(): halo = lax.ppermute(edge, ('sub', 'node'), ring)]
    ppermute x1, waiting for transfers between devices: 0.01 us -> 2.33 us  [shards(): halo = lax.ppermute(edge, ('sub', 'node'), ring)]
  transfers between devices with their start and end apart: 6 -> 6, of which waited for: 2 -> 3; matrix products, arithmetic and copies ran while one was open for 0% -> 0% of each run, Pallas kernels for 12% -> 12%
where the time goes in v9:
time: 133 us
  blocking collectives  89.8 us (68%)
  Pallas kernels  24.4 us (18%)
  starting transfers between devices  9.31 us (7%)
  waiting for transfers between devices  7.67 us (6%)
    all_to_all x1, blocking collectives, shards(): received = lax.all_to_all(pieces, 'sub', 0, 0, tiled=True)  41.9 us
    all_to_all x1, blocking collectives, shards(): picked = lax.all_to_all(back, 'sub', 0, 0, tiled=True)  34 us
    all_to_all x1, blocking collectives, shards(): gathered = lax.all_to_all(squares, 'sub', 0, 0, tiled=True)  13.9 us
    pallas_call x1, Pallas kernels, shards(): call(prepare_kernel, 'prepare', [SMEM] + [HBM] * 6, [half((blocks, BLK, w...  10.5 us
    ppermute x1, starting transfers between devices, shards(): halo = lax.ppermute(edge, ('sub', 'node'), ring)  5.01 us
    ppermute x1, waiting for transfers between devices, shards(): far_a = lax.ppermute(both(1 - chip, keep_a, theirs_a), 'node', swap_chip)  3.13 us
  transfers between devices with their start and end apart: 6, of which 3 were waited for; matrix products, arithmetic and copies ran while one was open for 0% of the time, Pallas kernels for 12%

profile of v9, /device:TPU:0, one launch (start us, length us, event | category | flops | bytes accessed | tf_op | source)
XLA Modules:
  0.0 132.7 jit_solution(7524653477131965639)
XLA Ops:
  0.0 1.1 constant_dynamic-slice_fusion
  1.1 5.0 %collective-permute-start = (f32[512,256]{1,0:T(8,128)S(1)}, f32[512,256]{1,0:T(8,128)S(1)}, u32[]{:S(2)}, u32[]{:S(2)}) collective-permute-start(f32[512,256]{1,0:T(8,128)S(1)} %constant_dynamic-slice_fusion), channel_id=1, source_target_pairs={{0,6},{2,4},{4,2},{5,11},{6,0},{7,9},{8,14},{9,7},{10,12},{11,5},{... | collective-permute-start | bytes 1572872 | tf_op jit(solution)/shard_map/ppermute | solution.py:316
  6.1 0.1 pad_add_fusion.place
  6.2 0.0 copy-start.1
  6.2 10.5 %prepare.1 = (bf16[8,128,256]{2,1,0:T(8,128)(2,1)S(1)}, bf16[8,128,256]{2,1,0:T(8,128)(2,1)S(1)}, f32[4,128,256]{2,1,0:T(8,128)S(1)}, bf16[4,128,512]{2,1,0:T(8,...) custom-call(s32[3]{0:T(128)S(1)} %pad_add_fusion.place, ...), custom_call_target="tpu_custom_call" | custom-call | flops 8000000000 | bytes 8388608 | tf_op jit(solution)/shard_map/prepare/pallas_call | solution.py:321
  16.7 2.3 %collective-permute-done.halo = f32[512,256]{1,0:T(8,128)S(1)} collective-permute-done((f32[512,256]{1,0:T(8,128)S(1)}, f32[512,256]{1,0:T(8,128)S(1)}, u32[]{:S(2)}, u32[]{:S(2)}) %collective-permute-start) | collective-permute-done | bytes 524320 | tf_op jit(solution)/shard_map/ppermute | solution.py:316
  19.0 0.0 copy-done.1
  19.0 1.4 %residual.1 = (f32[512,256]{1,0:T(8,128)S(1)}, bf16[512,256]{1,0:T(8,128)(2,1)S(1)}, bf16[512,256]{1,0:T(8,128)(2,1)S(1)}) custom-call(s32[3]{0:T(128)S(1)} %pad_add_fusion.place, s32[4,8]{1,0:T(4,128)S(1)} %bitcast.30, f32[512,256]{1,0:T(8,128)S(1)} %collective-permute-done.halo, bf16[8,128,256]{2,1,0:T(8,128)(2,1)S(1)} %get-tuple-element.39.own_hi, ...), custom_call_target="tpu_custom_call" | custom-call | flops 1000000000 | bytes 8388608 | tf_op jit(solution)/shard_map/residual/pallas_call | solution.py:358
  20.3 0.1 collective-permute-start.1
  20.4 2.4 %mine.1.sums = f32[2048,256]{1,0:T(8,128)S(1)} custom-call(s32[3]{0:T(128)S(1)} %pad_add_fusion.place, bf16[2,2048,512]{2,1,0:T(8,128)(2,1)S(1)} %get-tuple-element.45.e_hi, bf16[2,2048,512]{2,1,0:T(8,128)(2,1)S(1)} %get-tuple-element.46.e_lo, bf16[512,256]{1,0:T(8,128)(2,1)S(1)} %get-tuple-element.47.r_hi.m_hi, bf16[512,256]{1,0:T(8,128)(2,1)S(1)} %get-tuple-element.48.r_lo.m_lo), custom_call_target="tpu_custom_call" | custom-call | flops 4000000000 | bytes 8388608 | tf_op jit(solution)/shard_map/mine/pallas_call | solution.py:367
  22.9 0.0 collective-permute-done.1.theirs
  22.9 2.4 %theirs.1 = (bf16[2,512,256]{2,1,0:T(8,128)(2,1)S(1)}, bf16[2,512,256]{2,1,0:T(8,128)(2,1)S(1)}, f32[32,136,128]{2,1,0:T(8,128)S(1)}) custom-call(s32[3]{0:T(128)S(1)} %pad_add_fusion.place, f32[2048,256]{1,0:T(8,128)S(1)} %mine.1.sums, f32[512,256]{1,0:T(8,128)S(1)} %collective-permute-done.1.theirs, bf16[2,2048,512]{2,1,0:T(8,128)(2,1)S(1)} %get-tuple-element.45.e_hi, ...), custom_call_target="tpu_custom_call" | custom-call | flops 4000000000 | bytes 8388608 | tf_op jit(solution)/shard_map/theirs/pallas_call | solution.py:375
  25.3 0.0 copy-start
  25.3 41.9 %all_to_all.15.received = f32[32,136,128]{2,1,0:T(8,128)S(1)} all-to-all(f32[32,136,128]{2,1,0:T(8,128)S(1)} %get-tuple-element.52), channel_id=1, replica_groups=mesh['sub'=32,'node'=4] {'sub'}, dimensions={0} | all-to-all | bytes 4456448 | tf_op jit(solution)/shard_map/all_to_all | solution.py:382
  67.2 0.0 copy-done
  67.2 1.6 %owner.1 = f32[32,128,128]{2,1,0:T(8,128)S(1)} custom-call(s32[3]{0:T(128)S(1)} %pad_add_fusion.place, s32[32,4]{1,0:T(8,128)S(1)} %bitcast.28, f32[8,128]{1,0:T(8,128)S(1)} %bitcast.29, f32[32,136,128]{2,1,0:T(8,128)S(1)} %all_to_all.15.received), custom_call_target="tpu_custom_call" | custom-call | bytes 8388608 | tf_op jit(solution)/shard_map/owner/pallas_call | solution.py:384
  68.8 34.0 %all_to_all.16.picked = f32[32,128,128]{2,1,0:T(8,128)S(1)} all-to-all(f32[32,128,128]{2,1,0:T(8,128)S(1)} %owner.1), channel_id=1, replica_groups=mesh['sub'=32,'node'=4] {'sub'}, dimensions={0} | all-to-all | bytes 4194304 | tf_op jit(solution)/shard_map/all_to_all | solution.py:391
  102.8 2.6 %first.1 = (f32[2,256,128]{2,1,0:T(8,128)S(1)}, f32[2,256,128]{2,1,0:T(8,128)S(1)}, bf16[2048,256]{1,0:T(8,128)(2,1)S(1)}, bf16[2048,256]{1,0:T(8,128)(2,1)S(1)}) custom-call(s32[3]{0:T(128)S(1)} %pad_add_fusion.place, f32[32,128,128]{2,1,0:T(8,128)S(1)} %all_to_all.16.picked, bf16[1024,2048]{1,0:T(8,128)(2,1)S(1)} %get-tuple-element.53.f_hi, ...), custom_call_target="tpu_custom_call" | custom-call | flops 2000000000 | bytes 8388608 | tf_op jit(solution)/shard_map/first/pallas_call | solution.py:393
  105.4 0.1 collective-permute-start.2
  105.5 2.6 %second.1 = (f32[2,256,128]{2,1,0:T(8,128)S(1)}, f32[2,256,128]{2,1,0:T(8,128)S(1)}) custom-call(s32[3]{0:T(128)S(1)} %pad_add_fusion.place, bf16[2048,256]{1,0:T(8,128)(2,1)S(1)} %get-tuple-element.61.x_hi, bf16[2048,256]{1,0:T(8,128)(2,1)S(1)} %get-tuple-element.62.x_lo, bf16[1024,2048]{1,0:T(8,128)(2,1)S(1)} %get-tuple-element.53.f_hi, ...), custom_call_target="tpu_custom_call" | custom-call | flops 2000000000 | bytes 8388608 | tf_op jit(solution)/shard_map/second/pallas_call | solution.py:401
  108.1 0.0 collective-permute-done.2
  108.1 0.6 collective-permute-start.4
  108.7 2.4 %collective-permute-start.3 = (f32[256,128]{1,0:T(8,128)S(1)}, f32[256,128]{1,0:T(8,128)S(1)}, u32[]{:S(2)}, u32[]{:S(2)}) collective-permute-start(f32[256,128]{1,0:T(8,128)S(1)} %add_bitcast_fusion.1), channel_id=1, source_target_pairs={{0,2},{1,3},{2,0},{3,1},{4,6},{5,7},{6,4},{7,5},{8,10},{9,11},{10,... | collective-permute-start | bytes 393224 | tf_op jit(solution)/shard_map/ppermute | solution.py:417
  111.1 0.0 collective-permute-done.4
  111.2 1.2 collective-permute-start.5
  112.3 3.1 %collective-permute-done.3 = f32[256,128]{1,0:T(8,128)S(1)} collective-permute-done((f32[256,128]{1,0:T(8,128)S(1)}, f32[256,128]{1,0:T(8,128)S(1)}, u32[]{:S(2)}, u32[]{:S(2)}) %collective-permute-start.3) | collective-permute-done | bytes 131104 | tf_op jit(solution)/shard_map/ppermute | solution.py:417
  115.4 2.2 %collective-permute-done.5 = f32[256,128]{1,0:T(8,128)S(1)} collective-permute-done((f32[256,128]{1,0:T(8,128)S(1)}, f32[256,128]{1,0:T(8,128)S(1)}, u32[]{:S(2)}, u32[]{:S(2)}) %collective-permute-start.5) | collective-permute-done | bytes 131104 | tf_op jit(solution)/shard_map/ppermute | solution.py:418
  117.7 0.1 multiply_reduce_fusion
  117.7 0.1 fusion.4
  117.8 0.1 maximum_add_fusion
  117.9 13.9 %all_to_all.17.squares = f32[32,1,128]{2,1,0:T(1,128)S(1)} all-to-all(f32[32,1,128]{2,1,0:T(1,128)S(1)} %broadcast_in_dim.10), channel_id=1, replica_groups=mesh['sub'=32,'node'=4] {'sub'}, dimensions={0} | all-to-all | bytes 32768 | tf_op jit(solution)/shard_map/all_to_all | solution.py:424
  131.8 0.9 scale.1
  (5 shorter events, 0.1 us)
Async XLA Ops:
  1.1 17.9 %collective-permute-start = (f32[512,256]{1,0:T(8,128)S(1)}, f32[512,256]{1,0:T(8,128)S(1)}, u32[]{:S(2)}, u32[]{:S(2)}) collective-permute-start(f32[512,256]{1,0:T(8,128)S(1)} %constant_dynamic-slice_fusion), channel_id=1, source_target_pairs={{0,6},{2,4},{4,2},{5,11},{6,0},{7,9},{8,14},{9,7},{10,12},{11,5},{... | collective-permute-start | bytes 1572872 | tf_op jit(solution)/shard_map/ppermute | solution.py:316
  6.2 12.8 %copy-start.1 = (s32[8,4]{0,1:T(4,128)S(1)}, s32[8,4]{0,1:T(4,128)}, u32[]{:S(2)}) copy-start(s32[8,4]{0,1:T(4,128)} %param.11) | copy-start | bytes 388
  20.3 2.5 %collective-permute-start.1 = (f32[512,256]{1,0:T(8,128)S(1)}, f32[512,256]{1,0:T(8,128)S(1)}, u32[]{:S(2)}, u32[]{:S(2)}) collective-permute-start(f32[512,256]{1,0:T(8,128)S(1)} %get-tuple-element.44), channel_id=1, source_target_pairs={{0,1},{1,0},{2,3},{3,2},{4,5},{5,4},{6,7},{7,6},{8,9},{9,8},{10,11... | collective-permute-start | bytes 1572872 | tf_op jit(solution)/shard_map/ppermute | solution.py:366
  25.3 41.9 %copy-start = (f32[1024]{0:T(1024)S(1)}, f32[1024]{0:T(1024)}, u32[]{:S(2)}) copy-start(f32[1024]{0:T(1024)} %param.15) | copy-start | bytes 12292
  105.4 2.7 %collective-permute-start.2 = (f32[2,256,128]{2,1,0:T(8,128)S(1)}, f32[2,256,128]{2,1,0:T(8,128)S(1)}, u32[]{:S(2)}, u32[]{:S(2)}) collective-permute-start(f32[2,256,128]{2,1,0:T(8,128)S(1)} %get-tuple-element.60), channel_id=1, source_target_pairs={{0,1},{1,0},{2,3},{3,2},{4,5},{5,4},{6,7},{7,6},{8,9},{9,8},{10,11... | collective-permute-start | bytes 786440 | tf_op jit(solution)/shard_map/ppermute | solution.py:400
  108.1 3.0 %collective-permute-start.4 = (f32[2,256,128]{2,1,0:T(8,128)S(1)}, f32[2,256,128]{2,1,0:T(8,128)S(1)}, u32[]{:S(2)}, u32[]{:S(2)}) collective-permute-start(f32[2,256,128]{2,1,0:T(8,128)S(1)} %get-tuple-element.66), channel_id=1, source_target_pairs={{0,1},{1,0},{2,3},{3,2},{4,5},{5,4},{6,7},{7,6},{8,9},{9,8},{10,11... | collective-permute-start | bytes 786440 | tf_op jit(solution)/shard_map/ppermute | solution.py:409
  108.7 6.7 %collective-permute-start.3 = (f32[256,128]{1,0:T(8,128)S(1)}, f32[256,128]{1,0:T(8,128)S(1)}, u32[]{:S(2)}, u32[]{:S(2)}) collective-permute-start(f32[256,128]{1,0:T(8,128)S(1)} %add_bitcast_fusion.1), channel_id=1, source_target_pairs={{0,2},{1,3},{2,0},{3,1},{4,6},{5,7},{6,4},{7,5},{8,10},{9,11},{10,... | collective-permute-start | bytes 393224 | tf_op jit(solution)/shard_map/ppermute | solution.py:417
  111.2 6.5 %collective-permute-start.5 = (f32[256,128]{1,0:T(8,128)S(1)}, f32[256,128]{1,0:T(8,128)S(1)}, u32[]{:S(2)}, u32[]{:S(2)}) collective-permute-start(f32[256,128]{1,0:T(8,128)S(1)} %add_bitcast_fusion), channel_id=1, source_target_pairs={{0,2},{1,3},{2,0},{3,1},{4,6},{5,7},{6,4},{7,5},{8,10},{9,11},{10,... | collective-permute-start | bytes 393224 | tf_op jit(solution)/shard_map/ppermute | solution.py:418
